TPU v7x, 32 devices: a whole 2x2x4 slice. The times are simulated.
32 devices in a mesh: dp: 8 (over z, y), seq: 4 (over x, core).
Axes of the slice: x: 2, y: 2, z: 4, core: 2. Of those that a mesh axis runs over, the one named last changes fastest.
Arguments:
- layer_input: bfloat16 [16, 1024, 1536], P('dp', 'seq'), may hold values from -6 to 6
- document_index: int32 [16, 1024], P('dp', 'seq'), may hold values from 0 to 7, never falling along the last dimension, each value on 1 to 512 neighbouring positions
- adapter_index: int32 [16], P('dp'), may hold values from 0 to 7
- input_norm_gain: bfloat16 [1536], P(('dp', 'seq')), may hold values from 0.5 to 1.5
- input_projection: bfloat16 [1536, 6400], P(('dp', 'seq')), may hold values from -0.15625 to 0.15625
- step_projection: bfloat16 [1536, 48], P(('dp', 'seq')), may hold values from -0.15625 to 0.15625
- convolution_weight: bfloat16 [3328, 4], P(('dp', 'seq')), may hold values from -3 to 3
- convolution_bias: bfloat16 [3328], P(('dp', 'seq')), may hold values from -1.5 to 1.5
- head_step_bias: float32 [48], replicated, may hold values from -7 to -2.5
- log_decay_rate: float32 [48], replicated, may hold values from 0 to 1.5
- head_skip_gain: float32 [48], replicated, may hold values from 0.5 to 1.5
- gated_norm_gain: bfloat16 [3072], P(('dp', 'seq')), may hold values from 0.5 to 1.5
- output_projection: bfloat16 [3072, 1536], P(('dp', 'seq')), may hold values from -0.109375 to 0.109375
- adapter_input_down: bfloat16 [8, 16, 1536], P(None, None, ('dp', 'seq')), may hold values from -0.15625 to 0.15625
- adapter_input_up: bfloat16 [8, 16, 6400], P(None, None, ('dp', 'seq')), may hold values from -0.75 to 0.75
- adapter_output_down: bfloat16 [8, 16, 3072], P(None, None, ('dp', 'seq')), may hold values from -0.109375 to 0.109375
- adapter_output_up: bfloat16 [8, 16, 1536], P(None, None, ('dp', 'seq')), may hold values from -0.75 to 0.75
- output_gradient: bfloat16 [16, 1024, 1536], P('dp', 'seq'), may hold values from -6 to 6
Outputs:
- output: bfloat16 [16, 1024, 1536], P('dp', 'seq')
- grad_in: float32 [16, 1024, 1536], P('dp', 'seq')
- grad_lora_in_down: float32 [8, 16, 1536], P(None, None, ('dp', 'seq'))
- grad_lora_in_up: float32 [8, 16, 6400], P(None, None, ('dp', 'seq'))
- grad_lora_out_down: float32 [8, 16, 3072], P(None, None, ('dp', 'seq'))
- grad_lora_out_up: float32 [8, 16, 1536], P(None, None, ('dp', 'seq'))
Inputs may be any that keep to these rules, and one draw needn't show every extreme that they name: `document_index`: in each sequence the numbers start at 0, never fall, and each of the 8 segments has 1 to 512 tokens, one exactly 512.
All inputs are finite; a program needn't handle non-finite values.
Results may differ from a plain program's by a relative error of at most 0.0086.
Values may be sent and summed in bfloat16 or wider, within the bound.
No kernel may reach another device: no remote copies, remote signals or barrier semaphores. Data moves between devices by JAX's collectives and lax.ppermute only.
A program may use at most 192 MiB of HBM per device.

v0:
```python
import functools

import jax
import jax.numpy as jnp
from jax import lax
from jax.experimental import pallas as pl
from jax.experimental.pallas import tpu as pltpu
from jax.sharding import PartitionSpec as P

EPS = 1e-05
f32 = jnp.float32
bf16 = jnp.bfloat16
BLOCK = 256


def mm(form, a, b):
    return jnp.einsum(form, a, b, preferred_element_type=f32)


LOG2E = 1.4426950408889634
VMEM_BYTES = 66_000_000


def dot_nn(a, b):
    return lax.dot_general(a, b, (((1,), (0,)), ((), ())), preferred_element_type=f32)


def dot_nt(a, b):
    return lax.dot_general(a, b, (((1,), (1,)), ((), ())), preferred_element_type=f32)


def dot_tn(a, b):
    return lax.dot_general(a, b, (((0,), (0,)), ((), ())), preferred_element_type=f32)


def dot_exact(a, b):
    return lax.dot_general(
        a, b, (((1,), (0,)), ((), ())), preferred_element_type=f32, precision=lax.Precision.HIGHEST
    )


def sigmoid(v):
    return 0.5 * jnp.tanh(0.5 * v) + 0.5


def spread_pair(cols, j):
    rows = cols.shape[0]
    lane = lax.broadcasted_iota(jnp.int32, (rows, 128), 1)
    return jnp.where(lane < 64, cols[:, 2 * j : 2 * j + 1], cols[:, 2 * j + 1 : 2 * j + 2])


def spread_all(cols, pairs):
    return jnp.concatenate([spread_pair(cols, j) for j in range(pairs)], 1)


def per_head(v, select):
    hi = v.astype(bf16)
    lo = (v - hi.astype(f32)).astype(bf16)
    return dot_nn(hi, select) + dot_nn(lo, select)


def forward_kernel(
    x_ref, meta_ref, doc_ref, wa_ref, up_ref, conv_ref, gain_ref, head_ref, mask_ref, half_ref,
    normed_ref, rank_ref, vbc_ref, pre_ref, ssm_ref, state_ref, tok_ref,
    buf, carry,
    *, hn, hc,
):
    pairs = hn // 2
    cc = hc + 256

    @pl.when(pl.program_id(1) == 0)
    def _():
        carry[...] = jnp.zeros_like(carry)
        buf[0:8, :] = jnp.zeros((8, cc), f32)

    x = x_ref[0].astype(f32)
    inv = lax.rsqrt(jnp.mean(x * x, -1, keepdims=True) + EPS)
    normed = (x * inv * gain_ref[0:1, :]).astype(bf16)
    normed_ref[0] = normed
    pa = dot_nn(normed, wa_ref[...])
    rank = (pa[:, cc : cc + 128] * mask_ref[0, 0:1, :]).astype(bf16)
    rank_ref[0] = rank
    conv_in = (pa[:, :cc] + dot_nt(rank, up_ref[...])).astype(bf16).astype(f32)
    buf[8:, :] = conv_in
    meta = meta_ref[0]
    pre = conv_ref[4:5, :] + conv_ref[3:4, :] * conv_in
    for k in (1, 2, 3):
        pre = pre + conv_ref[3 - k : 4 - k, :] * (buf[8 - k : 8 - k + BLOCK, :] * meta[:, k - 1 : k])
    buf[0:8, :] = buf[BLOCK : BLOCK + 8, :]
    pre_ref[0] = pre
    vbc = (pre * sigmoid(pre)).astype(bf16)
    vbc_ref[0] = vbc
    values = vbc[:, :hc]
    in_state = vbc[:, hc : hc + 128]
    out_state = vbc[:, hc + 128 :]
    arg = pa[:, cc + 128 : cc + 256] + head_ref[0:1, :]
    dt = jnp.maximum(arg, 0.0) + jnp.log1p(jnp.exp(-jnp.abs(arg)))
    row = lax.broadcasted_iota(jnp.int32, (BLOCK, BLOCK), 0)
    col = lax.broadcasted_iota(jnp.int32, (BLOCK, BLOCK), 1)
    cum = dot_exact((row >= col).astype(f32), dt * head_ref[1:2, :])
    tok_ref[0, :, 0:128] = dt
    tok_ref[0, :, 128:256] = cum
    tok_ref[0, :, 256:384] = arg
    left = cum * LOG2E
    right = (left - jnp.log(jnp.maximum(dt, 1e-37)) * LOG2E).T
    ok = (row >= col) & (meta[:, 5:6] == doc_ref[0, 0])
    bias = jnp.where(ok, 0.0, -1e30)
    contact = dot_nt(out_state, in_state)
    entry = jnp.exp(cum) * meta[:, 3:4]
    weight = jnp.exp(cum[BLOCK - 1 :, :] - cum) * dt * meta[:, 4:5]
    state = carry[...]
    state_low = state.astype(bf16)
    state_ref[0, 0] = state_low
    readout = dot_nt(out_state, state_low)
    half = BLOCK // 2
    scaled = []
    for j in range(pairs):
        at = slice(128 * j, 128 * j + 128)
        v = values[:, at]
        ys = []
        for r0, c1 in ((0, half), (half, BLOCK)):
            ws = []
            for h in (2 * j, 2 * j + 1):
                e = jnp.exp2(
                    (left[r0 : r0 + half, h : h + 1] - right[h : h + 1, :c1])
                    + bias[r0 : r0 + half, :c1]
                )
                ws.append((contact[r0 : r0 + half, :c1] * e).astype(bf16))
            vv = jnp.concatenate([v[:c1] * half_ref[0:1, :], v[:c1] * half_ref[1:2, :]], 0)
            ys.append(dot_nn(jnp.concatenate(ws, 1), vv))
        y = jnp.concatenate(ys, 0)
        ssm_ref[0, :, at] = y + readout[:, at] * spread_pair(entry, j)
        scaled.append((v.astype(f32) * spread_pair(weight, j)).astype(bf16))
    local = dot_tn(jnp.concatenate(scaled, 1), in_state)
    passing = entry[BLOCK - 1 :, :]
    for h in range(hn):
        at = slice(64 * h, 64 * h + 64)
        carry[at, :] = passing[:, h : h + 1] * state[at] + local[at]


def middle_kernel(
    normed_ref, rank_ref, vbc_ref, ssm_ref, og_ref, wb_ref, up_ref, wo_ref, upo_ref, row_ref, mask_ref,
    g_ref, q_ref, gro_ref, part_ref, stat_ref,
    *, hc, width,
):
    gate = dot_nn(normed_ref[0], wb_ref[...]) + dot_nt(rank_ref[0], up_ref[...])
    g_ref[0] = gate
    mixed = ssm_ref[0] + row_ref[0:1, :] * vbc_ref[0, :, :hc].astype(f32)
    gated = mixed * (gate * sigmoid(gate))
    og = og_ref[0]
    gro = (dot_nt(og, upo_ref[...]) * mask_ref[0, 0:1, :]).astype(bf16)
    gro_ref[0] = gro
    q = dot_nt(og, wo_ref[:, :width]) + dot_nt(gro, wo_ref[:, width : width + 128])
    q = q * row_ref[1:2, :]
    q_ref[0] = q
    lane = lax.broadcasted_iota(jnp.int32, (BLOCK, 128), 1)
    s0 = jnp.sum(gated * gated, -1, keepdims=True)
    s1 = jnp.sum(q * gated, -1, keepdims=True)
    stat_ref[0] = jnp.where(lane == 0, s0, s1).T[:8]
    part_ref[0] = dot_nn((gated * row_ref[1:2, :]).astype(bf16), wo_ref[:, : width + 128]).astype(
        part_ref.dtype
    )


def backward_kernel(
    q_ref, g_ref, ssm_ref, vbc_ref, pre_ref, tok_ref, rm_ref, meta_ref, doc_ref, state_ref, next_ref,
    rank_ref, gro_ref, conv_ref, head_ref, row_ref, half_ref, select_ref,
    gpg_ref, gpc_ref, gs_ref, up_ref, down_ref,
    buf, carry,
    *, hn, hc,
):
    pairs = hn // 2
    cc = hc + 256
    first = pl.program_id(1) == 0

    @pl.when(first)
    def _():
        carry[...] = jnp.zeros_like(carry)
        buf[BLOCK:, :] = jnp.zeros((8, cc), f32)
        up_ref[...] = jnp.zeros_like(up_ref)
        down_ref[...] = jnp.zeros_like(down_ref)

    rm = jnp.concatenate([rm_ref[0]] * 16, 0).T
    inv = rm[:, 0:1]
    mean = rm[:, 1:2]
    meta = meta_ref[0]
    gate = g_ref[0]
    ssm = ssm_ref[0]
    q = q_ref[0]
    vbc = vbc_ref[0]
    values = vbc[:, :hc]
    values_f = values.astype(f32)
    in_state = vbc[:, hc : hc + 128]
    out_state = vbc[:, hc + 128 :]
    skip = row_ref[0:1, :]
    mixed = ssm + skip * values_f
    sg = sigmoid(gate)
    act = gate * sg
    gated = mixed * act
    gated_r = gated * inv
    grad_gated = inv * (q - gated_r * (inv * mean))
    gated_low = (gated_r * row_ref[1:2, :]).astype(bf16)
    down_ref[0] = down_ref[0] + dot_tn(gro_ref[0], gated_low)
    grad_mixed = grad_gated * act
    gp_gate = (grad_gated * mixed * (sg + act * (1.0 - sg))).astype(bf16)
    gpg_ref[0] = gp_gate
    gsum = grad_mixed.astype(bf16)
    gsum_f = gsum.astype(f32)

    dt = tok_ref[0, :, 0:128]
    cum = tok_ref[0, :, 128:256]
    arg = tok_ref[0, :, 256:384]
    scaled_cum = cum * LOG2E
    down = scaled_cum - jnp.log(jnp.maximum(dt, 1e-37)) * LOG2E
    across = scaled_cum.T
    row = lax.broadcasted_iota(jnp.int32, (BLOCK, BLOCK), 0)
    col = lax.broadcasted_iota(jnp.int32, (BLOCK, BLOCK), 1)
    ok = (col >= row) & (meta[:, 5:6] == doc_ref[0, 0])
    bias = jnp.where(ok, 0.0, -1e30)
    contact = dot_nt(in_state, out_state)
    entry = jnp.exp(cum) * meta[:, 3:4]
    weight = jnp.exp(cum[BLOCK - 1 :, :] - cum) * dt * meta[:, 4:5]
    later = carry[...]
    later_low = later.astype(bf16)
    grad_scaled = dot_nt(in_state, later_low)
    weight_wide = spread_all(weight, pairs)
    entry_wide = spread_all(entry, pairs)
    scaled = (values_f * weight_wide).astype(bf16)
    weighted = (gsum_f * entry_wide).astype(bf16)
    half = BLOCK // 2
    g_con = [jnp.zeros((half, BLOCK), f32), jnp.zeros((half, half), f32)]
    g_val = []
    for j in range(pairs):
        at = slice(128 * j, 128 * j + 128)
        v = values[:, at]
        gs = gsum[:, at]
        tops = []
        for i, (r0, c0) in enumerate(((0, 0), (half, half))):
            ws = []
            for side in (0, 1):
                h = 2 * j + side
                gw = dot_nt(v[r0 : r0 + half] * half_ref[side : side + 1, :], gs[c0:])
                e = jnp.exp2(
                    (across[h : h + 1, c0:] - down[r0 : r0 + half, h : h + 1])
                    + bias[r0 : r0 + half, c0:]
                )
                ws.append((contact[r0 : r0 + half, c0:] * e).astype(bf16))
                g_con[i] = g_con[i] + gw * e
            gg = jnp.concatenate([gs[c0:] * half_ref[0:1, :], gs[c0:] * half_ref[1:2, :]], 0)
            tops.append(dot_nn(jnp.concatenate(ws, 1), gg))
        g_val.append(jnp.concatenate(tops, 0))
    g_val = jnp.concatenate(g_val, 1) + grad_scaled * weight_wide
    con_low = jnp.concatenate(
        [g_con[0], jnp.concatenate([jnp.zeros((half, half), f32), g_con[1]], 1)], 0
    ).astype(bf16)
    g_in = dot_nn(con_low, out_state) + dot_nn(scaled, later_low)
    g_out = dot_tn(con_low, in_state) + dot_nn(weighted, state_ref[0, 0])
    select = select_ref[...]
    spent = per_head(values_f * g_val, select)
    gained = per_head(gsum_f * ssm, select)
    ends = later * next_ref[0, 0].astype(f32)
    parts = [jnp.sum(ends[64 * h : 64 * h + 64], 0, keepdims=True) for h in range(hn)]
    parts.append(jnp.zeros((128 - hn, 128), f32))
    last = jnp.sum(jnp.concatenate(parts, 0).T, 0, keepdims=True)
    where_last = lax.broadcasted_iota(jnp.int32, (BLOCK, 128), 0) == BLOCK - 1
    grad_cum = gained - spent + jnp.where(where_last, last, 0.0)
    grad_log = dot_exact((col >= row).astype(f32), grad_cum)
    sig = sigmoid(arg)
    gs_ref[0] = (
        spent * (sig / jnp.maximum(dt, 1e-37)) + head_ref[1:2, :] * grad_log * sig
    ).astype(bf16)
    passing = entry[BLOCK - 1 :, :]
    direct = dot_tn(weighted, out_state)
    for h in range(hn):
        at = slice(64 * h, 64 * h + 64)
        carry[at, :] = passing[:, h : h + 1] * later[at] + direct[at]

    pre = pre_ref[0]
    sp = sigmoid(pre)
    grad_out = jnp.concatenate([skip * grad_mixed + g_val, g_in, g_out], 1)
    grad_pre = grad_out * (sp + pre * sp * (1.0 - sp))
    buf[:BLOCK, :] = grad_pre
    total = conv_ref[3:4, :] * grad_pre
    for k in (1, 2, 3):
        total = total + conv_ref[3 - k : 4 - k, :] * (buf[k : k + BLOCK, :] * meta[:, 5 + k : 6 + k])
    buf[BLOCK:, :] = grad_pre[:8]
    gp_conv = total.astype(bf16)
    gpc_ref[0] = gp_conv
    rank = rank_ref[0]
    up_ref[0, :, :hc] = up_ref[0, :, :hc] + dot_tn(rank, gp_gate)
    up_ref[0, :, hc:] = up_ref[0, :, hc:] + dot_tn(rank, gp_conv)


def per_device(
    layer_input,
    document_index,
    adapter_index,
    input_norm_gain,
    input_projection,
    step_projection,
    convolution_weight,
    convolution_bias,
    head_step_bias,
    log_decay_rate,
    head_skip_gain,
    gated_norm_gain,
    output_projection,
    adapter_input_down,
    adapter_input_up,
    adapter_output_down,
    adapter_output_up,
    output_gradient,
):
    both = ("dp", "seq")
    dps, n = lax.axis_size("dp"), lax.axis_size("seq")
    here = lax.axis_index("seq")
    seqs, own_len, width = layer_input.shape
    adapters, rank, _ = adapter_input_down.shape
    ranks = adapters * rank
    heads = head_step_bias.shape[0]
    inner = output_projection.shape[0] * dps * n
    cols = input_projection.shape[1]
    state2 = cols - 2 * inner
    state = state2 // 2
    taps = convolution_weight.shape[1]
    hn = heads // n
    hc = inner // n
    hd = inner // heads
    length = own_len * n
    nb = length // BLOCK

    x_all = lax.all_gather(layer_input, "seq", axis=1, tiled=True)
    og_all = lax.all_gather(output_gradient, "seq", axis=1, tiled=True)
    docs = lax.all_gather(document_index, "seq", axis=1, tiled=True)

    rows = input_projection.shape[0]
    down_rows = adapter_input_down.reshape(ranks, rows).T
    step_pad = 128 - hn
    per_target = []
    for t in range(n):
        per_target.append(
            jnp.concatenate(
                [
                    input_projection[:, inner + t * hc : inner + (t + 1) * hc],
                    input_projection[:, 2 * inner :],
                    down_rows,
                    jnp.pad(step_projection[:, t * hn : (t + 1) * hn], ((0, 0), (0, step_pad))),
                    input_projection[:, t * hc : (t + 1) * hc],
                ],
                1,
            )
        )
    w_mine = lax.all_to_all(jnp.stack(per_target), "seq", 0, 0, tiled=True)
    w_mine = w_mine.reshape(n * rows, -1)
    w_in = lax.all_gather(w_mine, "dp", axis=0, tiled=True)
    conv_cols = hc + state2
    wa_cols = conv_cols + ranks + 128
    wa, wb = w_in[:, :wa_cols], w_in[:, wa_cols:]

    out_rows = output_projection.shape[0]
    w_o = jnp.concatenate(
        [
            output_projection,
            adapter_output_down.reshape(ranks, out_rows).T,
            jnp.pad(gated_norm_gain[:, None], ((0, 0), (0, 127))),
        ],
        1,
    )
    w_o = lax.ppermute(
        w_o, both, [(dps * s + d, n * d + s) for d in range(dps) for s in range(n)]
    )
    w_o = lax.all_gather(w_o, "dp", axis=0, tiled=True)
    gate_gain = w_o[:, width + ranks].astype(f32)

    up_rows = adapter_input_up.shape[2]
    conv_rows = convolution_weight.shape[0]

    wide = -(-conv_rows // 128) * 128

    def as_row(v):
        return jnp.pad(v, ((0, 0), (0, wide - v.shape[1])))

    misc = jnp.concatenate(
        [
            as_row(convolution_weight.T),
            as_row(convolution_bias[None]),
            as_row(input_norm_gain[None]),
            as_row(adapter_index.astype(bf16)[None]),
        ],
        0,
    )
    misc_rows = misc.shape[0]
    small = jnp.concatenate(
        [
            adapter_input_up.reshape(ranks, up_rows).T,
            adapter_output_up.reshape(ranks, rows).T,
            misc.reshape(-1, 128),
        ],
        0,
    )
    small = lax.all_gather(small, both, axis=0)
    up_full = small[:, :up_rows].reshape(cols, ranks)
    up_out = small[:, up_rows : up_rows + rows].reshape(width, ranks)
    misc = small[:, up_rows + rows :].reshape(dps * n, misc_rows, wide)
    conv_w = jnp.moveaxis(misc[:, :taps, :conv_rows], 1, 0).reshape(taps, -1).astype(f32)
    conv_b = misc[:, taps, :conv_rows].reshape(-1).astype(f32)
    gain = misc[:, taps + 1, :rows].reshape(-1).astype(f32)
    every_index = misc[:, taps + 2, :seqs].reshape(dps, n, seqs)[:, 0].astype(jnp.int32)

    def mine(v, size, base=0):
        return lax.dynamic_slice_in_dim(v, base + here * size, size, 0)

    up_gate = mine(up_full, hc)
    up_conv = jnp.concatenate([mine(up_full, hc, inner), up_full[2 * inner :]], 0)
    conv_w = jnp.concatenate([mine(conv_w.T, hc), conv_w.T[inner:]], 0).T
    conv_b = jnp.concatenate([mine(conv_b, hc), conv_b[inner:]], 0)
    step_bias = mine(head_step_bias, hn)
    decay_rate = -jnp.exp(mine(log_decay_rate, hn))
    skip = mine(head_skip_gain, hn)

    chosen = (adapter_index[:, None] == jnp.arange(adapters, dtype=jnp.int32)[None, :]).astype(f32)
    mask = jnp.repeat(chosen, rank, axis=1)[:, None, :]

    doc_f = docs.astype(f32)

    def before(k):
        return jnp.pad(doc_f, ((0, 0), (k, 0)), constant_values=-1.0)[:, :length] == doc_f

    def after(k):
        return jnp.pad(doc_f, ((0, 0), (0, k)), constant_values=-1.0)[:, k:] == doc_f

    blocks = doc_f.reshape(seqs, nb, BLOCK)
    prior = jnp.concatenate([blocks[:, :1, 0], blocks[:, :-1, -1]], 1)
    keep = (blocks == prior[:, :, None]).reshape(seqs, length)
    ends = (blocks == blocks[:, :, -1:]).reshape(seqs, length)
    flags = [before(1), before(2), before(3), keep, ends, doc_f, after(1), after(2), after(3)]
    meta = jnp.stack([v.astype(f32) for v in flags], -1)
    meta = jnp.pad(meta, ((0, 0), (0, 0), (0, 128 - len(flags))))
    doc_rows = blocks[:, :, None, :]

    def rows8(*vs):
        return jnp.pad(jnp.stack(vs), ((0, 8 - len(vs)), (0, 0)))

    conv_rows8 = rows8(conv_w[0], conv_w[1], conv_w[2], conv_w[3], conv_b)
    head_rows = rows8(
        jnp.pad(step_bias, (0, 128 - hn)), jnp.pad(decay_rate, (0, 128 - hn))
    )
    wide_rows = rows8(jnp.repeat(skip, hd), gate_gain)
    gain_rows = rows8(gain)
    halves = jnp.pad(
        (jnp.arange(128)[None, :] // 64 == jnp.arange(2)[:, None]).astype(bf16), ((0, 14), (0, 0))
    )
    select = (jnp.arange(hc)[:, None] // hd == jnp.arange(128)[None, :]).astype(bf16)
    mask8 = jnp.broadcast_to(mask, (seqs, 8, ranks))
    grid = (seqs, nb)

    def tile(w, flip=False):
        return pl.BlockSpec(
            (1, BLOCK, w), (lambda s, b: (s, nb - 1 - b, 0)) if flip else (lambda s, b: (s, b, 0))
        )

    def fixed(v):
        return pl.BlockSpec(v.shape, lambda s, b: (0,) * v.ndim, pipeline_mode=pl.Buffered(1))

    def by_seq(v):
        return pl.BlockSpec((1,) + v.shape[1:], lambda s, b: (s, 0, 0))

    def shape(w, dtype):
        return jax.ShapeDtypeStruct((seqs, length, w), dtype)

    params = pltpu.CompilerParams(
        dimension_semantics=("arbitrary", "arbitrary"), vmem_limit_bytes=VMEM_BYTES
    )
    cc = conv_cols
    tokens = seqs * length
    state_shape = jax.ShapeDtypeStruct((seqs, nb, hc, state), bf16)
    normed, rank_in, vbc, pre, ssm, states_low, tok = pl.pallas_call(
        functools.partial(forward_kernel, hn=hn, hc=hc),
        grid=grid,
        in_specs=[
            tile(width), tile(128), pl.BlockSpec((1, 1, 1, BLOCK), lambda s, b: (s, b, 0, 0)),
            fixed(wa), fixed(up_conv), fixed(conv_rows8), fixed(gain_rows), fixed(head_rows),
            by_seq(mask8), fixed(halves),
        ],
        out_specs=[
            tile(width), tile(128), tile(cc), tile(cc), tile(hc),
            pl.BlockSpec((1, 1, hc, state), lambda s, b: (s, b, 0, 0)), tile(384),
        ],
        out_shape=[
            shape(width, bf16), shape(128, bf16), shape(cc, bf16), shape(cc, f32), shape(hc, f32),
            state_shape, shape(384, f32),
        ],
        scratch_shapes=[pltpu.VMEM((BLOCK + 8, cc), f32), pltpu.VMEM((hc, state), f32)],
        compiler_params=params,
        name="ssm_forward",
        cost_estimate=pl.CostEstimate(
            flops=2 * tokens * (width * wa_cols + 3 * BLOCK * hc), bytes_accessed=40 << 20, transcendentals=0
        ),
    )(x_all, meta, doc_rows, wa, up_conv, conv_rows8, gain_rows, head_rows, mask8, halves)

    w_ext = w_o[:, : width + ranks]
    gate, q, grad_rank_out, branch, stats = pl.pallas_call(
        functools.partial(middle_kernel, hc=hc, width=width),
        grid=grid,
        in_specs=[
            tile(width), tile(128), tile(cc), tile(hc), tile(width), fixed(wb), fixed(up_gate),
            fixed(w_ext), fixed(up_out.T), fixed(wide_rows), by_seq(mask8),
        ],
        out_specs=[
            tile(hc), tile(hc), tile(128), tile(width + ranks),
            pl.BlockSpec((1, 8, BLOCK), lambda s, b: (s, 0, b)),
        ],
        out_shape=[
            shape(hc, f32), shape(hc, f32), shape(128, bf16), shape(width + ranks, f32),
            jax.ShapeDtypeStruct((seqs, 8, length), f32),
        ],
        compiler_params=params,
        name="gate_and_output",
        cost_estimate=pl.CostEstimate(
            flops=2 * tokens * width * hc * 3, bytes_accessed=50 << 20, transcendentals=0
        ),
    )(normed, rank_in, vbc, ssm, og_all, wb, up_gate, w_ext, up_out.T, wide_rows, mask8)

    stats = lax.psum(stats[:, :2], "seq")
    inv_gated = lax.rsqrt(stats[:, :1] / inner + EPS)
    rm = jnp.concatenate([inv_gated, stats[:, 1:] / inner], 1)
    rm = jnp.pad(rm, ((0, 0), (0, 6), (0, 0)))
    branch = lax.psum_scatter(branch, "seq", scatter_dimension=1, tiled=True)
    inv_mine = lax.dynamic_slice_in_dim(inv_gated[:, 0], here * own_len, own_len, 1)[..., None]
    branch = branch * inv_mine
    rank_out = (branch[..., width:] * mask).astype(bf16)
    output = (
        layer_input.astype(f32) + branch[..., :width] + mm("str,dr->std", rank_out, up_out)
    ).astype(bf16)

    def compact(v):
        return v.reshape(seqs, adapters, rank, -1).sum(1)

    g_out_up = compact(mm("str,std->srd", rank_out, output_gradient))

    def back_state(at):
        return pl.BlockSpec((1, 1, hc, state), lambda s, b: (s, at(nb - 1 - b), 0, 0))

    gp_gate, gp_conv, g_step, g_in_up, g_out_down = pl.pallas_call(
        functools.partial(backward_kernel, hn=hn, hc=hc),
        grid=grid,
        in_specs=[
            tile(hc, True), tile(hc, True), tile(hc, True), tile(cc, True), tile(cc, True),
            tile(384, True), pl.BlockSpec((1, 8, BLOCK), lambda s, b: (s, 0, nb - 1 - b)),
            tile(128, True), pl.BlockSpec((1, 1, 1, BLOCK), lambda s, b: (s, nb - 1 - b, 0, 0)),
            back_state(lambda b: b), back_state(lambda b: jnp.minimum(b + 1, nb - 1)),
            tile(128, True), tile(128, True), fixed(conv_rows8), fixed(head_rows), fixed(wide_rows),
            fixed(halves), fixed(select),
        ],
        out_specs=[
            tile(hc, True), tile(cc, True), tile(128, True),
            pl.BlockSpec((1, ranks, hc + cc), lambda s, b: (s, 0, 0)),
            pl.BlockSpec((1, ranks, hc), lambda s, b: (s, 0, 0)),
        ],
        out_shape=[
            shape(hc, bf16), shape(cc, bf16), shape(128, bf16),
            jax.ShapeDtypeStruct((seqs, ranks, hc + cc), f32),
            jax.ShapeDtypeStruct((seqs, ranks, hc), f32),
        ],
        scratch_shapes=[pltpu.VMEM((BLOCK + 8, cc), f32), pltpu.VMEM((hc, state), f32)],
        compiler_params=params,
        name="ssm_backward",
        cost_estimate=pl.CostEstimate(
            flops=2 * tokens * 8 * BLOCK * hc, bytes_accessed=50 << 20, transcendentals=0
        ),
    )(
        q, gate, ssm, vbc, pre, tok, rm, meta, doc_rows, states_low, states_low, rank_in,
        grad_rank_out, conv_rows8, head_rows, wide_rows, halves, select,
    )
    g_in_up = compact(g_in_up)
    g_in_up_gate, g_in_up_conv = g_in_up[..., :hc], g_in_up[..., hc:]
    g_out_down = compact(g_out_down)
    partial = jnp.concatenate(
        [
            mm("stc,dc->std", gp_gate, wb)
            + mm("stc,dc->std", gp_conv, wa[:, :conv_cols])
            + mm("sth,dh->std", g_step, wa[:, conv_cols + ranks :]),
            mm("stc,cr->str", gp_gate, up_gate) + mm("stc,cr->str", gp_conv, up_conv),
        ],
        -1,
    )
    partial = lax.psum_scatter(partial, "seq", scatter_dimension=1, tiled=True)
    grad_rank_in = (partial[..., width:] * mask).astype(bf16)
    down_in = wa[:, conv_cols : conv_cols + ranks]
    grad_normed = partial[..., :width] + mm("str,dr->std", grad_rank_in, down_in)
    own = layer_input.astype(f32)
    inv_own = lax.rsqrt(jnp.mean(own * own, -1, keepdims=True) + EPS)
    normed_own = (own * inv_own * gain).astype(bf16)
    g_in_down = compact(mm("str,std->srd", grad_rank_in, normed_own))
    scaled_in = grad_normed * gain
    grad_in = (
        inv_own * scaled_in
        - own * inv_own**3 * jnp.mean(scaled_in * own, -1, keepdims=True)
        + output_gradient.astype(f32)
    )

    def placed(parts, total):
        full = jnp.zeros((seqs, rank, total), f32)
        for part, start in parts:
            full = lax.dynamic_update_slice_in_dim(full, part, start, 2)
        return full

    everything = [
        g_in_down,
        placed(
            [
                (g_in_up_gate, here * hc),
                (g_in_up_conv[..., :hc], inner + here * hc),
                (g_in_up_conv[..., hc:], 2 * inner),
            ],
            cols,
        ),
        placed([(g_out_down, here * hc)], inner),
        g_out_up,
    ]
    owners = dps * n
    widths = [v.shape[-1] // owners for v in everything]
    packed = jnp.concatenate(
        [v.reshape(seqs, rank, owners, -1) for v in everything], -1
    ).transpose(2, 0, 1, 3)
    got = lax.all_to_all(packed, both, 0, 0, tiled=True)
    got = got.reshape(dps, n, seqs, rank, -1).sum(1)
    all_chosen = (every_index[..., None] == jnp.arange(adapters)).astype(f32)
    table = jnp.einsum("dsk,dsrc->krc", all_chosen, got, precision=lax.Precision.HIGHEST)
    cuts = [sum(widths[:i]) for i in range(len(widths) + 1)]
    grads = [table[..., cuts[i] : cuts[i + 1]] for i in range(len(widths))]
    return (output, grad_in, grads[0], grads[1], grads[2], grads[3])


def solution(mesh):
    return jax.shard_map(
        per_device,
        mesh=mesh,
        in_specs=(
            P("dp", "seq", None),
            P("dp", "seq"),
            P("dp"),
            P(("dp", "seq")),
            P(("dp", "seq"), None),
            P(("dp", "seq"), None),
            P(("dp", "seq"), None),
            P(("dp", "seq")),
            P(),
            P(),
            P(),
            P(("dp", "seq")),
            P(("dp", "seq"), None),
            P(None, None, ("dp", "seq")),
            P(None, None, ("dp", "seq")),
            P(None, None, ("dp", "seq")),
            P(None, None, ("dp", "seq")),
            P("dp", "seq", None),
        ),
        out_specs=(
            P("dp", "seq", None),
            P("dp", "seq", None),
            P(None, None, ("dp", "seq")),
            P(None, None, ("dp", "seq")),
            P(None, None, ("dp", "seq")),
            P(None, None, ("dp", "seq")),
        ),
        check_vma=False,
    )
```

profile of v0, /device:TPU:0, one launch (start us, length us, event | category | flops | bytes accessed | tf_op | source)
XLA Modules:
  0.0 656.0 jit_solution(9978315248882230004)
XLA Ops:
  21.1 41.8 %all_to_all.10 = bf16[4,48,2048]{2,1,0:T(8,128)(2,1)} all-to-all(bf16[4,48,2048]{2,1,0:T(8,128)(2,1)S(1)} %pad_maximum_fusion.1), channel_id=1, replica_groups=mesh['dp'=8,'seq'=4] {'seq'}, dimensions={0} | all-to-all | bytes 1572864 | tf_op jit(solution)/shard_map/all_to_all | solution.py:353
  64.2 5.2 all_gather.22
  74.6 4.3 all-gather.16.cloned.1.call-done
  88.2 48.4 %all-gather.14.cloned.1.call-done = bf16[768,1792]{1,0:T(8,128)(2,1)} async-done(((bf16[96,1792]{1,0:T(8,128)(2,1)}), bf16[768,1792]{1,0:T(8,128)(2,1)}) %all-gather.14.cloned.1.call-update) | async-done | bytes 2752528 | tf_op jit(solution)/shard_map/all_gather | solution.py:372
  137.7 3.4 slice.244.wo_ref
  141.7 94.8 %all-gather.10.cloned.1.call-done = bf16[1536,2048]{1,0:T(8,128)(2,1)} async-done(((bf16[192,2048]{1,0:T(8,128)(2,1)}), bf16[1536,2048]{1,0:T(8,128)(2,1)}) %all-gather.10.cloned.1.call-update) | async-done | bytes 6291472 | tf_op jit(solution)/shard_map/all_gather | solution.py:355
  236.5 3.3 slice.243.wb_ref
  239.7 4.3 slice.235.wa_ref
  244.1 38.5 %all-gather.8.cloned.1.call-done.x_ref = bf16[2,1024,1536]{2,1,0:T(8,128)(2,1)} async-done(((bf16[2,256,1536]{2,1,0:T(8,128)(2,1)}), bf16[2,1024,1536]{2,1,0:T(8,128)(2,1)}) %all-gather.8.cloned.1.call-update) | async-done | bytes 6291472 | tf_op jit(solution)/shard_map/all_gather | solution.py:332
  283.1 42.4 %ssm_forward.1 = (bf16[2,1024,1536]{2,1,0:T(8,128)(2,1)}, bf16[2,1024,128]{2,1,0:T(8,128)(2,1)}, bf16[2,1024,1024]{2,1,0:T(8,128)(2,1)}, f32[2,1024,1024]{2,1,0:...) custom-call(bf16[2,1024,1536]{2,1,0:T(8,128)(2,1)} %all-gather.8.cloned.1.call-done.x_r, ...), custom_call_target="tpu_custom_call" | custom-call | flops 10468982784 | bytes 41943040 | tf_op jit(solution)/shard_map/ssm_forward/pallas_call | solution.py:477
  325.5 4.8 all-gather.12.cloned.1.call-done.og_ref
  330.3 26.5 %gate_and_output.1 = (f32[2,1024,768]{2,1,0:T(8,128)}, f32[2,1024,768]{2,1,0:T(8,128)}, bf16[2,1024,128]{2,1,0:T(8,128)(2,1)}, f32[2,1024,1664]{2,1,0:T(8,128)}, f32[2,8,1024]{2,1,0:T(8,128)}) custom-call(bf16[2,1024,1536]{2,1,0:T(8,128)(2,1)} %get-tuple-element.23.normed_ref, bf16[2,1024,128]{2,1,0:T(8,128)(2,1)} %get-tuple-element.24.rank_ref, ...), custom_call_target="tpu_custom_call" | custom-call | flops 14495514624 | bytes 52428800 | tf_op jit(solution)/shard_map/gate_and_output/pallas_call | solution.py:502
  358.6 10.5 %psum.7 = f32[2,2,1024]{2,1,0:T(2,128)S(1)} all-reduce(f32[2,2,1024]{2,1,0:T(2,128)S(1)} %slice.213), channel_id=1, replica_groups=mesh['dp'=8,'seq'=4] {'seq'}, use_global_device_ids=true, to_apply=%region_1.2 | all-reduce | flops 4096 | bytes 32768 | tf_op jit(solution)/shard_map/psum | solution.py:524
  369.8 45.5 %ssm_backward.1 = (bf16[2,1024,768]{2,1,0:T(8,128)(2,1)}, bf16[2,1024,1024]{2,1,0:T(8,128)(2,1)}, bf16[2,1024,128]{2,1,0:T(8,128)(2,1)}, f32[2,128,1792]{2,1,0:T(8,128)}, f32[2,128,768]{2,1,0:T(8,128)}) custom-call(f32[2,1024,768]{2,1,0:T(8,128)} %get-tuple-element.29.q_ref, f32[2,1024,768]{2,1,0:T(8,128)} %get-tuple-element.30.g_ref, ...), custom_call_target="tpu_custom_call" | custom-call | flops 6442450944 | bytes 52428800 | tf_op jit(solution)/shard_map/ssm_backward/pallas_call | solution.py:544
  415.3 3.8 fusion.24
  420.2 7.2 %fusion.10 = f32[2,1024,1536]{2,1,0:T(8,128)S(1)} fusion(bf16[2,1024,768]{2,1,0:T(8,128)(2,1)S(1)} %copy-done.5, bf16[1536,2048]{1,0:T(8,128)(2,1)} %all-gather.10.cloned.1.call-done), kind=kOutput, calls=%fused_computation.20 | convolution fusion | flops 4831838208 | bytes 18087936 | tf_op jit(solution)/shard_map/stc,dc->std/dot_general | solution.py:17
  427.4 9.7 %fusion.8 = f32[2,1024,1536]{2,1,0:T(8,128)} fusion(bf16[2,1024,1024]{2,1,0:T(8,128)(2,1)S(1)} %copy-done.3, bf16[1536,2048]{1,0:T(8,128)(2,1)S(1)} %bitcast.133), kind=kOutput, calls=%fused_computation.18 | convolution fusion | flops 6442450944 | bytes 19922944 | tf_op jit(solution)/shard_map/stc,dc->std/dot_general | solution.py:17
  437.1 11.5 %add_add_fusion = f32[2,1024,1536]{2,1,0:T(8,128)} fusion(f32[2,1024,1536]{2,1,0:T(8,128)S(1)} %fusion.10, f32[2,1024,1536]{2,1,0:T(8,128)} %fusion.8, bf16[2,1024,128]{2,1,0:T(8,128)(2,1)S(1)} %copy-done.9, bf16[1536,2048]{1,0:T(8,128)(2,1)} %all-gather.10.cloned.1.call-done), kind=kOutput, calls=%fused_computation.1 | convolution fusion | flops 811597824 | bytes 38666240 | tf_op jit(solution)/shard_map/sth,dh->std/dot_general | solution.py:17
  448.6 10.5 %pad_maximum_fusion = f32[2,1024,1664]{2,1,0:T(8,128)} fusion(f32[2,1024,128]{2,1,0:T(8,128)S(1)} %convolution_add_fusion.2, f32[2,1024,1536]{2,1,0:T(8,128)} %add_add_fusion), kind=kLoop, calls=%fused_computation | loop fusion | flops 3407872 | bytes 27262976 | tf_op jit(solution)/shard_map/concatenate | solution.py:578
  475.0 96.5 %reduce-scatter.5.cloned.1.call-done = f32[2,256,1664]{2,1,0:T(8,128)} async-done(((f32[2,1024,1664]{2,1,0:T(8,128)}), f32[2,256,1664]{2,1,0:T(8,128)}) %reduce-scatter.5.cloned.1.call-update) | async-done | bytes 3407888 | tf_op jit(solution)/shard_map/reduce_scatter | solution.py:587
  571.5 5.3 fusion.1
  589.5 5.0 all-to-all-start.1
  597.7 3.7 fusion.9
  603.9 39.4 %all-to-all-done.1 = f32[32,2,16,392]{3,2,1,0:T(8,128)} async-done(((f32[32,2,16,392]{3,2,1,0:T(8,128)}), f32[32,2,16,392]{3,2,1,0:T(8,128)}, u32[]{:S(2)}, u32[]{:S(2)}) %all-to-all-start.1) | async-done | bytes 1605664 | tf_op jit(solution)/shard_map/all_to_all | solution.py:626
  (197 shorter events, 74.8 us)
Async XLA Ops:
  7.2 13.8 %slice-start.2 = ((bf16[48,6400]{1,0:T(8,128)(2,1)}), bf16[48,1024]{1,0:T(8,128)(2,1)S(1)}, s32[]{:S(2)}) async-start(bf16[48,6400]{1,0:T(8,128)(2,1)} %param.22), calls=%async_computation.13 | async-start | bytes 196608 | tf_op jit(solution)/shard_map/slice | solution.py:344
  7.2 71.7 %all-gather.16.cloned.1.call-start = ((), (), s32[]{:S(2)}) async-start(), calls=%async_computation.10 | async-start | bytes 2162688 | tf_op jit(solution)/shard_map/all_gather | solution.py:401
  12.1 124.5 %all-gather.14.cloned.1.call-start = ((), (), s32[]{:S(2)}) async-start(), calls=%async_computation.7 | async-start | bytes 3096576 | tf_op jit(solution)/shard_map/all_gather | solution.py:372
  14.8 0.7 collective-permute-start
  16.3 220.2 %all-gather.10.cloned.1.call-start = ((), (), s32[]{:S(2)}) async-start(), calls=%async_computation.5 | async-start | bytes 7077888 | tf_op jit(solution)/shard_map/all_gather | solution.py:355
  21.1 43.1 %copy-start.15 = (s32[2,256]{1,0:T(2,128)S(1)}, s32[2,256]{1,0:T(2,128)}, u32[]{:S(2)}) copy-start(s32[2,256]{1,0:T(2,128)} %param.19) | copy-start | bytes 6148
  21.1 49.1 %copy-start.16 = (f32[48]{0:T(128)S(1)}, f32[48]{0:T(128)}, u32[]{:S(2)}) copy-start(f32[48]{0:T(128)} %param.26) | copy-start | bytes 580
  21.1 49.1 %copy-start.17 = (f32[48]{0:T(128)S(1)}, f32[48]{0:T(128)}, u32[]{:S(2)}) copy-start(f32[48]{0:T(128)} %param.28) | copy-start | bytes 580
  21.1 49.2 %copy-start.18 = (s32[2]{0:T(128)S(1)}, s32[2]{0:T(128)}, u32[]{:S(2)}) copy-start(s32[2]{0:T(128)} %param.20) | copy-start | bytes 28
  62.9 10.4 %copy-start.19 = (f32[48]{0:T(128)S(1)}, f32[48]{0:T(128)}, u32[]{:S(2)}) copy-start(f32[48]{0:T(128)} %param.27) | copy-start | bytes 580
  62.9 219.6 %all-gather.8.cloned.1.call-start = ((), (), s32[]{:S(2)}) async-start(), calls=%async_computation.4 | async-start | bytes 7864320 | tf_op jit(solution)/shard_map/all_gather | solution.py:332
  63.5 266.8 %all-gather.12.cloned.1.call-start = ((), (), s32[]{:S(2)}) async-start(), calls=%async_computation.6 | async-start | bytes 7864320 | tf_op jit(solution)/shard_map/all_gather | solution.py:333
  64.1 400.4 %reduce-scatter.3.cloned.1.call-start = ((), (), s32[]{:S(2)}) async-start(), calls=%async_computation.8 | async-start | bytes 17039360 | tf_op jit(solution)/shard_map/reduce_scatter | solution.py:528
  70.5 506.9 %copy-start.11 = (f32[2,128]{1,0:T(2,128)}, f32[2,128]{1,0:T(2,128)S(1)}, u32[]{:S(2)}) copy-start(f32[2,128]{1,0:T(2,128)S(1)} %broadcast_in_dim.24) | copy-start | bytes 3076
  356.8 214.7 %reduce-scatter.5.cloned.1.call-start = ((), (), s32[]{:S(2)}) async-start(), calls=%async_computation.9 | async-start | bytes 17039360 | tf_op jit(solution)/shard_map/reduce_scatter | solution.py:587
  419.2 8.2 %slice-start = ((s8[6291456]{0:T(1024)(128)(4,1)}), s8[4194304]{0:T(1024)(128)(4,1)S(1)}, s32[]{:S(2)}) async-start(s8[6291456]{0:T(1024)(128)(4,1)} %bitcast.132), calls=%async_computation.11 | async-start | bytes 8388608
  420.2 7.2 %slice-start.1 = ((s8[6291456]{0:T(1024)(128)(4,1)}), s8[2097152]{0:T(1024)(128)(4,1)S(1)}, s32[]{:S(2)}) async-start(s8[6291456]{0:T(1024)(128)(4,1)} %bitcast.132), calls=%async_computation.12 | async-start | bytes 4194304
  420.2 7.2 %copy-start.3 = (bf16[2,1024,1024]{2,1,0:T(8,128)(2,1)S(1)}, bf16[2,1024,1024]{2,1,0:T(8,128)(2,1)}, u32[]{:S(2)}) copy-start(bf16[2,1024,1024]{2,1,0:T(8,128)(2,1)} %get-tuple-element.36) | copy-start | bytes 12582916
  427.4 9.7 %copy-start.9 = (bf16[2,1024,128]{2,1,0:T(8,128)(2,1)S(1)}, bf16[2,1024,128]{2,1,0:T(8,128)(2,1)}, u32[]{:S(2)}) copy-start(bf16[2,1024,128]{2,1,0:T(8,128)(2,1)} %get-tuple-element.37) | copy-start | bytes 1572868
  468.8 102.8 %copy-start = (bf16[2,256,1536]{2,1,0:T(8,128)(2,1)S(1)}, bf16[2,256,1536]{2,1,0:T(8,128)(2,1)}, u32[]{:S(2)}) copy-start(bf16[2,256,1536]{2,1,0:T(8,128)(2,1)} %param.18) | copy-start | bytes 4718596
  589.5 53.9 %all-to-all-start.1 = ((f32[32,2,16,392]{3,2,1,0:T(8,128)}), f32[32,2,16,392]{3,2,1,0:T(8,128)}, u32[]{:S(2)}, u32[]{:S(2)}) async-start(f32[32,2,16,392]{3,2,1,0:T(8,128)} %copy.400), calls=%async_computation.3 | async-start | bytes 4194304 | tf_op jit(solution)/shard_map/all_to_all | solution.py:626
  595.9 5.5 copy-start.13
  595.9 5.5 copy-start.14
  596.7 4.7 copy-start.4
  (8 other events, 20.4 us)
Sparse Core Ops, SparseCore 0:
  12.2 66.6 all-gather.15
  81.7 54.9 all-gather.13
  138.8 97.6 all-gather.9
  237.9 44.5 all-gather.7
  283.9 46.3 all-gather.11
  357.0 105.9 reduce-scatter.2
  465.5 105.9 reduce-scatter.4
where the time goes:
time: 665 us; the launch traced here: 656 us
  waiting for transfers between devices  328 us (49%)
  Pallas kernels  114 us (17%)
  blocking collectives  57.4 us (9%)
  local copies, waits for them, and re-layouts  49.9 us (8%)
  matrix products  47 us (7%)
  other arithmetic  38.3 us (6%)
  between operations  15.1 us (2%)
    reduce_scatter x1, waiting for transfers between devices, per_device(): partial = lax.psum_scatter(partial, 'seq', scatter_dimension=1, tiled=True)  96.5 us
    all_gather x1, waiting for transfers between devices, per_device(): w_in = lax.all_gather(w_mine, 'dp', axis=0, tiled=True)  94.8 us
    all_gather x1, waiting for transfers between devices, per_device(): w_o = lax.all_gather(w_o, 'dp', axis=0, tiled=True)  48.4 us
    dot_general x9, matrix products, mm(): return jnp.einsum(form, a, b, preferred_element_type=f32)  46.4 us
    pallas_call x1, Pallas kernels, per_device(): pl.pallas_call(functools.partial(backward_kernel, hn=hn, hc=hc), grid=gri...  45.5 us
    pallas_call x1, Pallas kernels, per_device(): pl.pallas_call(functools.partial(forward_kernel, hn=hn, hc=hc), grid=grid...  42.4 us
    all_to_all x1, blocking collectives, per_device(): w_mine = lax.all_to_all(jnp.stack(per_target), 'seq', 0, 0, tiled=True)  41.8 us
    all_to_all x1, waiting for transfers between devices, per_device(): got = lax.all_to_all(packed, both, 0, 0, tiled=True)  39.4 us
  transfers between devices with their start and end apart: 9, of which 7 were waited for; matrix products, arithmetic and copies ran while one was open for 16% of the time, Pallas kernels for 13%

commit v1 on v0

v1 whole, which is shorter than its diff:
```python
import functools

import jax
import jax.numpy as jnp
from jax import lax
from jax.experimental import pallas as pl
from jax.experimental.pallas import tpu as pltpu
from jax.sharding import PartitionSpec as P

EPS = 1e-05
f32 = jnp.float32
bf16 = jnp.bfloat16
BLOCK = 256


def mm(form, a, b):
    return jnp.einsum(form, a, b, preferred_element_type=f32)


LOG2E = 1.4426950408889634
VMEM_BYTES = 66_000_000


def dot_nn(a, b):
    return lax.dot_general(a, b, (((1,), (0,)), ((), ())), preferred_element_type=f32)


def dot_nt(a, b):
    return lax.dot_general(a, b, (((1,), (1,)), ((), ())), preferred_element_type=f32)


def dot_tn(a, b):
    return lax.dot_general(a, b, (((0,), (0,)), ((), ())), preferred_element_type=f32)


def dot_exact(a, b):
    return lax.dot_general(
        a, b, (((1,), (0,)), ((), ())), preferred_element_type=f32, precision=lax.Precision.HIGHEST
    )


def sigmoid(v):
    return 0.5 * jnp.tanh(0.5 * v) + 0.5


def spread_pair(cols, j):
    rows = cols.shape[0]
    lane = lax.broadcasted_iota(jnp.int32, (rows, 128), 1)
    return jnp.where(lane < 64, cols[:, 2 * j : 2 * j + 1], cols[:, 2 * j + 1 : 2 * j + 2])


def spread_all(cols, pairs):
    return jnp.concatenate([spread_pair(cols, j) for j in range(pairs)], 1)


def per_head(v, select):
    hi = v.astype(bf16)
    lo = (v - hi.astype(f32)).astype(bf16)
    return dot_nn(hi, select) + dot_nn(lo, select)


def by_rank(t, rank):
    out = t[:rank]
    for k in range(rank, 128, rank):
        out = out + t[k : k + rank]
    return out


def fold(v, rank):
    return by_rank(v.T, rank)


def assemble(order_ref, base, pieces, target, sems):
    copies = []
    for i, piece in enumerate(pieces):
        size = piece.shape[0]
        at = pl.multiple_of(order_ref[base + i] * size, 16)
        copies.append(pltpu.make_async_copy(piece, target.at[pl.ds(at, size)], sems.at[i]))
    for copy in copies:
        copy.start()
    for copy in copies:
        copy.wait()


def choose(order_ref, b, blocks, target):
    for i, block in enumerate(blocks):

        @pl.when(order_ref[b] == i)
        def _(block=block):
            target[...] = block[0]


def forward_kernel(order_ref, *refs, hn, hc, count, base, total):
    (x0, x1, x2, x3, meta_ref, doc_ref, up_ref, conv_ref, head_ref, mask_ref, half_ref) = refs[:11]
    pieces = refs[11 : 11 + count]
    rest = refs[11 + count :]
    if base:
        carry_in, rest = rest[0], rest[8:]
    else:
        full_ref, rest = rest[0], rest[1:]
    normed_ref, rank_ref, vbc_ref, pre_ref, ssm_ref, state_ref, tok_ref, *rest = rest
    if base + 2 < total:
        carry_out, rest = rest[0], rest[1:]
    buf, carry, x_buf, wa_ref, gain_ref, sems, full_sem = rest
    pairs = hn // 2
    cc = hc + 256
    b = pl.program_id(0)
    last = b == pl.num_programs(0) - 1

    @pl.when(b == 0)
    def _():
        assemble(order_ref, 4, pieces, wa_ref, sems)
        gain_ref[...] = wa_ref[:, cc + 128 :].astype(f32).T[120:, :]
        if base:
            carry[...] = carry_in[0:hc, 0:128]
            for i in range(cc // 128):
                buf[0:8, 128 * i : 128 * i + 128] = carry_in[hc + 8 * i : hc + 8 * i + 8, :]
        else:
            pltpu.make_async_copy(wa_ref, full_ref, full_sem).start()
            carry[...] = jnp.zeros_like(carry)
            buf[0:8, :] = jnp.zeros((8, cc), f32)

    choose(order_ref, b + base, (x0, x1, x2, x3), x_buf)
    x = x_buf[...].astype(f32)
    inv = lax.rsqrt(jnp.mean(x * x, -1, keepdims=True) + EPS)
    normed = (x * inv * gain_ref[7:8, :]).astype(bf16)
    normed_ref[0] = normed
    pa = dot_nn(normed, wa_ref[...])
    rank = (pa[:, cc : cc + 128] * mask_ref[0, 0:1, :]).astype(bf16)
    rank_ref[0] = rank
    conv_in = (pa[:, :cc] + dot_nt(rank, up_ref[...])).astype(bf16).astype(f32)
    buf[8:, :] = conv_in
    meta = meta_ref[0]
    pre = conv_ref[4:5, :] + conv_ref[3:4, :] * conv_in
    for k in (1, 2, 3):
        pre = pre + conv_ref[3 - k : 4 - k, :] * (buf[8 - k : 8 - k + BLOCK, :] * meta[:, k - 1 : k])
    buf[0:8, :] = buf[BLOCK : BLOCK + 8, :]
    pre_ref[0] = pre
    vbc = (pre * sigmoid(pre)).astype(bf16)
    vbc_ref[0] = vbc
    values = vbc[:, :hc]
    in_state = vbc[:, hc : hc + 128]
    out_state = vbc[:, hc + 128 :]
    arg = pa[:, cc + 128 : cc + 256] + head_ref[0:1, :]
    dt = jnp.maximum(arg, 0.0) + jnp.log1p(jnp.exp(-jnp.abs(arg)))
    row = lax.broadcasted_iota(jnp.int32, (BLOCK, BLOCK), 0)
    col = lax.broadcasted_iota(jnp.int32, (BLOCK, BLOCK), 1)
    cum = dot_exact((row >= col).astype(f32), dt * head_ref[1:2, :])
    tok_ref[0, :, 0:128] = dt
    tok_ref[0, :, 128:256] = cum
    tok_ref[0, :, 256:384] = arg
    left = cum * LOG2E
    right = (left - jnp.log(jnp.maximum(dt, 1e-37)) * LOG2E).T
    ok = (row >= col) & (meta[:, 5:6] == doc_ref[0, 0])
    bias = jnp.where(ok, 0.0, -1e30)
    contact = dot_nt(out_state, in_state)
    entry = jnp.exp(cum) * meta[:, 3:4]
    weight = jnp.exp(cum[BLOCK - 1 :, :] - cum) * dt * meta[:, 4:5]
    state = carry[...]
    state_low = state.astype(bf16)
    state_ref[0, 0] = state_low
    readout = dot_nt(out_state, state_low)
    half = BLOCK // 2
    scaled = []
    for j in range(pairs):
        at = slice(128 * j, 128 * j + 128)
        v = values[:, at]
        ys = []
        for r0, c1 in ((0, half), (half, BLOCK)):
            ws = []
            for h in (2 * j, 2 * j + 1):
                e = jnp.exp2(
                    (left[r0 : r0 + half, h : h + 1] - right[h : h + 1, :c1])
                    + bias[r0 : r0 + half, :c1]
                )
                ws.append((contact[r0 : r0 + half, :c1] * e).astype(bf16))
            vv = jnp.concatenate([v[:c1] * half_ref[0:1, :], v[:c1] * half_ref[1:2, :]], 0)
            ys.append(dot_nn(jnp.concatenate(ws, 1), vv))
        y = jnp.concatenate(ys, 0)
        ssm_ref[0, :, at] = y + readout[:, at] * spread_pair(entry, j)
        scaled.append((v.astype(f32) * spread_pair(weight, j)).astype(bf16))
    local = dot_tn(jnp.concatenate(scaled, 1), in_state)
    passing = entry[BLOCK - 1 :, :]
    for h in range(hn):
        at = slice(64 * h, 64 * h + 64)
        carry[at, :] = passing[:, h : h + 1] * state[at] + local[at]

    @pl.when(last)
    def _():
        if base + 2 < total:
            carry_out[0:hc, :] = carry[...]
            for i in range(cc // 128):
                carry_out[hc + 8 * i : hc + 8 * i + 8, :] = buf[0:8, 128 * i : 128 * i + 128]
        if not base:
            pltpu.make_async_copy(wa_ref, full_ref, full_sem).wait()


def gate_kernel(order_ref, normed_ref, rank_ref, up_ref, *refs, hc, count):
    pieces = refs[:count]
    g_ref, full_ref, wb_ref, sems, full_sem = refs[count:]
    b = pl.program_id(0)
    full_copy = pltpu.make_async_copy(wb_ref, full_ref, full_sem)

    @pl.when(b == 0)
    def _():
        assemble(order_ref, 4, pieces, wb_ref, sems)
        full_copy.start()

    g_ref[0] = dot_nn(normed_ref[0], wb_ref[:, :hc]) + dot_nt(rank_ref[0], up_ref[...])

    @pl.when(b == pl.num_programs(0) - 1)
    def _():
        full_copy.wait()


def middle_kernel(order_ref, *refs, hc, width, rank, count):
    g_ref, vbc_ref, ssm_ref, og0, og1, og2, og3, upo_ref, row_ref, mask_ref = refs[:10]
    pieces = refs[10 : 10 + count]
    q_ref, gro_ref, *part_refs, stat_ref, og_buf, wo_ref, sems = refs[10 + count :]
    b = pl.program_id(0)

    @pl.when(b == 0)
    def _():
        assemble(order_ref, 4, pieces, wo_ref, sems)

    choose(order_ref, b, (og0, og1, og2, og3), og_buf)
    gate = g_ref[0]
    mixed = ssm_ref[0] + row_ref[0:1, :] * vbc_ref[0, :, :hc].astype(f32)
    gated = mixed * (gate * sigmoid(gate))
    og = og_buf[...]
    gro = (dot_nn(og, upo_ref[...]) * mask_ref[0, 0:1, :]).astype(bf16)
    gro_ref[0] = gro
    q = dot_nt(og, wo_ref[:, :width]) + dot_nt(gro, wo_ref[:, width : width + 128])
    q = q * row_ref[1:2, :]
    q_ref[0] = q
    lane = lax.broadcasted_iota(jnp.int32, (BLOCK, 128), 1)
    s0 = jnp.sum(gated * gated, -1, keepdims=True)
    s1 = jnp.sum(q * gated, -1, keepdims=True)
    stat_ref[0, 0:8, :] = jnp.where(lane == 0, s0, s1).T[:8]
    low = (gated * row_ref[1:2, :]).astype(bf16)
    part = dot_nn(low, wo_ref[:, :width]).astype(bf16)
    for i, part_ref in enumerate(part_refs):

        @pl.when(order_ref[b] == i)
        def _(part_ref=part_ref):
            part_ref[...] = part

    stat_ref[0, 8:, :] = fold(dot_nn(low, wo_ref[:, width : width + 128]) * mask_ref[0, 0:1, :], rank)


def backward_kernel(
    q_ref, g_ref, ssm_ref, vbc_ref, pre_ref, tok_ref, rm_ref, meta_ref, doc_ref, state_ref, next_ref,
    rank_ref, gro_ref, conv_ref, head_ref, row_ref, half_ref, select_ref, upg_ref, upc_ref, mask_ref,
    gpg_ref, gpc_ref, gs_ref, grads_ref, gri_ref,
    buf, carry,
    *, hn, hc, rank,
):
    pairs = hn // 2
    cc = hc + 256
    first = pl.program_id(0) == 0

    @pl.when(first)
    def _():
        carry[...] = jnp.zeros_like(carry)
        buf[BLOCK:, :] = jnp.zeros((8, cc), f32)
        grads_ref[...] = jnp.zeros_like(grads_ref)

    rm = jnp.concatenate([rm_ref[0]] * 16, 0).T
    inv = rm[:, 0:1]
    mean = rm[:, 1:2]
    meta = meta_ref[0]
    gate = g_ref[0]
    ssm = ssm_ref[0]
    q = q_ref[0]
    vbc = vbc_ref[0]
    values = vbc[:, :hc]
    values_f = values.astype(f32)
    in_state = vbc[:, hc : hc + 128]
    out_state = vbc[:, hc + 128 :]
    skip = row_ref[0:1, :]
    mixed = ssm + skip * values_f
    sg = sigmoid(gate)
    act = gate * sg
    gated = mixed * act
    gated_r = gated * inv
    grad_gated = inv * (q - gated_r * (inv * mean))
    gated_low = (gated_r * row_ref[1:2, :]).astype(bf16)
    grads_ref[0, :, hc + cc :] = grads_ref[0, :, hc + cc :] + by_rank(
        dot_tn(gro_ref[0], gated_low), rank
    )
    grad_mixed = grad_gated * act
    gp_gate = (grad_gated * mixed * (sg + act * (1.0 - sg))).astype(bf16)
    gpg_ref[0] = gp_gate
    gsum = grad_mixed.astype(bf16)
    gsum_f = gsum.astype(f32)

    dt = tok_ref[0, :, 0:128]
    cum = tok_ref[0, :, 128:256]
    arg = tok_ref[0, :, 256:384]
    scaled_cum = cum * LOG2E
    down = scaled_cum - jnp.log(jnp.maximum(dt, 1e-37)) * LOG2E
    across = scaled_cum.T
    row = lax.broadcasted_iota(jnp.int32, (BLOCK, BLOCK), 0)
    col = lax.broadcasted_iota(jnp.int32, (BLOCK, BLOCK), 1)
    ok = (col >= row) & (meta[:, 5:6] == doc_ref[0, 0])
    bias = jnp.where(ok, 0.0, -1e30)
    contact = dot_nt(in_state, out_state)
    entry = jnp.exp(cum) * meta[:, 3:4]
    weight = jnp.exp(cum[BLOCK - 1 :, :] - cum) * dt * meta[:, 4:5]
    later = carry[...]
    later_low = later.astype(bf16)
    grad_scaled = dot_nt(in_state, later_low)
    weight_wide = spread_all(weight, pairs)
    entry_wide = spread_all(entry, pairs)
    scaled = (values_f * weight_wide).astype(bf16)
    weighted = (gsum_f * entry_wide).astype(bf16)
    half = BLOCK // 2
    g_con = [jnp.zeros((half, BLOCK), f32), jnp.zeros((half, half), f32)]
    g_val = []
    for j in range(pairs):
        at = slice(128 * j, 128 * j + 128)
        v = values[:, at]
        gs = gsum[:, at]
        tops = []
        for i, (r0, c0) in enumerate(((0, 0), (half, half))):
            ws = []
            for side in (0, 1):
                h = 2 * j + side
                gw = dot_nt(v[r0 : r0 + half] * half_ref[side : side + 1, :], gs[c0:])
                e = jnp.exp2(
                    (across[h : h + 1, c0:] - down[r0 : r0 + half, h : h + 1])
                    + bias[r0 : r0 + half, c0:]
                )
                ws.append((contact[r0 : r0 + half, c0:] * e).astype(bf16))
                g_con[i] = g_con[i] + gw * e
            gg = jnp.concatenate([gs[c0:] * half_ref[0:1, :], gs[c0:] * half_ref[1:2, :]], 0)
            tops.append(dot_nn(jnp.concatenate(ws, 1), gg))
        g_val.append(jnp.concatenate(tops, 0))
    g_val = jnp.concatenate(g_val, 1) + grad_scaled * weight_wide
    con_low = jnp.concatenate(
        [g_con[0], jnp.concatenate([jnp.zeros((half, half), f32), g_con[1]], 1)], 0
    ).astype(bf16)
    g_in = dot_nn(con_low, out_state) + dot_nn(scaled, later_low)
    g_out = dot_tn(con_low, in_state) + dot_nn(weighted, state_ref[0, 0])
    select = select_ref[...]
    spent = per_head(values_f * g_val, select)
    gained = per_head(gsum_f * ssm, select)
    ends = later * next_ref[0, 0].astype(f32)
    parts = [jnp.sum(ends[64 * h : 64 * h + 64], 0, keepdims=True) for h in range(hn)]
    parts.append(jnp.zeros((128 - hn, 128), f32))
    last = jnp.sum(jnp.concatenate(parts, 0).T, 0, keepdims=True)
    where_last = lax.broadcasted_iota(jnp.int32, (BLOCK, 128), 0) == BLOCK - 1
    grad_cum = gained - spent + jnp.where(where_last, last, 0.0)
    grad_log = dot_exact((col >= row).astype(f32), grad_cum)
    sig = sigmoid(arg)
    gs_ref[0] = (
        spent * (sig / jnp.maximum(dt, 1e-37)) + head_ref[1:2, :] * grad_log * sig
    ).astype(bf16)
    passing = entry[BLOCK - 1 :, :]
    direct = dot_tn(weighted, out_state)
    for h in range(hn):
        at = slice(64 * h, 64 * h + 64)
        carry[at, :] = passing[:, h : h + 1] * later[at] + direct[at]

    pre = pre_ref[0]
    sp = sigmoid(pre)
    grad_out = jnp.concatenate([skip * grad_mixed + g_val, g_in, g_out], 1)
    grad_pre = grad_out * (sp + pre * sp * (1.0 - sp))
    buf[:BLOCK, :] = grad_pre
    total = conv_ref[3:4, :] * grad_pre
    for k in (1, 2, 3):
        total = total + conv_ref[3 - k : 4 - k, :] * (buf[k : k + BLOCK, :] * meta[:, 5 + k : 6 + k])
    buf[BLOCK:, :] = grad_pre[:8]
    gp_conv = total.astype(bf16)
    gpc_ref[0] = gp_conv
    rows = rank_ref[0]
    grads_ref[0, :, :hc] = grads_ref[0, :, :hc] + by_rank(dot_tn(rows, gp_gate), rank)
    grads_ref[0, :, hc : hc + cc] = grads_ref[0, :, hc : hc + cc] + by_rank(
        dot_tn(rows, gp_conv), rank
    )
    gri_ref[0] = fold(
        (dot_nn(gp_gate, upg_ref[...]) + dot_nn(gp_conv, upc_ref[...])) * mask_ref[0, 0:1, :], rank
    )


def input_gradient_kernel(order_ref, gpg_ref, gpc_ref, gs_ref, wa_ref, wb_ref, *outs, hc, cc):
    out = (
        dot_nt(gpg_ref[0], wb_ref[:, :hc])
        + dot_nt(gpc_ref[0], wa_ref[:, :cc])
        + dot_nt(gs_ref[0], wa_ref[:, cc + 128 :])
    ).astype(bf16)
    for i, out_ref in enumerate(outs):

        @pl.when(pl.program_id(0) == i)
        def _(out_ref=out_ref):
            out_ref[...] = out


def swap(v, axis, bit):
    size = lax.axis_size(axis)
    return lax.ppermute(v, axis, [(i, i ^ bit) for i in range(size)])


def put(pieces):
    rows = pieces[0][0].shape[0]
    out = jnp.zeros((len(pieces) * rows, pieces[0][0].shape[1]), pieces[0][0].dtype)
    for piece, slot in pieces:
        out = lax.dynamic_update_slice_in_dim(out, piece, slot * rows, 0)
    return out


def rotate(v, r):
    size = lax.axis_size("dp")
    return lax.ppermute(v, "dp", [(i, (i + 2 * r) % size) for i in range(size)])


def after(v, *others):
    return lax.optimization_barrier((v, others))[0]


def gather_seq(v):
    if lax.axis_size("seq") != 4:
        return lax.all_gather(v, "seq", axis=0, tiled=True)
    s = lax.axis_index("seq")
    far = swap(v, "seq", 2)
    return put([(v, s), (swap(v, "seq", 1), s ^ 1), (far, s ^ 2), (swap(far, "seq", 1), s ^ 3)])


def fence(*values):
    return lax.optimization_barrier(values)


def others(v):
    return [swap(v, "seq", k) for k in (1, 2, 3)]


def total_of(v, got):
    return (v + got[0]) + (got[1] + got[2])


def near_sums(k0, k1, k2, k3, r1, r3):
    return k0.astype(f32) + r1.astype(f32), (k2.astype(f32) + r3.astype(f32)).astype(bf16)


def scatter_plain(parts):
    v = jnp.concatenate(parts, 0).astype(f32)
    return lax.psum_scatter(v, "seq", scatter_dimension=0, tiled=True)


def per_device(
    layer_input,
    document_index,
    adapter_index,
    input_norm_gain,
    input_projection,
    step_projection,
    convolution_weight,
    convolution_bias,
    head_step_bias,
    log_decay_rate,
    head_skip_gain,
    gated_norm_gain,
    output_projection,
    adapter_input_down,
    adapter_input_up,
    adapter_output_down,
    adapter_output_up,
    output_gradient,
):
    both = ("dp", "seq")
    dps, n = lax.axis_size("dp"), lax.axis_size("seq")
    here = lax.axis_index("seq")
    seqs, own_len, width = layer_input.shape
    adapters, rank, _ = adapter_input_down.shape
    ranks = adapters * rank
    heads = head_step_bias.shape[0]
    inner = output_projection.shape[0] * dps * n
    cols = input_projection.shape[1]
    state2 = cols - 2 * inner
    state = state2 // 2
    taps = convolution_weight.shape[1]
    hn = heads // n
    hc = inner // n
    hd = inner // heads
    length = own_len * n
    nb = length // BLOCK

    staged = n == 4 and dps == 8
    rows = input_projection.shape[0]
    conv_cols = hc + state2
    wa_cols = conv_cols + ranks + 128
    shared = jnp.concatenate(
        [input_projection[:, 2 * inner :], adapter_input_down.reshape(ranks, rows).T], 1
    )
    late = adapter_output_up.reshape(ranks, rows).T
    doc_cols = -(-seqs * own_len // rows)
    doc_block = document_index.astype(bf16).reshape(-1)
    doc_block = jnp.pad(doc_block, (0, rows * doc_cols - doc_block.shape[0])).reshape(rows, -1)
    gap = jnp.zeros((rows, 127 - hn - doc_cols), bf16)
    payload = jnp.concatenate(
        [
            jnp.concatenate(
                [
                    input_projection[:, inner + t * hc : inner + (t + 1) * hc],
                    shared,
                    step_projection[:, t * hn : (t + 1) * hn],
                    gap,
                    doc_block,
                    input_norm_gain[:, None],
                ],
                1,
            )
            for t in range(n)
        ],
        0,
    )
    w_a = lax.all_to_all(payload, "seq", 0, 0, tiled=True)
    payload = jnp.concatenate(
        [
            jnp.concatenate([input_projection[:, t * hc : (t + 1) * hc], late], 1)
            for t in range(n)
        ],
        0,
    )

    up_rows = adapter_input_up.shape[2]
    conv_rows = convolution_weight.shape[0]
    wide = -(-conv_rows // 128) * 128

    def as_row(v):
        return jnp.pad(v, ((0, 0), (0, wide - v.shape[1])))

    misc = jnp.concatenate(
        [
            as_row(convolution_weight.T),
            as_row(convolution_bias[None]),
            as_row(adapter_index.astype(bf16)[None]),
            as_row(gated_norm_gain[None]),
        ],
        0,
    )
    misc_rows = misc.shape[0]
    small = jnp.concatenate([adapter_input_up.reshape(ranks, up_rows).T, misc.reshape(-1, 128)], 0)
    small = jnp.pad(small, ((0, -small.shape[0] % 16), (0, 0)))
    small_rows = small.shape[0]
    out_rows = output_projection.shape[0]
    w_o = jnp.concatenate([output_projection, adapter_output_down.reshape(ranks, out_rows).T], 1)
    to_head = [(dps * s + d, n * d + s) for d in range(dps) for s in range(n)]

    if staged:
        d = lax.axis_index("dp")
        y, z = d % 2, d // 2
        pair = put([(small, y), (swap(small, "dp", 1), 1 - y)])
        small = put(
            [(pair, z)] + [(rotate(pair, r), lax.rem(z + 4 - r, 4)) for r in (1, 2, 3)]
        )
        x_near = swap(layer_input, "seq", 1)
        w_a, payload, x_near = fence(w_a, payload, x_near)
        a1, a3, a0y = rotate(w_a, 1), rotate(w_a, 3), swap(w_a, "dp", 1)
        w_b = lax.all_to_all(payload, "seq", 0, 0, tiled=True)
        small_far = swap(small, "seq", 2)
        a1, a3, a0y, w_a, w_b, small, small_far, x0, x1, w_o = fence(
            a1, a3, a0y, w_a, w_b, small, small_far, layer_input[:1], layer_input[1:], w_o
        )
        a2 = rotate(w_a, 2)
        a1y, a3y = swap(a1, "dp", 1), swap(a3, "dp", 1)
        x_far0 = swap(x0, "seq", 2)
        small_near = swap(small, "seq", 1)
        small_both = swap(small_far, "seq", 1)
        a2, a1y, a3y, x_far0, small_near, small_both, w_b, x1 = fence(
            a2, a1y, a3y, x_far0, small_near, small_both, w_b, x1
        )
        small = put(
            [(small, here), (small_near, here ^ 1), (small_far, here ^ 2), (small_both, here ^ 3)]
        )
        a2y = swap(a2, "dp", 1)
        x_both0 = swap(x_far0, "seq", 1)
        wa_pieces = [w_a, a0y, a1, a1y, a2, a2y, a3, a3y]
        slots = []
        for r in (0, 1, 2, 3):
            at = 2 * lax.rem(z + 4 - r, 4) + y
            slots += [at, at ^ 1]
        slots = jnp.stack(slots).astype(jnp.int32)
        x_order = jnp.arange(4, dtype=jnp.int32) ^ here
        xs = [[layer_input, x_near, x_far0, x_both0]]
    else:
        w_b = lax.all_to_all(payload, "seq", 0, 0, tiled=True)
        w_o = lax.ppermute(w_o, both, to_head)
        small = lax.all_gather(lax.all_gather(small, "dp", tiled=True), "seq", tiled=True)
        wa_pieces = [lax.all_gather(w_a, "dp", tiled=True)]
        slots = jnp.zeros((1,), jnp.int32)
        x_order = jnp.arange(nb, dtype=jnp.int32)
        xs = [jnp.split(lax.all_gather(layer_input, "seq", axis=1, tiled=True), nb, axis=1)] * seqs
    docs = w_a[:, wa_cols - 1 - doc_cols : wa_cols - 1].reshape(n, -1)[:, : seqs * own_len]
    docs = jnp.moveaxis(docs.reshape(n, seqs, own_len), 0, 1).reshape(seqs, length)
    order = jnp.concatenate([x_order, slots])
    order_whole = jnp.concatenate([x_order, jnp.zeros((1,), jnp.int32)])

    small = small.reshape(n, dps, small_rows, 128)
    small = jnp.moveaxis(small, 0, 1).reshape(dps * n, small_rows, 128)
    up_full = small[:, :up_rows].reshape(cols, ranks)
    misc = small[:, up_rows : up_rows + misc_rows * wide // 128].reshape(dps * n, misc_rows, wide)
    conv_w = jnp.moveaxis(misc[:, :taps, :conv_rows], 1, 0).reshape(taps, -1).astype(f32)
    conv_b = misc[:, taps, :conv_rows].reshape(-1).astype(f32)
    every_index = misc[:, taps + 1, :seqs].reshape(dps, n, seqs)[:, 0].astype(jnp.int32)
    gate_gain = misc[:, taps + 2, :out_rows].reshape(-1).astype(f32)

    def mine(v, size, base=0):
        return lax.dynamic_slice_in_dim(v, base + here * size, size, 0)

    up_gate = mine(up_full, hc)
    up_conv = jnp.concatenate([mine(up_full, hc, inner), up_full[2 * inner :]], 0)
    conv_w = jnp.concatenate([mine(conv_w.T, hc), conv_w.T[inner:]], 0).T
    conv_b = jnp.concatenate([mine(conv_b, hc), conv_b[inner:]], 0)
    step_bias = mine(head_step_bias, hn)
    decay_rate = -jnp.exp(mine(log_decay_rate, hn))
    skip = mine(head_skip_gain, hn)
    gate_gain = mine(gate_gain, hc)

    chosen = (adapter_index[:, None] == jnp.arange(adapters, dtype=jnp.int32)[None, :]).astype(f32)
    mask = jnp.repeat(chosen, rank, axis=1)[:, None, :]

    doc_f = docs.astype(f32)

    def same_before(k):
        return jnp.pad(doc_f, ((0, 0), (k, 0)), constant_values=-1.0)[:, :length] == doc_f

    def same_after(k):
        return jnp.pad(doc_f, ((0, 0), (0, k)), constant_values=-1.0)[:, k:] == doc_f

    blocks = doc_f.reshape(seqs, nb, BLOCK)
    prior = jnp.concatenate([blocks[:, :1, 0], blocks[:, :-1, -1]], 1)
    keep = (blocks == prior[:, :, None]).reshape(seqs, length)
    ends = (blocks == blocks[:, :, -1:]).reshape(seqs, length)
    flags = [
        same_before(1), same_before(2), same_before(3), keep, ends, doc_f,
        same_after(1), same_after(2), same_after(3),
    ]
    meta = jnp.stack([v.astype(f32) for v in flags], -1)
    meta = jnp.pad(meta, ((0, 0), (0, 0), (0, 128 - len(flags))))
    doc_rows = blocks[:, :, None, :]

    def rows8(*vs):
        return jnp.pad(jnp.stack(vs), ((0, 8 - len(vs)), (0, 0)))

    conv_rows8 = rows8(conv_w[0], conv_w[1], conv_w[2], conv_w[3], conv_b)
    head_rows = rows8(
        jnp.pad(step_bias, (0, 128 - hn)), jnp.pad(decay_rate, (0, 128 - hn))
    )
    wide_rows = rows8(jnp.repeat(skip, hd), gate_gain)
    halves = jnp.pad(
        (jnp.arange(128)[None, :] // 64 == jnp.arange(2)[:, None]).astype(bf16), ((0, 14), (0, 0))
    )
    select = (jnp.arange(hc)[:, None] // hd == jnp.arange(128)[None, :]).astype(bf16)
    mask8 = jnp.broadcast_to(mask, (seqs, 8, ranks))
    cc = conv_cols
    anywhere = pl.BlockSpec(memory_space=pl.ANY)
    params = pltpu.CompilerParams(
        dimension_semantics=("arbitrary",), vmem_limit_bytes=VMEM_BYTES
    )

    def at(w, k=0):
        return pl.BlockSpec((1, BLOCK, w), lambda b, o: (k, b, 0))

    def once(v, *block):
        block = block or v.shape
        return pl.BlockSpec(block, lambda b, o: (0,) * len(block), pipeline_mode=pl.Buffered(1))

    def of_seq(v, s0):
        k = s0 if v.shape[0] > 1 else 0
        return pl.BlockSpec(
            (1,) + v.shape[1:], lambda b, o: (k, 0, 0), pipeline_mode=pl.Buffered(1)
        )

    def one(w, dtype):
        return jax.ShapeDtypeStruct((1, length, w), dtype)

    def cost(flops, mib):
        return pl.CostEstimate(flops=int(flops), bytes_accessed=mib << 20, transcendentals=0)

    def weight_scratch(pieces, *shape):
        return [
            pltpu.VMEM(shape, bf16), pltpu.SemaphoreType.DMA((len(pieces),)),
            pltpu.SemaphoreType.DMA,
        ]

    def forward(s0, base, order, blocks, pieces, held=()):
        def part(w, k=0):
            return pl.BlockSpec((1, BLOCK, w), lambda b, o: (k, b + base, 0))

        carry_shape = jax.ShapeDtypeStruct((hc + cc // 16, 128), f32)
        whole_w = jax.ShapeDtypeStruct((width, wa_cols), bf16)
        carry_spec = once(None, *carry_shape.shape)
        more = base + 2 < nb
        inputs = [*blocks, meta, doc_rows, up_conv, conv_rows8, head_rows, mask8, halves, *pieces]
        lead = 0 if base else 1
        return pl.pallas_call(
            functools.partial(
                forward_kernel, hn=hn, hc=hc, count=len(pieces), base=base, total=nb
            ),
            grid_spec=pltpu.PrefetchScalarGridSpec(
                num_scalar_prefetch=1,
                grid=(2,),
                in_specs=[
                    *(of_seq(v, s0) for v in blocks), part(128, s0),
                    pl.BlockSpec((1, 1, 1, BLOCK), lambda b, o: (s0, b + base, 0, 0)),
                    once(up_conv), once(conv_rows8), once(head_rows), of_seq(mask8, s0), once(halves),
                    *([anywhere] * len(pieces)),
                    *([carry_spec] + [anywhere] * 7 if base else []),
                ],
                out_specs=[
                    *([] if base else [anywhere]),
                    part(width), part(128), part(cc), part(cc), part(hc),
                    pl.BlockSpec((1, 1, hc, state), lambda b, o: (0, b + base, 0, 0)), part(384),
                    *([carry_spec] if more else []),
                ],
                scratch_shapes=[
                    pltpu.VMEM((BLOCK + 8, cc), f32), pltpu.VMEM((hc, state), f32),
                    pltpu.VMEM((BLOCK, width), bf16), pltpu.VMEM((width, wa_cols), bf16),
                    pltpu.VMEM((8, width), f32), pltpu.SemaphoreType.DMA((len(pieces),)),
                    pltpu.SemaphoreType.DMA,
                ],
            ),
            out_shape=[
                *([] if base else [whole_w]),
                one(width, bf16), one(128, bf16), one(cc, bf16), one(cc, f32), one(hc, f32),
                jax.ShapeDtypeStruct((1, nb, hc, state), bf16), one(384, f32),
                *([carry_shape] if more else []),
            ],
            input_output_aliases={2 + len(inputs) + i: lead + i for i in range(7)} if base else {},
            compiler_params=params,
            name="ssm_forward",
            cost_estimate=cost(2 * length * (width * wa_cols + 3 * BLOCK * hc), 20),
        )(order, *inputs, *held)

    def gates(order, normed, rank_in, pieces):
        return pl.pallas_call(
            functools.partial(gate_kernel, hc=hc, count=len(pieces)),
            grid_spec=pltpu.PrefetchScalarGridSpec(
                num_scalar_prefetch=1,
                grid=(nb,),
                in_specs=[at(width), at(128), once(up_gate), *([anywhere] * len(pieces))],
                out_specs=[at(hc), anywhere],
                scratch_shapes=weight_scratch(pieces, width, hc + ranks),
            ),
            out_shape=[one(hc, f32), jax.ShapeDtypeStruct((width, hc + ranks), bf16)],
            compiler_params=params,
            name="gate",
            cost_estimate=cost(2 * length * width * hc, 10),
        )(order, normed, rank_in, up_gate, *pieces)

    def middle(s0, order, gate, vbc, ssm, blocks, pieces):
        return pl.pallas_call(
            functools.partial(middle_kernel, hc=hc, width=width, rank=rank, count=len(pieces)),
            grid_spec=pltpu.PrefetchScalarGridSpec(
                num_scalar_prefetch=1,
                grid=(nb,),
                in_specs=[
                    at(hc), at(cc), at(hc), *(of_seq(v, s0) for v in blocks), once(up_out),
                    once(wide_rows), of_seq(mask8, s0), *([anywhere] * len(pieces)),
                ],
                out_specs=[
                    at(hc), at(128), *(once(None, BLOCK, width) for _ in range(nb)),
                    pl.BlockSpec((1, 8 + rank, BLOCK), lambda b, o: (0, 0, b)),
                ],
                scratch_shapes=[
                    pltpu.VMEM((BLOCK, width), bf16), pltpu.VMEM((hc, width + ranks), bf16),
                    pltpu.SemaphoreType.DMA((len(pieces),)),
                ],
            ),
            out_shape=[
                one(hc, f32), one(128, bf16),
                *(jax.ShapeDtypeStruct((BLOCK, width), bf16) for _ in range(nb)),
                jax.ShapeDtypeStruct((1, 8 + rank, length), f32),
            ],
            compiler_params=params,
            name="output_side",
            cost_estimate=cost(2 * length * width * hc * 2, 15),
        )(order, gate, vbc, ssm, *blocks, up_out, wide_rows, mask8, *pieces)

    def backward(s0, q, gate, ssm, vbc, pre, tok, rm, states_low, rank_in, grad_rank_out):
        def back(w, k=0):
            return pl.BlockSpec((1, BLOCK, w), lambda b: (k, nb - 1 - b, 0))

        def whole(v):
            return pl.BlockSpec(v.shape, lambda b: (0,) * v.ndim, pipeline_mode=pl.Buffered(1))

        def back_state(shift):
            return pl.BlockSpec(
                (1, 1, hc, state), lambda b: (0, jnp.minimum(nb - 1 - b + shift, nb - 1), 0, 0)
            )

        return pl.pallas_call(
            functools.partial(backward_kernel, hn=hn, hc=hc, rank=rank),
            grid=(nb,),
            in_specs=[
                back(hc), back(hc), back(hc), back(cc), back(cc), back(384),
                pl.BlockSpec((1, 8, BLOCK), lambda b: (0, 0, nb - 1 - b)), back(128, s0),
                pl.BlockSpec((1, 1, 1, BLOCK), lambda b: (s0, nb - 1 - b, 0, 0)),
                back_state(0), back_state(1), back(128), back(128), whole(conv_rows8),
                whole(head_rows), whole(wide_rows), whole(halves), whole(select), whole(up_gate),
                whole(up_conv), pl.BlockSpec((1,) + mask8.shape[1:], lambda b: (s0, 0, 0)),
            ],
            out_specs=[
                back(hc), back(cc), back(128),
                pl.BlockSpec((1, rank, 2 * hc + cc), lambda b: (0, 0, 0)),
                pl.BlockSpec((1, rank, BLOCK), lambda b: (0, 0, nb - 1 - b)),
            ],
            out_shape=[
                one(hc, bf16), one(cc, bf16), one(128, bf16),
                jax.ShapeDtypeStruct((1, rank, 2 * hc + cc), f32),
                jax.ShapeDtypeStruct((1, rank, length), f32),
            ],
            scratch_shapes=[
                pltpu.VMEM((BLOCK + 8, cc), f32), pltpu.VMEM((hc, state), f32),
            ],
            compiler_params=params,
            name="ssm_backward",
            cost_estimate=cost(2 * length * 8 * BLOCK * hc, 25),
        )(
            q, gate, ssm, vbc, pre, tok, rm, meta, doc_rows, states_low, states_low, rank_in,
            grad_rank_out, conv_rows8, head_rows, wide_rows, halves, select, up_gate, up_conv, mask8,
        )

    def input_gradient(blocks, gp_gate, gp_conv, g_step):
        steps = blocks.shape[0]

        def of(w):
            return pl.BlockSpec((1, BLOCK, w), lambda b, o: (0, o[b], 0))

        return pl.pallas_call(
            functools.partial(input_gradient_kernel, hc=hc, cc=cc),
            grid_spec=pltpu.PrefetchScalarGridSpec(
                num_scalar_prefetch=1,
                grid=(steps,),
                in_specs=[of(hc), of(cc), of(128), once(wa), once(wb)],
                out_specs=[once(None, BLOCK, width) for _ in range(steps)],
            ),
            out_shape=[jax.ShapeDtypeStruct((BLOCK, width), bf16) for _ in range(steps)],
            compiler_params=params,
            name="input_gradient",
            cost_estimate=cost(2 * steps * BLOCK * width * (hc + cc), 10),
        )(blocks, gp_gate, gp_conv, g_step, wa, wb)

    def own_tokens(v, axis):
        return lax.dynamic_slice_in_dim(v, here * own_len, own_len, axis)

    def with_adapter(rows_of, table, s0):
        wide_rows_of = jnp.tile(rows_of, (adapters, 1)) * mask[s0, 0][:, None].astype(bf16)
        return mm("rt,dr->td", wide_rows_of, table)

    def halves_of(s0, order, blocks, pieces, held=None):
        out, whole_w = None, None
        for base in range(0, nb, 2):
            if base:
                got = forward(s0, base, order_whole, blocks, [whole_w], (out[7], *out[:7]))
            else:
                first, *got = forward(s0, 0, order, blocks, pieces)
                whole_w = first if whole_w is None else whole_w
            got = yield got, whole_w
            out, whole_w = got

    if staged:
        wa_pieces, xs[0], w_b, x1 = fence(wa_pieces, xs[0], w_b, x1)
        scan = halves_of(0, order, xs[0], wa_pieces)
        held = next(scan)
        b1, b3, b0y = rotate(w_b, 1), rotate(w_b, 3), swap(w_b, "dp", 1)
        x_far1 = swap(x1, "seq", 2)
        held, b1, b3, b0y, w_b = fence(held, b1, b3, b0y, w_b)
        held = scan.send(held)
        b2, b1y, b3y = rotate(w_b, 2), swap(b1, "dp", 1), swap(b3, "dp", 1)
        w_o = lax.ppermute(w_o, both, to_head)
        held, b2, b1y, b3y, x_far1, w_o = fence(held, b2, b1y, b3y, x_far1, w_o)
        fwd0, wa = held
        xs.append([layer_input, x_near, x_far1, swap(x_far1, "seq", 1)])
        xs[1], b2, w_o, og0, og1 = fence(xs[1], b2, w_o, output_gradient[:1], output_gradient[1:])
        scan = halves_of(1, order_whole, xs[1], [wa])
        held = next(scan)
        b2y = swap(b2, "dp", 1)
        o1, o3, o0y = rotate(w_o, 1), rotate(w_o, 3), swap(w_o, "dp", 1)
        og_far0 = swap(og0, "seq", 2)
        held, b2y, o1, o3, o0y, w_o = fence(held, b2y, o1, o3, o0y, w_o)
        held = scan.send((held[0], wa))
        o2, o1y, o3y = rotate(w_o, 2), swap(o1, "dp", 1), swap(o3, "dp", 1)
        og_near = swap(output_gradient, "seq", 1)
        held, o2, o1y, o3y, og_far0, og_near, og1 = fence(
            held, o2, o1y, o3y, og_far0, og_near, og1
        )
        fwd = [fwd0, held[0]]
        wb_pieces = [w_b, b0y, b1, b1y, b2, b2y, b3, b3y]
        gate0, wb = gates(order, fwd[0][0], fwd[0][1], wb_pieces)
        o2y = swap(o2, "dp", 1)
        og_far1 = swap(og1, "seq", 2)
        og_both0 = swap(og_far0, "seq", 1)
        gate0, wb, o2y, og_both0 = fence(gate0, wb, o2y, og_both0)
        gate1, _ = gates(order_whole, fwd[1][0], fwd[1][1], [wb])
        wo_pieces = [w_o, o0y, o1, o1y, o2, o2y, o3, o3y]
        gate1, og_far1 = fence(gate1, og_far1)
        og_both1 = swap(og_far1, "seq", 1)
        ogs = [
            [output_gradient, og_near, og_far0, og_both0],
            [output_gradient, og_near, og_far1, og_both1],
        ]
    else:
        fwd = []
        for s0 in range(seqs):
            scan = halves_of(s0, order, xs[s0], wa_pieces)
            held = next(scan)
            for _ in range(nb // 2 - 1):
                held = scan.send(held)
            fwd.append(held[0])
            wa = held[1]
        wb_pieces = [lax.all_gather(w_b, "dp", tiled=True)]
        gate0, wb = gates(order, fwd[0][0], fwd[0][1], wb_pieces)
        gate1, _ = gates(order_whole, fwd[1][0], fwd[1][1], [wb])
        wo_pieces = [lax.all_gather(w_o, "dp", tiled=True)]
        full = lax.all_gather(output_gradient, "seq", axis=1, tiled=True)
        ogs = [jnp.split(full, nb, axis=1)] * seqs
    up_out = wb[:, hc:]
    gain = wa[:, -1].astype(f32)
    gates_pre = [gate0, gate1]

    def side(s0):
        return middle(s0, order, gates_pre[s0], fwd[s0][2], fwd[s0][4], ogs[s0], wo_pieces)

    def normalisers(stats):
        inv_gated = lax.rsqrt(stats[:1] / inner + EPS)
        rm = jnp.pad(jnp.concatenate([inv_gated, stats[1:2] / inner], 0), ((0, 6), (0, 0)))[None]
        return inv_gated, rm, own_tokens((stats[8:] * inv_gated).astype(bf16), 1)

    def scan_back(s0, q, rm, grad_rank_out):
        _, rank_in, vbc, pre, ssm, states_low, tok = fwd[s0][:7]
        return backward(
            s0, q, gates_pre[s0], ssm, vbc, pre, tok, rm, states_low, rank_in, grad_rank_out
        )

    def layer_output(s0, branch, inv_gated, rank_out):
        return (
            layer_input[s0].astype(f32)
            + branch * own_tokens(inv_gated, 1).T
            + with_adapter(rank_out, up_out, s0)
        ).astype(bf16)

    def down_gradient(s0, grad_rank_in):
        return mm("rt,td->rd", grad_rank_in, fwd[s0][0][0]).astype(bf16)

    def layer_gradient(s0, partial, grad_rank_in):
        grad_normed = partial + with_adapter(
            own_tokens(grad_rank_in, 1), wa[:, cc : cc + ranks], s0
        )
        own = layer_input[s0].astype(f32)
        inv_own = lax.rsqrt(jnp.mean(own * own, -1, keepdims=True) + EPS)
        scaled_in = grad_normed * gain
        return (
            inv_own * scaled_in
            - own * inv_own**3 * jnp.mean(scaled_in * own, -1, keepdims=True)
            + output_gradient[s0].astype(f32)
        )

    if staged:
        gates_pre[1], ogs, wo_pieces = fence(gates_pre[1], ogs, wo_pieces)
        q0, gro0, *part0, stats0 = side(0)
        q0, gro0, part0, stats0 = fence(q0, gro0, part0, stats0)
        q1, gro1, *part1, stats1 = side(1)
        got = others(stats0[0])
        r3, r1 = swap(part0[3], "seq", 1), swap(part0[1], "seq", 1)
        q1, gro1, part1, stats1, got, r3, r1, part0 = fence(
            q1, gro1, part1, stats1, got, r3, r1, part0
        )
        inv0, rm0, rank_out0 = normalisers(total_of(stats0[0], got))
        mine0, away0 = near_sums(*part0, r1, r3)
        rm0, mine0, away0, stats1 = fence(rm0, mine0, away0, stats1)

        back0 = scan_back(0, q0, rm0, gro0)
        far0 = swap(away0, "seq", 2)
        got = others(stats1[0])
        r3 = swap(part1[3], "seq", 1)
        back0, far0, got, r3, part1 = fence(back0, far0, got, r3, part1)
        gp_gate, gp_conv, g_step, compact0, gri0 = back0
        output0 = layer_output(0, mine0 + far0.astype(f32), inv0, rank_out0)
        inv1, rm1, rank_out1 = normalisers(total_of(stats1[0], got))
        gri0, rm1, output0 = fence(gri0, rm1, output0)

        four = here ^ jnp.array([3, 2, 1, 0], jnp.int32)
        parts = input_gradient(four, gp_gate, gp_conv, g_step)
        got = others(gri0[0])
        r1 = swap(part1[1], "seq", 1)
        parts, got, r1 = fence(parts, got, r1)
        gri0 = total_of(gri0[0], got).astype(bf16)
        mine1, away1 = near_sums(*part1, r1, r3)
        s3, s1 = swap(parts[0], "seq", 1), swap(parts[2], "seq", 1)
        mine_g0, away_g0 = near_sums(*parts[::-1], s1, s3)
        down0 = down_gradient(0, gri0)
        mine_g0, away_g0, mine1, away1, rm1, down0 = fence(
            mine_g0, away_g0, mine1, away1, rm1, down0
        )

        back1 = scan_back(1, q1, rm1, gro1)
        far_g0 = swap(away_g0, "seq", 2)
        far1 = swap(away1, "seq", 2)
        back1, far_g0, far1 = fence(back1, far_g0, far1)
        gp_gate, gp_conv, g_step, compact1, gri1 = back1
        far = input_gradient(four[:2], gp_gate, gp_conv, g_step)
        got = others(gri1[0])
        far, got = fence(far, got)
        s3 = swap(far[0], "seq", 1)
        gri1 = total_of(gri1[0], got).astype(bf16)
        output1 = layer_output(1, mine1 + far1.astype(f32), inv1, rank_out1)
        away_g1 = (far[1].astype(f32) + s3.astype(f32)).astype(bf16)
        away_g1, output1, gri1 = fence(away_g1, output1, gri1)

        near = input_gradient(four[2:], gp_gate, gp_conv, g_step)
        far_g1 = swap(away_g1, "seq", 2)
        g_out_up = mm("srt,std->srd", jnp.stack([rank_out0, rank_out1]), output_gradient)
        split = [compact0[0], compact1[0]]
        downs = [down0, down_gradient(1, gri1)]
        grad0 = layer_gradient(0, mine_g0 + far_g0.astype(f32), gri0)
        mine_g1 = near[1].astype(f32) + swap(near[0], "seq", 1).astype(f32)
    else:
        split, downs, ranks_out, outputs, grads_in = [], [], [], [], []
        for s0 in range(seqs):
            q, gro, *parts, stats = side(s0)
            inv_gated, rm, rank_out = normalisers(lax.psum(stats[0], "seq"))
            outputs.append(layer_output(s0, scatter_plain(parts), inv_gated, rank_out))
            gp_gate, gp_conv, g_step, compacted, gri = scan_back(s0, q, rm, gro)
            gri = lax.psum(gri[0], "seq").astype(bf16)
            parts = input_gradient(jnp.arange(nb, dtype=jnp.int32), gp_gate, gp_conv, g_step)
            split.append(compacted[0])
            downs.append(down_gradient(s0, gri))
            ranks_out.append(rank_out)
            grads_in.append(layer_gradient(s0, scatter_plain(parts), gri))
        g_out_up = mm("srt,std->srd", jnp.stack(ranks_out), output_gradient)
        output = jnp.stack(outputs)
        grad_in = jnp.stack(grads_in)

    g_out_up = g_out_up.astype(bf16)
    g_in_down = jnp.stack(downs)
    split = jnp.concatenate([jnp.stack(split).astype(bf16), g_out_up], -1).reshape(seqs * rank, -1)
    split = gather_seq(split).reshape(n, seqs, rank, -1)

    def by_heads(start):
        return jnp.concatenate([split[t, :, :, start : start + hc] for t in range(n)], -1)

    def summed(start, size):
        return split[..., start : start + size].astype(f32).sum(0).astype(bf16)

    full = [
        g_in_down,
        jnp.concatenate([by_heads(0), by_heads(hc), summed(2 * hc, state2)], -1),
        by_heads(2 * hc + state2),
        summed(3 * hc + state2, width),
    ]
    widths = [v.shape[-1] // (dps * n) for v in full]
    packed = jnp.concatenate(
        [
            lax.dynamic_index_in_dim(
                v.reshape(seqs, rank, dps, n, -1), here, 3, keepdims=False
            )
            for v in full
        ],
        -1,
    ).transpose(2, 0, 1, 3)
    got = lax.all_to_all(packed, "dp", 0, 0, tiled=True).astype(f32)
    if staged:
        output = jnp.stack([output0, output1])
        grad_in = jnp.stack([grad0, layer_gradient(1, mine_g1 + far_g1.astype(f32), gri1)])
    all_chosen = (every_index[..., None] == jnp.arange(adapters)).astype(f32)
    table = jnp.einsum("dsk,dsrc->krc", all_chosen, got, precision=lax.Precision.HIGHEST)
    cuts = [sum(widths[:i]) for i in range(len(widths) + 1)]
    grads = [table[..., cuts[i] : cuts[i + 1]] for i in range(len(widths))]
    return (output, grad_in, grads[0], grads[1], grads[2], grads[3])


def solution(mesh):
    return jax.shard_map(
        per_device,
        mesh=mesh,
        in_specs=(
            P("dp", "seq", None),
            P("dp", "seq"),
            P("dp"),
            P(("dp", "seq")),
            P(("dp", "seq"), None),
            P(("dp", "seq"), None),
            P(("dp", "seq"), None),
            P(("dp", "seq")),
            P(),
            P(),
            P(),
            P(("dp", "seq")),
            P(("dp", "seq"), None),
            P(None, None, ("dp", "seq")),
            P(None, None, ("dp", "seq")),
            P(None, None, ("dp", "seq")),
            P(None, None, ("dp", "seq")),
            P("dp", "seq", None),
        ),
        out_specs=(
            P("dp", "seq", None),
            P("dp", "seq", None),
            P(None, None, ("dp", "seq")),
            P(None, None, ("dp", "seq")),
            P(None, None, ("dp", "seq")),
            P(None, None, ("dp", "seq")),
        ),
        check_vma=False,
    )
```

time: 665 us -> 482 us (0.72)
  waiting for transfers between devices: 328 us -> 61.4 us
  Pallas kernels: 114 us -> 201 us
  starting transfers between devices: 5.95 us -> 81.1 us
  blocking collectives: 57.4 us -> 0 us
  matrix products: 47 us -> 11.9 us
  local copies, waits for them, and re-layouts: 49.9 us -> 72 us
  between operations: 15.1 us -> 2.39 us
    all_gather x5 -> x0, waiting for transfers between devices: 191 us -> none  [the longest x1 94.8 us: per_device(): w_in = lax.all_gather(w_mine, 'dp', axis=0, tiled=True)]
    reduce_scatter x2 -> x0, waiting for transfers between devices: 96.5 us -> none  [the longest x1 96.5 us: per_device(): partial = lax.psum_scatter(partial, 'seq', scatter_dimension=1, tiled=True)]
    pallas_call x3 -> x13, Pallas kernels: 114 us -> 201 us  [the longest x4 66.7 us: forward(): pl.pallas_call(functools.partial(forward_kernel, hn=hn, hc=hc, count=len(...]
    ppermute x1 -> x66, starting transfers between devices: 0.68 us -> 69.4 us  [the longest x53 38.8 us: swap(): return lax.ppermute(v, axis, [(i, i ^ bit) for i in range(size)])]
    ppermute x1 -> x66, waiting for transfers between devices: 0.01 us -> 51.2 us  [the longest x12 28.5 us: rotate(): return lax.ppermute(v, 'dp', [(i, (i + 2 * r) % size) for i in range(size)])]
    all_to_all x1 -> x0, blocking collectives: 41.8 us -> none  [per_device(): w_mine = lax.all_to_all(jnp.stack(per_target), 'seq', 0, 0, tiled=True)]
    dot_general x9 -> x7, matrix products: 46.4 us -> 11.6 us  [mm(): return jnp.einsum(form, a, b, preferred_element_type=f32)]
    all_to_all x1 -> x3, waiting for transfers between devices: 39.4 us -> 10.3 us  [the longest x1 8.32 us: per_device(): got = lax.all_to_all(packed, 'dp', 0, 0, tiled=True).astype(f32)]
  transfers between devices with their start and end apart: 9 -> 69, of which waited for: 7 -> 13; matrix products, arithmetic and copies ran while one was open for 16% -> 21% of each run, Pallas kernels for 13% -> 39%
where the time goes in v1:
time: 482 us; the launch traced here: 474 us
  Pallas kernels  201 us (42%)
  starting transfers between devices  81.1 us (17%)
  local copies, waits for them, and re-layouts  72 us (15%)
  waiting for transfers between devices  61.4 us (13%)
  other arithmetic  44.5 us (9%)
  matrix products  11.9 us (2%)
    pallas_call x4, Pallas kernels, forward(): pl.pallas_call(functools.partial(forward_kernel, hn=hn, hc=hc, count=len(...  66.7 us
    pallas_call x2, Pallas kernels, backward(): pl.pallas_call(functools.partial(backward_kernel, hn=hn, hc=hc, rank=rank...  50.4 us
    ppermute x53, starting transfers between devices, swap(): return lax.ppermute(v, axis, [(i, i ^ bit) for i in range(size)])  38.8 us
    pallas_call x2, Pallas kernels, middle(): pl.pallas_call(functools.partial(middle_kernel, hc=hc, width=width, rank=...  33 us
    pallas_call x3, Pallas kernels, input_gradient(): pl.pallas_call(functools.partial(input_gradient_kernel, hc=hc, cc=cc), gr...  32.4 us
    ppermute x12, waiting for transfers between devices, rotate(): return lax.ppermute(v, 'dp', [(i, (i + 2 * r) % size) for i in range(size)])  28.5 us
    ppermute x12, starting transfers between devices, rotate(): return lax.ppermute(v, 'dp', [(i, (i + 2 * r) % size) for i in range(size)])  26.7 us
    ppermute x53, waiting for transfers between devices, swap(): return lax.ppermute(v, axis, [(i, i ^ bit) for i in range(size)])  22.6 us
  transfers between devices with their start and end apart: 69, of which 13 were waited for; matrix products, arithmetic and copies ran while one was open for 21% of the time, Pallas kernels for 39%

profile of v1, /device:TPU:0, one launch (start us, length us, event | category | flops | bytes accessed | tf_op | source)
XLA Modules:
  0.0 473.9 jit_solution(11689186429234826832)
XLA Ops:
  8.2 4.2 all-to-all-start
  51.5 4.1 all-to-all-start.1
  58.5 4.0 collective-permute-done.8
  84.8 15.1 %collective-permute-done.9.refs_15_ = bf16[192,1280]{1,0:T(8,128)(2,1)} collective-permute-done((bf16[192,1280]{1,0:T(8,128)(2,1)}, bf16[192,1280]{1,0:T(8,128)(2,1)}, u32[]{:S(2)}, u32[]{:S(2)}) %collective-permute-start.9) | collective-permute-done | bytes 491552 | tf_op jit(solution)/shard_map/ppermute | solution.py:414
  99.9 4.7 %collective-permute-done.12.refs_2_ = bf16[1,256,1536]{2,1,0:T(8,128)(2,1)} collective-permute-done((bf16[1,256,1536]{2,1,0:T(8,128)(2,1)}, bf16[1,256,1536]{2,1,0:T(8,128)(2,1)}, u32[]{:S(2)}, u32[]{:S(2)}) %collective-permute-start.12) | collective-permute-done | bytes 786464 | tf_op jit(solution)/shard_map/ppermute | solution.py:401
  109.3 4.4 collective-permute-done.15.refs_16_
  113.7 4.0 collective-permute-start.18
  120.9 16.7 %ssm_forward.4 = (bf16[1536,1280]{1,0:T(8,128)(2,1)}, bf16[1,1024,1536]{2,1,0:T(8,128)(2,1)}, bf16[1,1024,128]{2,1,0:T(8,128)(2,1)}, bf16[1,1024,1024]{2,1,0:T(8...) custom-call(s32[12]{0:T(128)} %concatenate.88.order_ref, ...), custom_call_target="tpu_custom_call" | custom-call | flops 5234491392 | bytes 20971520 | tf_op jit(solution)/shard_map/ssm_forward/pallas_call | solution.py:697
  139.7 16.5 %ssm_forward.5 = (bf16[1,1024,1536]{2,1,0:T(8,128)(2,1)}, bf16[1,1024,128]{2,1,0:T(8,128)(2,1)}, bf16[1,1024,1024]{2,1,0:T(8,128)(2,1)}, f32[1,1024,1024]{2,1,0:...) custom-call(s32[5]{0:T(128)} %pad_add_fusion.order_ref, ...), custom_call_target="tpu_custom_call", output_to_operand_aliasing={{0}: (14, {}), {1}: (15, {}), {2}: (16, {}), {3}: (17, {}),... | custom-call | flops 5234491392 | bytes 20971520 | tf_op jit(solution)/shard_map/ssm_forward/pallas_call | solution.py:697
  166.3 6.6 %collective-permute-done.27.refs_12_ = bf16[96,1664]{1,0:T(8,128)(2,1)S(1)} collective-permute-done((bf16[96,1664]{1,0:T(8,128)(2,1)}, bf16[96,1664]{1,0:T(8,128)(2,1)S(1)}, u32[]{:S(2)}, u32[]{:S(2)}) %collective-permute-start.27) | collective-permute-done | bytes 319520 | tf_op jit(solution)/shard_map/ppermute | solution.py:414
  174.7 17.1 %ssm_forward.6 = (bf16[1536,1280]{1,0:T(8,128)(2,1)}, bf16[1,1024,1536]{2,1,0:T(8,128)(2,1)}, bf16[1,1024,128]{2,1,0:T(8,128)(2,1)}, bf16[1,1024,1024]{2,1,0:T(8...) custom-call(s32[5]{0:T(128)} %pad_add_fusion.order_ref, ...), custom_call_target="tpu_custom_call" | custom-call | flops 5234491392 | bytes 20971520 | tf_op jit(solution)/shard_map/ssm_forward/pallas_call | solution.py:697
  192.7 7.0 %collective-permute-start.30 = (bf16[96,1664]{1,0:T(8,128)(2,1)}, bf16[96,1664]{1,0:T(8,128)(2,1)}, u32[]{:S(2)}, u32[]{:S(2)}) collective-permute-start(bf16[96,1664]{1,0:T(8,128)(2,1)} %collective-permute-done.24.refs_10_), channel_id=1, source_target_pairs={{0,16},{4,20},{8,24},{12,28},{16,0},{20,4},{24,8},{28,12},{1,17},{... | collective-permute-start | bytes 958472 | tf_op jit(solution)/shard_map/ppermute | solution.py:414
  201.7 16.5 %ssm_forward.7 = (bf16[1,1024,1536]{2,1,0:T(8,128)(2,1)}, bf16[1,1024,128]{2,1,0:T(8,128)(2,1)}, bf16[1,1024,1024]{2,1,0:T(8,128)(2,1)}, f32[1,1024,1024]{2,1,0:...) custom-call(s32[5]{0:T(128)} %pad_add_fusion.order_ref, ...), custom_call_target="tpu_custom_call", output_to_operand_aliasing={{0}: (14, {}), {1}: (15, {}), {2}: (16, {}), {3}: (17, {}),... | custom-call | flops 5234491392 | bytes 20971520 | tf_op jit(solution)/shard_map/ssm_forward/pallas_call | solution.py:697
  220.7 9.0 %gate.2 = (f32[1,1024,768]{2,1,0:T(8,128)}, bf16[1536,896]{1,0:T(8,128)(2,1)}) custom-call(s32[12]{0:T(128)} %concatenate.88.order_ref, bf16[1,1024,1536]{2,1,0:T(8,128)(2,1)} %get-tuple-element.316.normed_ref, bf16[1,1024,128]{2,1,0:T(8,128)(2,1)} %get-tuple-element.317.rank_ref, bf16[768,128]{1,0:T(8,128)(2,1)} %get-tuple-element.566.up_ref.upg_ref, ...), custom_call_target="tpu_custom_call" | custom-call | flops 2415919104 | bytes 10485760 | tf_op jit(solution)/shard_map/gate/pallas_call | solution.py:737
  229.8 9.0 %gate.3 = (f32[1,1024,768]{2,1,0:T(8,128)}, bf16[1536,896]{1,0:T(8,128)(2,1)}) custom-call(s32[5]{0:T(128)} %pad_add_fusion.order_ref, bf16[1,1024,1536]{2,1,0:T(8,128)(2,1)} %get-tuple-element.367.normed_ref, bf16[1,1024,128]{2,1,0:T(8,128)(2,1)} %get-tuple-element.368.rank_ref, bf16[768,128]{1,0:T(8,128)(2,1)} %get-tuple-element.566.up_ref.upg_ref, ...), custom_call_target="tpu_custom_call" | custom-call | flops 2415919104 | bytes 10485760 | tf_op jit(solution)/shard_map/gate/pallas_call | solution.py:737
  243.8 16.7 %output_side.2 = (f32[1,1024,768]{2,1,0:T(8,128)}, bf16[1,1024,128]{2,1,0:T(8,128)(2,1)}, bf16[256,1536]{1,0:T(8,128)(2,1)}, bf16[256,1536]{1,0:T(8,128)(2,1)}, ...) custom-call(s32[12]{0:T(128)} %concatenate.88.order_ref, ...), custom_call_target="tpu_custom_call" | custom-call | flops 4831838208 | bytes 15728640 | tf_op jit(solution)/shard_map/output_side/pallas_call | solution.py:753
  267.0 16.4 %output_side.3 = (f32[1,1024,768]{2,1,0:T(8,128)}, bf16[1,1024,128]{2,1,0:T(8,128)(2,1)}, bf16[256,1536]{1,0:T(8,128)(2,1)}, bf16[256,1536]{1,0:T(8,128)(2,1)}, ...) custom-call(s32[12]{0:T(128)} %concatenate.88.order_ref, ...), custom_call_target="tpu_custom_call" | custom-call | flops 4831838208 | bytes 15728640 | tf_op jit(solution)/shard_map/output_side/pallas_call | solution.py:753
  293.2 25.3 %ssm_backward.2 = (bf16[1,1024,768]{2,1,0:T(8,128)(2,1)}, bf16[1,1024,1024]{2,1,0:T(8,128)(2,1)}, bf16[1,1024,128]{2,1,0:T(8,128)(2,1)}, f32[1,16,2560]{2,1,0:T(8,128)}, f32[1,16,1024]{2,1,0:T(8,128)}) custom-call(f32[1,1024,768]{2,1,0:T(8,128)} %get-tuple-element.392.q_ref, f32[1,1024,768]{2,1,0:T(8,128)} %get-tuple-element.364.refs_0_.g_ref, ...), custom_call_target="tpu_custom_call" | custom-call | flops 3221225472 | bytes 26214400 | tf_op jit(solution)/shard_map/ssm_backward/pallas_call | solution.py:793
  327.9 13.7 %input_gradient.3 = (bf16[256,1536]{1,0:T(8,128)(2,1)}, bf16[256,1536]{1,0:T(8,128)(2,1)}, bf16[256,1536]{1,0:T(8,128)(2,1)}, bf16[256,1536]{1,0:T(8,128)(2,1)}) custom-call(s32[4]{0:T(128)} %copy-done.37, bf16[1,1024,768]{2,1,0:T(8,128)(2,1)} %get-tuple-element.446.gpg_ref, bf16[1,1024,1024]{2,1,0:T(8,128)(2,1)} %get-tuple-element.447.gpc_ref, ...), custom_call_target="tpu_custom_call" | custom-call | flops 5637144576 | bytes 10485760 | tf_op jit(solution)/shard_map/input_gradient/pallas_call | solution.py:831
  356.4 25.1 %ssm_backward.3 = (bf16[1,1024,768]{2,1,0:T(8,128)(2,1)}, bf16[1,1024,1024]{2,1,0:T(8,128)(2,1)}, bf16[1,1024,128]{2,1,0:T(8,128)(2,1)}, f32[1,16,2560]{2,1,0:T(8,128)}, f32[1,16,1024]{2,1,0:T(8,128)}) custom-call(f32[1,1024,768]{2,1,0:T(8,128)} %get-tuple-element.443.q_ref, f32[1,1024,768]{2,1,0:T(8,128)} %get-tuple-element.396.refs_0_.g_ref, ...), custom_call_target="tpu_custom_call" | custom-call | flops 3221225472 | bytes 26214400 | tf_op jit(solution)/shard_map/ssm_backward/pallas_call | solution.py:793
  381.5 7.7 %collective-permute-done.56 = bf16[256,1536]{1,0:T(8,128)(2,1)} collective-permute-done((bf16[256,1536]{1,0:T(8,128)(2,1)}, bf16[256,1536]{1,0:T(8,128)(2,1)}, u32[]{:S(2)}, u32[]{:S(2)}) %collective-permute-start.56) | collective-permute-done | bytes 786464 | tf_op jit(solution)/shard_map/ppermute | solution.py:401
  398.0 9.5 %input_gradient.4 = (bf16[256,1536]{1,0:T(8,128)(2,1)}, bf16[256,1536]{1,0:T(8,128)(2,1)}) custom-call(s32[2]{0:T(128)} %get-tuple-element.602.order_ref, bf16[1,1024,768]{2,1,0:T(8,128)(2,1)} %get-tuple-element.477.gpg_ref, bf16[1,1024,1024]{2,1,0:T(8,128)(2,1)} %get-tuple-element.478.gpc_ref, bf16[1,1024,128]{2,1,0:T(8,128)(2,1)} %get-tuple-element.479.gs_ref, ...), custom_call_target="tpu_custom_call" | custom-call | flops 2818572288 | bytes 10485760 | tf_op jit(solution)/shard_map/input_gradient/pallas_call | solution.py:831
  410.9 9.3 %input_gradient.5 = (bf16[256,1536]{1,0:T(8,128)(2,1)}, bf16[256,1536]{1,0:T(8,128)(2,1)}) custom-call(s32[2]{0:T(128)} %get-tuple-element.601.order_ref, bf16[1,1024,768]{2,1,0:T(8,128)(2,1)} %get-tuple-element.477.gpg_ref, bf16[1,1024,1024]{2,1,0:T(8,128)(2,1)} %get-tuple-element.478.gpc_ref, bf16[1,1024,128]{2,1,0:T(8,128)(2,1)} %get-tuple-element.479.gs_ref, ...), custom_call_target="tpu_custom_call" | custom-call | flops 2818572288 | bytes 10485760 | tf_op jit(solution)/shard_map/input_gradient/pallas_call | solution.py:831
  453.3 8.3 %all-to-all-done.2 = bf16[8,2,16,392]{3,1,2,0:T(2,128)(2,1)S(1)} async-done(((bf16[8,2,16,392]{3,1,2,0:T(2,128)(2,1)}), bf16[8,2,16,392]{3,1,2,0:T(2,128)(2,1)S(1)}, u32[]{:S(2)}, u32[]{:S(2)}) %all-to-all-start.2) | async-done | bytes 200736 | tf_op jit(solution)/shard_map/all_to_all | solution.py:1063
  (452 shorter events, 200.8 us)
Async XLA Ops:
  8.2 35.4 %all-to-all-start = ((bf16[4,48,1280]{2,1,0:T(8,128)(2,1)}), bf16[4,48,1280]{2,1,0:T(8,128)(2,1)}, u32[]{:S(2)}, u32[]{:S(2)}) async-start(bf16[4,48,1280]{2,1,0:T(8,128)(2,1)} %bitcast.11), calls=%async_computation | async-start | bytes 983040 | tf_op jit(solution)/shard_map/all_to_all | solution.py:517
  12.4 31.2 %collective-permute-start = (bf16[2,256,1536]{2,1,0:T(8,128)(2,1)S(1)}, bf16[2,256,1536]{2,1,0:T(8,128)(2,1)S(1)}, u32[]{:S(2)}, u32[]{:S(2)}) collective-permute-start(bf16[2,256,1536]{2,1,0:T(8,128)(2,1)S(1)} %copy-done), channel_id=1, source_target_pairs={{0,1},{1,0},{2,3},{3,2},{4,5},{5,4},{6,7},{7,6},{8,9},{9,8},{10,11... | collective-permute-start | bytes 4718600 | tf_op jit(solution)/shard_map/ppermute | solution.py:401
  67.6 32.3 %collective-permute-start.9 = (bf16[192,1280]{1,0:T(8,128)(2,1)}, bf16[192,1280]{1,0:T(8,128)(2,1)}, u32[]{:S(2)}, u32[]{:S(2)}) collective-permute-start(bf16[192,1280]{1,0:T(8,128)(2,1)} %bitcast.12.refs_11_), channel_id=1, source_target_pairs={{0,16},{4,20},{8,24},{12,28},{16,0},{20,4},{24,8},{28,12},{1,17},{... | collective-permute-start | bytes 1474568 | tf_op jit(solution)/shard_map/ppermute | solution.py:414
  71.4 28.5 %collective-permute-start.10 = (bf16[192,1280]{1,0:T(8,128)(2,1)}, bf16[192,1280]{1,0:T(8,128)(2,1)}, u32[]{:S(2)}, u32[]{:S(2)}) collective-permute-start(bf16[192,1280]{1,0:T(8,128)(2,1)} %collective-permute-done.1.refs_13_), channel_id=1, source_target_pairs={{0,4},{4,0},{8,12},{12,8},{16,20},{20,16},{24,28},{28,24},{1,5},{5... | collective-permute-start | bytes 1474568 | tf_op jit(solution)/shard_map/ppermute | solution.py:401
  71.9 28.0 %collective-permute-start.11 = (bf16[192,1280]{1,0:T(8,128)(2,1)}, bf16[192,1280]{1,0:T(8,128)(2,1)}, u32[]{:S(2)}, u32[]{:S(2)}) collective-permute-start(bf16[192,1280]{1,0:T(8,128)(2,1)} %collective-permute-done.2.refs_17_), channel_id=1, source_target_pairs={{0,4},{4,0},{8,12},{12,8},{16,20},{20,16},{24,28},{28,24},{1,5},{5... | collective-permute-start | bytes 1474568 | tf_op jit(solution)/shard_map/ppermute | solution.py:401
  73.5 31.2 %collective-permute-start.12 = (bf16[1,256,1536]{2,1,0:T(8,128)(2,1)}, bf16[1,256,1536]{2,1,0:T(8,128)(2,1)}, u32[]{:S(2)}, u32[]{:S(2)}) collective-permute-start(bf16[1,256,1536]{2,1,0:T(8,128)(2,1)} %get-tuple-element.259), channel_id=1, source_target_pairs={{0,2},{1,3},{2,0},{3,1},{4,6},{5,7},{6,4},{7,5},{8,10},{9,11},{10,... | collective-permute-start | bytes 2359304 | tf_op jit(solution)/shard_map/ppermute | solution.py:401
  80.9 75.3 %collective-permute-start.24 = (bf16[96,1664]{1,0:T(8,128)(2,1)}, bf16[96,1664]{1,0:T(8,128)(2,1)}, u32[]{:S(2)}, u32[]{:S(2)}) collective-permute-start(bf16[96,1664]{1,0:T(8,128)(2,1)} %pad_maximum_fusion.3), channel_id=1, source_target_pairs={{0,0},{8,1},{16,2},{24,3},{1,4},{9,5},{17,6},{25,7},{2,8},{10,9},{... | collective-permute-start | bytes 958472 | tf_op jit(solution)/shard_map/ppermute | solution.py:872
  120.1 36.2 %collective-permute-start.23 = (bf16[1,256,1536]{2,1,0:T(8,128)(2,1)}, bf16[1,256,1536]{2,1,0:T(8,128)(2,1)S(1)}, u32[]{:S(2)}, u32[]{:S(2)}) collective-permute-start(bf16[1,256,1536]{2,1,0:T(8,128)(2,1)} %get-tuple-element.314), channel_id=1, source_target_pairs={{0,2},{1,3},{2,0},{3,1},{4,6},{5,7},{6,4},{7,5},{8,10},{9,11},{10,... | collective-permute-start | bytes 2359304 | tf_op jit(solution)/shard_map/ppermute | solution.py:401
  156.4 61.8 %collective-permute-start.34 = (bf16[2,256,1536]{2,1,0:T(8,128)(2,1)}, bf16[2,256,1536]{2,1,0:T(8,128)(2,1)}, u32[]{:S(2)}, u32[]{:S(2)}) collective-permute-start(bf16[2,256,1536]{2,1,0:T(8,128)(2,1)} %refs_3_.1), channel_id=1, source_target_pairs={{0,1},{1,0},{2,3},{3,2},{4,5},{5,4},{6,7},{7,6},{8,9},{9,8},{10,11... | collective-permute-start | bytes 4718600 | tf_op jit(solution)/shard_map/ppermute | solution.py:401
  161.1 30.8 %collective-permute-start.28 = (bf16[96,1664]{1,0:T(8,128)(2,1)}, bf16[96,1664]{1,0:T(8,128)(2,1)S(1)}, u32[]{:S(2)}, u32[]{:S(2)}) collective-permute-start(bf16[96,1664]{1,0:T(8,128)(2,1)} %collective-permute-done.24.refs_10_), channel_id=1, source_target_pairs={{0,24},{4,28},{8,0},{12,4},{16,8},{20,12},{24,16},{28,20},{1,25},{... | collective-permute-start | bytes 958472 | tf_op jit(solution)/shard_map/ppermute | solution.py:414
  164.2 27.6 %collective-permute-start.29 = (bf16[96,1664]{1,0:T(8,128)(2,1)}, bf16[96,1664]{1,0:T(8,128)(2,1)}, u32[]{:S(2)}, u32[]{:S(2)}) collective-permute-start(bf16[96,1664]{1,0:T(8,128)(2,1)} %collective-permute-done.24.refs_10_), channel_id=1, source_target_pairs={{0,4},{4,0},{8,12},{12,8},{16,20},{20,16},{24,28},{28,24},{1,5},{5... | collective-permute-start | bytes 958472 | tf_op jit(solution)/shard_map/ppermute | solution.py:401
  172.9 45.4 %collective-permute-start.33 = (bf16[1,256,1536]{2,1,0:T(8,128)(2,1)}, bf16[1,256,1536]{2,1,0:T(8,128)(2,1)}, u32[]{:S(2)}, u32[]{:S(2)}) collective-permute-start(bf16[1,256,1536]{2,1,0:T(8,128)(2,1)} %get-tuple-element.360), channel_id=1, source_target_pairs={{0,2},{1,3},{2,0},{3,1},{4,6},{5,7},{6,4},{7,5},{8,10},{9,11},{10,... | collective-permute-start | bytes 2359304 | tf_op jit(solution)/shard_map/ppermute | solution.py:401
  290.0 28.6 %collective-permute-start.45 = (f32[24,1024]{1,0:T(8,128)S(1)}, f32[24,1024]{1,0:T(8,128)}, u32[]{:S(2)}, u32[]{:S(2)}) collective-permute-start(f32[24,1024]{1,0:T(8,128)S(1)} %bitcast.247), channel_id=1, source_target_pairs={{0,1},{1,0},{2,3},{3,2},{4,5},{5,4},{6,7},{7,6},{8,9},{9,8},{10,11... | collective-permute-start | bytes 294920 | tf_op jit(solution)/shard_map/ppermute | solution.py:401
  290.7 27.9 %collective-permute-start.46 = (f32[24,1024]{1,0:T(8,128)S(1)}, f32[24,1024]{1,0:T(8,128)}, u32[]{:S(2)}, u32[]{:S(2)}) collective-permute-start(f32[24,1024]{1,0:T(8,128)S(1)} %bitcast.248), channel_id=1, source_target_pairs={{0,2},{1,3},{2,0},{3,1},{4,6},{5,7},{6,4},{7,5},{8,10},{9,11},{10,... | collective-permute-start | bytes 294920 | tf_op jit(solution)/shard_map/ppermute | solution.py:401
  291.2 27.4 %collective-permute-start.47 = (f32[24,1024]{1,0:T(8,128)S(1)}, f32[24,1024]{1,0:T(8,128)}, u32[]{:S(2)}, u32[]{:S(2)}) collective-permute-start(f32[24,1024]{1,0:T(8,128)S(1)} %bitcast.249), channel_id=1, source_target_pairs={{0,3},{1,2},{2,1},{3,0},{4,7},{5,6},{6,5},{7,4},{8,11},{9,10},{10,... | collective-permute-start | bytes 294920 | tf_op jit(solution)/shard_map/ppermute | solution.py:401
  292.0 26.6 %collective-permute-start.44 = (bf16[256,1536]{1,0:T(8,128)(2,1)}, bf16[256,1536]{1,0:T(8,128)(2,1)S(1)}, u32[]{:S(2)}, u32[]{:S(2)}) collective-permute-start(bf16[256,1536]{1,0:T(8,128)(2,1)} %add_convert_fusion.3), channel_id=1, source_target_pairs={{0,2},{1,3},{2,0},{3,1},{4,6},{5,7},{6,4},{7,5},{8,10},{9,11},{10,... | collective-permute-start | bytes 2359304 | tf_op jit(solution)/shard_map/ppermute | solution.py:401
  352.5 29.0 %collective-permute-start.55 = (bf16[256,1536]{1,0:T(8,128)(2,1)}, bf16[256,1536]{1,0:T(8,128)(2,1)}, u32[]{:S(2)}, u32[]{:S(2)}) collective-permute-start(bf16[256,1536]{1,0:T(8,128)(2,1)} %add_convert_fusion.2), channel_id=1, source_target_pairs={{0,2},{1,3},{2,0},{3,1},{4,6},{5,7},{6,4},{7,5},{8,10},{9,11},{10,... | collective-permute-start | bytes 2359304 | tf_op jit(solution)/shard_map/ppermute | solution.py:401
  353.8 35.3 %collective-permute-start.56 = (bf16[256,1536]{1,0:T(8,128)(2,1)}, bf16[256,1536]{1,0:T(8,128)(2,1)}, u32[]{:S(2)}, u32[]{:S(2)}) collective-permute-start(bf16[256,1536]{1,0:T(8,128)(2,1)} %add_convert_fusion.1), channel_id=1, source_target_pairs={{0,2},{1,3},{2,0},{3,1},{4,6},{5,7},{6,4},{7,5},{8,10},{9,11},{10,... | collective-permute-start | bytes 2359304 | tf_op jit(solution)/shard_map/ppermute | solution.py:401
  389.2 31.0 %collective-permute-start.57 = (f32[16,1024]{1,0:T(8,128)}, f32[16,1024]{1,0:T(8,128)}, u32[]{:S(2)}, u32[]{:S(2)}) collective-permute-start(f32[16,1024]{1,0:T(8,128)} %bitcast.252), channel_id=1, source_target_pairs={{0,1},{1,0},{2,3},{3,2},{4,5},{5,4},{6,7},{7,6},{8,9},{9,8},{10,11... | collective-permute-start | bytes 196616 | tf_op jit(solution)/shard_map/ppermute | solution.py:401
  389.2 31.0 %collective-permute-start.58 = (f32[16,1024]{1,0:T(8,128)}, f32[16,1024]{1,0:T(8,128)}, u32[]{:S(2)}, u32[]{:S(2)}) collective-permute-start(f32[16,1024]{1,0:T(8,128)} %bitcast.253), channel_id=1, source_target_pairs={{0,2},{1,3},{2,0},{3,1},{4,6},{5,7},{6,4},{7,5},{8,10},{9,11},{10,... | collective-permute-start | bytes 196616 | tf_op jit(solution)/shard_map/ppermute | solution.py:401
  390.6 29.6 %collective-permute-start.59 = (f32[16,1024]{1,0:T(8,128)}, f32[16,1024]{1,0:T(8,128)}, u32[]{:S(2)}, u32[]{:S(2)}) collective-permute-start(f32[16,1024]{1,0:T(8,128)} %bitcast.254), channel_id=1, source_target_pairs={{0,3},{1,2},{2,1},{3,0},{4,7},{5,6},{6,5},{7,4},{8,11},{9,10},{10,... | collective-permute-start | bytes 196616 | tf_op jit(solution)/shard_map/ppermute | solution.py:401
  393.5 28.2 %collective-permute-start.63 = (bf16[32,4096]{1,0:T(8,128)(2,1)}, bf16[32,4096]{1,0:T(8,128)(2,1)}, u32[]{:S(2)}, u32[]{:S(2)}) collective-permute-start(bf16[32,4096]{1,0:T(8,128)(2,1)} %bitcast.78), channel_id=1, source_target_pairs={{0,1},{1,0},{2,3},{3,2},{4,5},{5,4},{6,7},{7,6},{8,9},{9,8},{10,11... | collective-permute-start | bytes 786440 | tf_op jit(solution)/shard_map/ppermute | solution.py:401
  393.8 27.8 %collective-permute-start.64 = (bf16[32,4096]{1,0:T(8,128)(2,1)}, bf16[32,4096]{1,0:T(8,128)(2,1)}, u32[]{:S(2)}, u32[]{:S(2)}) collective-permute-start(bf16[32,4096]{1,0:T(8,128)(2,1)} %bitcast.78), channel_id=1, source_target_pairs={{0,2},{1,3},{2,0},{3,1},{4,6},{5,7},{6,4},{7,5},{8,10},{9,11},{10,... | collective-permute-start | bytes 786440 | tf_op jit(solution)/shard_map/ppermute | solution.py:401
  420.2 44.6 %collective-permute-start.61 = (bf16[256,1536]{1,0:T(8,128)(2,1)}, bf16[256,1536]{1,0:T(8,128)(2,1)}, u32[]{:S(2)}, u32[]{:S(2)}) collective-permute-start(bf16[256,1536]{1,0:T(8,128)(2,1)} %get-tuple-element.494), channel_id=1, source_target_pairs={{0,1},{1,0},{2,3},{3,2},{4,5},{5,4},{6,7},{7,6},{8,9},{9,8},{10,11... | collective-permute-start | bytes 2359304 | tf_op jit(solution)/shard_map/ppermute | solution.py:401
  (98 other events, 1193.2 us)

commit v2 on v1

v2 whole, which is shorter than its diff:
```python
import functools

import jax
import jax.numpy as jnp
from jax import lax
from jax.experimental import pallas as pl
from jax.experimental.pallas import tpu as pltpu
from jax.sharding import PartitionSpec as P

EPS = 1e-05
f32 = jnp.float32
bf16 = jnp.bfloat16
BLOCK = 256


def mm(form, a, b):
    return jnp.einsum(form, a, b, preferred_element_type=f32)


LOG2E = 1.4426950408889634
VMEM_BYTES = 66_000_000


def dot_nn(a, b):
    return lax.dot_general(a, b, (((1,), (0,)), ((), ())), preferred_element_type=f32)


def dot_nt(a, b):
    return lax.dot_general(a, b, (((1,), (1,)), ((), ())), preferred_element_type=f32)


def dot_tn(a, b):
    return lax.dot_general(a, b, (((0,), (0,)), ((), ())), preferred_element_type=f32)


def dot_exact(a, b):
    return lax.dot_general(
        a, b, (((1,), (0,)), ((), ())), preferred_element_type=f32, precision=lax.Precision.HIGHEST
    )


def sigmoid(v):
    return 0.5 * jnp.tanh(0.5 * v) + 0.5


def spread_pair(cols, j):
    rows = cols.shape[0]
    lane = lax.broadcasted_iota(jnp.int32, (rows, 128), 1)
    return jnp.where(lane < 64, cols[:, 2 * j : 2 * j + 1], cols[:, 2 * j + 1 : 2 * j + 2])


def spread_all(cols, pairs):
    return jnp.concatenate([spread_pair(cols, j) for j in range(pairs)], 1)


def per_head(v, select):
    hi = v.astype(bf16)
    lo = (v - hi.astype(f32)).astype(bf16)
    return dot_nn(hi, select) + dot_nn(lo, select)


def by_rank(t, rank):
    out = t[:rank]
    for k in range(rank, 128, rank):
        out = out + t[k : k + rank]
    return out


def fold(v, rank):
    return by_rank(v.T, rank)


def shards(pieces, size):
    return [p.at[k : k + size] for p in pieces for k in range(0, p.shape[0], size)]


def assemble(order_ref, base, pieces, size, target, sems):
    copies = []
    for i, piece in enumerate(shards(pieces, size)):
        at = pl.multiple_of(order_ref[base + i] * size, 16)
        copies.append(pltpu.make_async_copy(piece, target.at[pl.ds(at, size)], sems.at[i]))
    for copy in copies:
        copy.start()
    for copy in copies:
        copy.wait()


def choose(order_ref, b, blocks, target):
    for i, block in enumerate(blocks):

        @pl.when(order_ref[b] == i)
        def _(block=block):
            target[...] = block[0]


def forward_kernel(order_ref, *refs, hn, hc, count, size, keep):
    (x0, x1, x2, x3, meta_ref, doc_ref, up_ref, conv_ref, head_ref, mask_ref, half_ref) = refs[:11]
    pieces = refs[11 : 11 + count]
    normed_ref, rank_ref, vbc_ref, pre_ref, ssm_ref, state_ref, tok_ref, *rest = refs[11 + count :]
    if keep:
        full_ref, rest = rest[0], rest[1:]
    buf, carry, x_buf, wa_ref, gain_ref, sems, full_sem = rest
    pairs = hn // 2
    cc = hc + 256
    b = pl.program_id(0)

    @pl.when(b == 0)
    def _():
        assemble(order_ref, 4, pieces, size, wa_ref, sems)
        if keep:
            pltpu.make_async_copy(wa_ref, full_ref, full_sem).start()
        gain_ref[...] = wa_ref[:, cc + 128 :].astype(f32).T[120:, :]
        carry[...] = jnp.zeros_like(carry)
        buf[0:8, :] = jnp.zeros((8, cc), f32)

    choose(order_ref, b, (x0, x1, x2, x3), x_buf)
    x = x_buf[...].astype(f32)
    inv = lax.rsqrt(jnp.mean(x * x, -1, keepdims=True) + EPS)
    normed = (x * inv * gain_ref[7:8, :]).astype(bf16)
    normed_ref[0] = normed
    pa = dot_nn(normed, wa_ref[...])
    rank = (pa[:, cc : cc + 128] * mask_ref[0, 0:1, :]).astype(bf16)
    rank_ref[0] = rank
    conv_in = (pa[:, :cc] + dot_nt(rank, up_ref[...])).astype(bf16).astype(f32)
    buf[8:, :] = conv_in
    meta = meta_ref[0]
    pre = conv_ref[4:5, :] + conv_ref[3:4, :] * conv_in
    for k in (1, 2, 3):
        pre = pre + conv_ref[3 - k : 4 - k, :] * (buf[8 - k : 8 - k + BLOCK, :] * meta[:, k - 1 : k])
    buf[0:8, :] = buf[BLOCK : BLOCK + 8, :]
    pre_ref[0] = pre
    vbc = (pre * sigmoid(pre)).astype(bf16)
    vbc_ref[0] = vbc
    values = vbc[:, :hc]
    in_state = vbc[:, hc : hc + 128]
    out_state = vbc[:, hc + 128 :]
    arg = pa[:, cc + 128 : cc + 256] + head_ref[0:1, :]
    dt = jnp.maximum(arg, 0.0) + jnp.log1p(jnp.exp(-jnp.abs(arg)))
    row = lax.broadcasted_iota(jnp.int32, (BLOCK, BLOCK), 0)
    col = lax.broadcasted_iota(jnp.int32, (BLOCK, BLOCK), 1)
    cum = dot_exact((row >= col).astype(f32), dt * head_ref[1:2, :])
    tok_ref[0, :, 0:128] = dt
    tok_ref[0, :, 128:256] = cum
    tok_ref[0, :, 256:384] = arg
    left = cum * LOG2E
    right = (left - jnp.log(jnp.maximum(dt, 1e-37)) * LOG2E).T
    ok = (row >= col) & (meta[:, 5:6] == doc_ref[0, 0])
    bias = jnp.where(ok, 0.0, -1e30)
    contact = dot_nt(out_state, in_state)
    entry = jnp.exp(cum) * meta[:, 3:4]
    weight = jnp.exp(cum[BLOCK - 1 :, :] - cum) * dt * meta[:, 4:5]
    state = carry[...]
    state_low = state.astype(bf16)
    state_ref[0, 0] = state_low
    readout = dot_nt(out_state, state_low)
    half = BLOCK // 2
    scaled = []
    for j in range(pairs):
        at = slice(128 * j, 128 * j + 128)
        v = values[:, at]
        ys = []
        for r0, c1 in ((0, half), (half, BLOCK)):
            ws = []
            for h in (2 * j, 2 * j + 1):
                e = jnp.exp2(
                    (left[r0 : r0 + half, h : h + 1] - right[h : h + 1, :c1])
                    + bias[r0 : r0 + half, :c1]
                )
                ws.append((contact[r0 : r0 + half, :c1] * e).astype(bf16))
            vv = jnp.concatenate([v[:c1] * half_ref[0:1, :], v[:c1] * half_ref[1:2, :]], 0)
            ys.append(dot_nn(jnp.concatenate(ws, 1), vv))
        y = jnp.concatenate(ys, 0)
        ssm_ref[0, :, at] = y + readout[:, at] * spread_pair(entry, j)
        scaled.append((v.astype(f32) * spread_pair(weight, j)).astype(bf16))
    local = dot_tn(jnp.concatenate(scaled, 1), in_state)
    passing = entry[BLOCK - 1 :, :]
    for h in range(hn):
        at = slice(64 * h, 64 * h + 64)
        carry[at, :] = passing[:, h : h + 1] * state[at] + local[at]

    if keep:

        @pl.when(b == pl.num_programs(0) - 1)
        def _():
            pltpu.make_async_copy(wa_ref, full_ref, full_sem).wait()


def route(order_ref, b, value, near_ref, pair_ref, far_ref):
    for k, target in enumerate(
        (near_ref, pair_ref.at[0:BLOCK], far_ref, pair_ref.at[BLOCK : 2 * BLOCK])
    ):

        @pl.when(order_ref[b] == k)
        def _(target=target):
            target[...] = value


def assemble_both(order_ref, base, pieces, rows, out_rows, wb_ref, wo_ref, sems):
    part = wb_ref.shape[1]
    copies = []
    for i, piece in enumerate(shards(pieces, rows + 2 * out_rows)):
        slot = order_ref[base + i]
        to = pl.ds(pl.multiple_of(slot * rows, 16), rows)
        to_out = pl.ds(pl.multiple_of(slot * out_rows, 16), out_rows)
        rest = wo_ref.shape[1] - part
        moves = (
            (piece.at[0:rows], wb_ref.at[to]),
            (piece.at[rows : rows + out_rows], wo_ref.at[to_out, 0:part]),
            (piece.at[rows + out_rows :, 0:rest], wo_ref.at[to_out, part : part + rest]),
        )
        for j, (source, target) in enumerate(moves):
            copies.append(pltpu.make_async_copy(source, target, sems.at[3 * i + j]))
    for copy in copies:
        copy.start()
    for copy in copies:
        copy.wait()


def middle_kernel(order_ref, *refs, hc, width, rank, count, keep, merged):
    (
        normed_ref, rank_ref, vbc_ref, ssm_ref, og0, og1, og2, og3, up_ref, row_ref, mask_ref,
    ) = refs[:11]
    gate_pieces = refs[11 : 11 + count]
    after_gate = 11 + count
    out_pieces = () if merged else refs[after_gate : after_gate + count]
    first_out = after_gate + len(out_pieces)
    g_ref, q_ref, gro_ref, near_ref, pair_ref, far_ref, stat_ref, *rest = refs[first_out:]
    if keep:
        wb_full, wo_full, rest = rest[0], rest[1], rest[2:]
    og_buf, wb_ref, wo_ref, sems, more_sems, full_sems = rest
    b = pl.program_id(0)

    def keeping():
        return (
            pltpu.make_async_copy(wb_ref, wb_full, full_sems.at[0]),
            pltpu.make_async_copy(wo_ref, wo_full, full_sems.at[1]),
        )

    @pl.when(b == 0)
    def _():
        if merged:
            assemble_both(order_ref, 4, gate_pieces, *merged, wb_ref, wo_ref, sems)
        else:
            assemble(order_ref, 4, gate_pieces, wb_ref.shape[0], wb_ref, sems)
            assemble(order_ref, 4, out_pieces, wo_ref.shape[0], wo_ref, more_sems)
        if keep:
            for copy in keeping():
                copy.start()

    choose(order_ref, b, (og0, og1, og2, og3), og_buf)
    gate = dot_nn(normed_ref[0], wb_ref[:, :hc]) + dot_nt(rank_ref[0], up_ref[...])
    g_ref[0] = gate
    mixed = ssm_ref[0] + row_ref[0:1, :] * vbc_ref[0, :, :hc].astype(f32)
    gated = mixed * (gate * sigmoid(gate))
    og = og_buf[...]
    gro = (dot_nn(og, wb_ref[:, hc:]) * mask_ref[0, 0:1, :]).astype(bf16)
    gro_ref[0] = gro
    q = dot_nt(og, wo_ref[:, :width]) + dot_nt(gro, wo_ref[:, width : width + 128])
    q = q * row_ref[1:2, :]
    q_ref[0] = q
    lane = lax.broadcasted_iota(jnp.int32, (BLOCK, 128), 1)
    s0 = jnp.sum(gated * gated, -1, keepdims=True)
    s1 = jnp.sum(q * gated, -1, keepdims=True)
    stat_ref[0, 0:8, :] = jnp.where(lane == 0, s0, s1).T[:8]
    low = (gated * row_ref[1:2, :]).astype(bf16)
    route(order_ref, b, dot_nn(low, wo_ref[:, :width]).astype(bf16), near_ref, pair_ref, far_ref)
    stat_ref[0, 8:, :] = fold(dot_nn(low, wo_ref[:, width : width + 128]) * mask_ref[0, 0:1, :], rank)

    if keep:

        @pl.when(b == pl.num_programs(0) - 1)
        def _():
            for copy in keeping():
                copy.wait()


def backward_kernel(
    order_ref, q_ref, g_ref, ssm_ref, vbc_ref, pre_ref, tok_ref, rm_ref, meta_ref, doc_ref, state_ref, next_ref,
    rank_ref, gro_ref, conv_ref, head_ref, row_ref, half_ref, select_ref, upg_ref, upc_ref, mask_ref,
    wa_ref, wb_ref,
    near_ref, pair_ref, far_ref, grads_ref, gri_ref,
    buf, carry,
    *, hn, hc, rank,
):
    pairs = hn // 2
    cc = hc + 256
    first = pl.program_id(0) == 0

    @pl.when(first)
    def _():
        carry[...] = jnp.zeros_like(carry)
        buf[BLOCK:, :] = jnp.zeros((8, cc), f32)
        grads_ref[...] = jnp.zeros_like(grads_ref)

    rm = jnp.concatenate([rm_ref[0]] * 16, 0).T
    inv = rm[:, 0:1]
    mean = rm[:, 1:2]
    meta = meta_ref[0]
    gate = g_ref[0]
    ssm = ssm_ref[0]
    q = q_ref[0]
    vbc = vbc_ref[0]
    values = vbc[:, :hc]
    values_f = values.astype(f32)
    in_state = vbc[:, hc : hc + 128]
    out_state = vbc[:, hc + 128 :]
    skip = row_ref[0:1, :]
    mixed = ssm + skip * values_f
    sg = sigmoid(gate)
    act = gate * sg
    gated = mixed * act
    gated_r = gated * inv
    grad_gated = inv * (q - gated_r * (inv * mean))
    gated_low = (gated_r * row_ref[1:2, :]).astype(bf16)
    grads_ref[0, :, hc + cc :] = grads_ref[0, :, hc + cc :] + by_rank(
        dot_tn(gro_ref[0], gated_low), rank
    )
    grad_mixed = grad_gated * act
    gp_gate = (grad_gated * mixed * (sg + act * (1.0 - sg))).astype(bf16)
    gsum = grad_mixed.astype(bf16)
    gsum_f = gsum.astype(f32)

    dt = tok_ref[0, :, 0:128]
    cum = tok_ref[0, :, 128:256]
    arg = tok_ref[0, :, 256:384]
    scaled_cum = cum * LOG2E
    down = scaled_cum - jnp.log(jnp.maximum(dt, 1e-37)) * LOG2E
    across = scaled_cum.T
    row = lax.broadcasted_iota(jnp.int32, (BLOCK, BLOCK), 0)
    col = lax.broadcasted_iota(jnp.int32, (BLOCK, BLOCK), 1)
    ok = (col >= row) & (meta[:, 5:6] == doc_ref[0, 0])
    bias = jnp.where(ok, 0.0, -1e30)
    contact = dot_nt(in_state, out_state)
    entry = jnp.exp(cum) * meta[:, 3:4]
    weight = jnp.exp(cum[BLOCK - 1 :, :] - cum) * dt * meta[:, 4:5]
    later = carry[...]
    later_low = later.astype(bf16)
    grad_scaled = dot_nt(in_state, later_low)
    weight_wide = spread_all(weight, pairs)
    entry_wide = spread_all(entry, pairs)
    scaled = (values_f * weight_wide).astype(bf16)
    weighted = (gsum_f * entry_wide).astype(bf16)
    half = BLOCK // 2
    g_con = [jnp.zeros((half, BLOCK), f32), jnp.zeros((half, half), f32)]
    g_val = []
    for j in range(pairs):
        at = slice(128 * j, 128 * j + 128)
        v = values[:, at]
        gs = gsum[:, at]
        tops = []
        for i, (r0, c0) in enumerate(((0, 0), (half, half))):
            ws = []
            for side in (0, 1):
                h = 2 * j + side
                gw = dot_nt(v[r0 : r0 + half] * half_ref[side : side + 1, :], gs[c0:])
                e = jnp.exp2(
                    (across[h : h + 1, c0:] - down[r0 : r0 + half, h : h + 1])
                    + bias[r0 : r0 + half, c0:]
                )
                ws.append((contact[r0 : r0 + half, c0:] * e).astype(bf16))
                g_con[i] = g_con[i] + gw * e
            gg = jnp.concatenate([gs[c0:] * half_ref[0:1, :], gs[c0:] * half_ref[1:2, :]], 0)
            tops.append(dot_nn(jnp.concatenate(ws, 1), gg))
        g_val.append(jnp.concatenate(tops, 0))
    g_val = jnp.concatenate(g_val, 1) + grad_scaled * weight_wide
    con_low = jnp.concatenate(
        [g_con[0], jnp.concatenate([jnp.zeros((half, half), f32), g_con[1]], 1)], 0
    ).astype(bf16)
    g_in = dot_nn(con_low, out_state) + dot_nn(scaled, later_low)
    g_out = dot_tn(con_low, in_state) + dot_nn(weighted, state_ref[0, 0])
    select = select_ref[...]
    spent = per_head(values_f * g_val, select)
    gained = per_head(gsum_f * ssm, select)
    ends = later * next_ref[0, 0].astype(f32)
    parts = [jnp.sum(ends[64 * h : 64 * h + 64], 0, keepdims=True) for h in range(hn)]
    parts.append(jnp.zeros((128 - hn, 128), f32))
    last = jnp.sum(jnp.concatenate(parts, 0).T, 0, keepdims=True)
    where_last = lax.broadcasted_iota(jnp.int32, (BLOCK, 128), 0) == BLOCK - 1
    grad_cum = gained - spent + jnp.where(where_last, last, 0.0)
    grad_log = dot_exact((col >= row).astype(f32), grad_cum)
    sig = sigmoid(arg)
    g_step = (
        spent * (sig / jnp.maximum(dt, 1e-37)) + head_ref[1:2, :] * grad_log * sig
    ).astype(bf16)
    passing = entry[BLOCK - 1 :, :]
    direct = dot_tn(weighted, out_state)
    for h in range(hn):
        at = slice(64 * h, 64 * h + 64)
        carry[at, :] = passing[:, h : h + 1] * later[at] + direct[at]

    pre = pre_ref[0]
    sp = sigmoid(pre)
    grad_out = jnp.concatenate([skip * grad_mixed + g_val, g_in, g_out], 1)
    grad_pre = grad_out * (sp + pre * sp * (1.0 - sp))
    buf[:BLOCK, :] = grad_pre
    total = conv_ref[3:4, :] * grad_pre
    for k in (1, 2, 3):
        total = total + conv_ref[3 - k : 4 - k, :] * (buf[k : k + BLOCK, :] * meta[:, 5 + k : 6 + k])
    buf[BLOCK:, :] = grad_pre[:8]
    gp_conv = total.astype(bf16)
    rows = rank_ref[0]
    grads_ref[0, :, :hc] = grads_ref[0, :, :hc] + by_rank(dot_tn(rows, gp_gate), rank)
    grads_ref[0, :, hc : hc + cc] = grads_ref[0, :, hc : hc + cc] + by_rank(
        dot_tn(rows, gp_conv), rank
    )
    gri_ref[0] = fold(
        (dot_nn(gp_gate, upg_ref[...]) + dot_nn(gp_conv, upc_ref[...])) * mask_ref[0, 0:1, :], rank
    )
    part = (
        dot_nt(gp_gate, wb_ref[:, :hc])
        + dot_nt(gp_conv, wa_ref[:, :cc])
        + dot_nt(g_step, wa_ref[:, cc + 128 :])
    ).astype(bf16)
    route(order_ref, pl.num_programs(0) - 1 - pl.program_id(0), part, near_ref, pair_ref, far_ref)


def pack_weights_kernel(
    ip_ref, sp_ref, idn_ref, iup_ref, odn_ref, oup_ref, op_ref, cw_ref, cb_ref, idx_ref, gg_ref, tail_ref,
    a_ref, b_ref, o_ref, small_ref,
    turn, misc,
    *, n, hn, hc, inner, planes,
):
    rows = ip_ref.shape[0]
    ranks = idn_ref.shape[0]
    up_rows = iup_ref.shape[1]

    def turned(ref):
        turn[...] = jnp.zeros_like(turn)
        turn[:, : ref.shape[1]] = ref[...].astype(f32)
        return turn[...].T

    down = turned(idn_ref)[:rows].astype(bf16)
    late = turned(oup_ref)[:rows].astype(bf16)
    step = jnp.concatenate([sp_ref[...].astype(f32), jnp.zeros((rows, 128 - n * hn), f32)], 1)
    lane = lax.broadcasted_iota(jnp.int32, (rows, 128), 1)
    chunk = hc // planes
    heads = hn // planes

    def columns(base, t, target, to):
        for p in range(0, planes, 2):
            got = []
            for q in (p, p + 1):
                start = base + (q * n + t) * chunk
                low = start // 128 * 128
                v = ip_ref[:, low : low + 256].astype(f32)
                got.append(pltpu.roll(v, 256 - (start - low), 1) if start > low else v)
            second = pltpu.roll(got[1], 64, 1)
            at = p * chunk
            target[to, at : at + 128] = got[0][:, :128].astype(bf16)
            target[to, at + 128 : at + 256] = jnp.where(
                lane < 64, got[0][:, 128:], second[:, :128]
            ).astype(bf16)
            target[to, at + 256 : at + 384] = second[:, 128:].astype(bf16)

    for t in range(n):
        to = slice(t * rows, (t + 1) * rows)
        columns(inner, t, a_ref, to)
        a_ref[to, hc : hc + 256] = ip_ref[:, 2 * inner :]
        a_ref[to, hc + 256 : hc + 256 + ranks] = down
        last = tail_ref[...]
        for p in range(planes):
            shift = (p * heads - (p * n + t) * heads) % 128
            mine = pltpu.roll(step, shift, 1) if shift else step
            last = jnp.where((lane >= p * heads) & (lane < (p + 1) * heads), mine, last)
        a_ref[to, hc + 256 + ranks :] = last.astype(bf16)
        columns(0, t, b_ref, to)
        b_ref[to, hc:] = late
    out_rows, width = op_ref.shape
    part = o_ref.shape[1]
    o_ref[:out_rows, :] = op_ref[:, :part]
    o_ref[out_rows:, : width - part] = op_ref[:, part:]
    o_ref[out_rows:, width - part : width - part + ranks] = turned(odn_ref)[:out_rows].astype(bf16)
    o_ref[out_rows:, width - part + ranks :] = jnp.zeros(
        (out_rows, 2 * part - width - ranks), bf16
    )
    keep = -(-up_rows // 16) * 16
    small_ref[:keep, :] = turned(iup_ref)[:keep].astype(bf16)
    turn[...] = jnp.zeros_like(turn)
    turn[: cw_ref.shape[0], : cw_ref.shape[1]] = cw_ref[...].astype(f32)
    misc[...] = jnp.zeros_like(misc)
    misc[0:8, :] = turn[:, 0:128].T[0:8]
    misc[4:5, : cb_ref.shape[1]] = cb_ref[...].astype(f32)
    misc[5:6, : idx_ref.shape[1]] = idx_ref[...].astype(f32)
    misc[6:7, : gg_ref.shape[1]] = gg_ref[...].astype(f32)
    small_ref[keep:, :] = misc[...].astype(bf16)


def pack_grads_kernel(
    order_ref, g0, g1, g2, g3, down_ref, out_ref, up, middle, total, *, n, hc, inner, width, widths, starts,
    planes,
):
    chunk = hc // planes
    lane = lax.broadcasted_iota(jnp.int32, (out_ref.shape[1], 128), 1)

    def place(g, source, target, base, t):
        for p in range(planes):
            low = (source + p * chunk) // 128 * 128
            v = g[:, low : low + 256].astype(f32)
            off = source + p * chunk - low
            v = pltpu.roll(v, 256 - off, 1) if off else v
            to = base + (p * n + t) * chunk
            if to % 128 == 0:
                target[:, to : to + chunk] = v[:, :chunk]
            else:
                v = pltpu.roll(v, 64, 1)
                here = slice(to - 64, to + 64)
                target[:, here] = jnp.where(lane < 64, target[:, here], v[:, :128])
                target[:, to + 64 : to + 192] = v[:, 128:]

    for t in range(n):
        for i, g in enumerate((g0, g1, g2, g3)):

            @pl.when(order_ref[t] == i)
            def _(t=t, g=g):
                place(g, 0, up, 0, t)
                place(g, hc, up, inner, t)
                place(g, 2 * hc + 256, middle, 0, t)

    def summed(at):
        first = g0[:, at].astype(f32) + g1[:, at].astype(f32)
        return first + (g2[:, at].astype(f32) + g3[:, at].astype(f32))

    up[:, 2 * inner : 2 * inner + 256] = summed(slice(2 * hc, 2 * hc + 256))
    total[:, :width] = summed(slice(3 * hc + 256, 3 * hc + 256 + width))
    sources = (None, up, middle, total)
    for t in range(n):

        @pl.when(order_ref[0] == t)
        def _(t=t):
            for d in range(out_ref.shape[0]):
                for ref, at, w in zip(sources, starts, widths):
                    start = (d * n + t) * w
                    low = start // 128 * 128
                    span = -(-w // 128) * 128
                    if ref is None:
                        window = down_ref[:, low : low + span + 128].astype(f32)
                    else:
                        window = ref[:, low : low + span + 128]
                    if start > low:
                        window = pltpu.roll(window, span + 128 - (start - low), 1)
                    out_ref[d, :, at : at + span] = window[:, :span].astype(bf16)


def swap(v, axis, bit):
    size = lax.axis_size(axis)
    return lax.ppermute(v, axis, [(i, i ^ bit) for i in range(size)])


def put(pieces):
    rows = pieces[0][0].shape[0]
    out = jnp.zeros((len(pieces) * rows, pieces[0][0].shape[1]), pieces[0][0].dtype)
    for piece, slot in pieces:
        out = lax.dynamic_update_slice_in_dim(out, piece, slot * rows, 0)
    return out


def rotate(v, r):
    size = lax.axis_size("dp")
    return lax.ppermute(v, "dp", [(i, (i + 2 * r) % size) for i in range(size)])


def after(v, *others):
    return lax.optimization_barrier((v, others))[0]


def fence(*values):
    return lax.optimization_barrier(values)


def others(v):
    return [swap(v, "seq", k) for k in (1, 2, 3)]


def total_of(v, got):
    return (v + got[0]) + (got[1] + got[2])


def across(far, pair):
    return (far.astype(f32) + pair[BLOCK:].astype(f32)).astype(bf16)


def own_sum(near, pair, far):
    return near.astype(f32) + pair[:BLOCK].astype(f32) + far.astype(f32)


def scatter_plain(near, pair, far):
    v = jnp.concatenate([near, pair[:BLOCK], far, pair[BLOCK:]], 0).astype(f32)
    return lax.psum_scatter(v, "seq", scatter_dimension=0, tiled=True)


def per_device(
    layer_input,
    document_index,
    adapter_index,
    input_norm_gain,
    input_projection,
    step_projection,
    convolution_weight,
    convolution_bias,
    head_step_bias,
    log_decay_rate,
    head_skip_gain,
    gated_norm_gain,
    output_projection,
    adapter_input_down,
    adapter_input_up,
    adapter_output_down,
    adapter_output_up,
    output_gradient,
):
    both = ("dp", "seq")
    dps, n = lax.axis_size("dp"), lax.axis_size("seq")
    here = lax.axis_index("seq")
    seqs, own_len, width = layer_input.shape
    adapters, rank, _ = adapter_input_down.shape
    ranks = adapters * rank
    heads = head_step_bias.shape[0]
    inner = output_projection.shape[0] * dps * n
    cols = input_projection.shape[1]
    state2 = cols - 2 * inner
    state = state2 // 2
    taps = convolution_weight.shape[1]
    hn = heads // n
    hc = inner // n
    hd = inner // heads
    length = own_len * n
    nb = length // BLOCK

    staged = n == 4 and dps == 8
    rows = input_projection.shape[0]
    conv_cols = hc + state2
    wa_cols = conv_cols + ranks + 128
    doc_cols = -(-seqs * own_len // rows)
    doc_block = document_index.astype(bf16).reshape(-1)
    doc_block = jnp.pad(doc_block, (0, rows * doc_cols - doc_block.shape[0])).reshape(rows, -1)
    tail = jnp.concatenate([doc_block, input_norm_gain[:, None]], 1)
    up_rows = adapter_input_up.shape[2]
    up_keep = -(-up_rows // 16) * 16
    conv_rows = convolution_weight.shape[0]
    wide = -(-conv_rows // 128) * 128
    misc_rows = 16
    small_rows = up_keep + misc_rows * wide // 128
    out_rows = output_projection.shape[0]
    planes = dps // 2 if staged else 1
    if staged:
        to_head = [
            (8 * z + 2 * t + y, 8 * z + 4 * y + t)
            for z in range(planes) for y in range(2) for t in range(n)
        ]
    else:
        to_head = [(dps * s + d, n * d + s) for d in range(dps) for s in range(n)]
    tables = [
        v.reshape(ranks, -1)
        for v in (adapter_input_down, adapter_input_up, adapter_output_down, adapter_output_up)
    ]
    if staged:
        tail = jnp.pad(tail.astype(f32), ((0, 0), (127 - doc_cols, 0)))
        payload, late_payload, w_o, small = pl.pallas_call(
            functools.partial(
                pack_weights_kernel, n=n, hn=hn, hc=hc, inner=inner, planes=planes
            ),
            out_shape=[
                jax.ShapeDtypeStruct((n * rows, wa_cols), bf16),
                jax.ShapeDtypeStruct((n * rows, hc + ranks), bf16),
                jax.ShapeDtypeStruct((2 * out_rows, hc + ranks), bf16),
                jax.ShapeDtypeStruct((small_rows, 128), bf16),
            ],
            scratch_shapes=[pltpu.VMEM((128, 256), f32), pltpu.VMEM((misc_rows, 128), f32)],
            name="pack_weights",
        )(
            input_projection, step_projection, *tables[:2], *tables[2:], output_projection,
            convolution_weight, convolution_bias[None], adapter_index[None], gated_norm_gain[None], tail,
        )
    else:
        gap = jnp.zeros((rows, 127 - hn - doc_cols), bf16)
        payload = jnp.concatenate(
            [
                jnp.concatenate(
                    [
                        input_projection[:, inner + t * hc : inner + (t + 1) * hc],
                        input_projection[:, 2 * inner :],
                        tables[0].T,
                        step_projection[:, t * hn : (t + 1) * hn],
                        gap,
                        tail,
                    ],
                    1,
                )
                for t in range(n)
            ],
            0,
        )
        late_payload = jnp.concatenate(
            [
                jnp.concatenate([input_projection[:, t * hc : (t + 1) * hc], tables[3].T], 1)
                for t in range(n)
            ],
            0,
        )
        w_o = jnp.concatenate([output_projection, tables[2].T], 1)

        def as_row(v):
            return jnp.pad(v, ((0, 0), (0, wide - v.shape[1])))

        misc = jnp.concatenate(
            [
                as_row(convolution_weight.T),
                as_row(convolution_bias[None]),
                as_row(adapter_index.astype(bf16)[None]),
                as_row(gated_norm_gain[None]),
            ],
            0,
        )
        misc = jnp.pad(misc, ((0, misc_rows - misc.shape[0]), (0, 0)))
        small = jnp.concatenate(
            [jnp.pad(tables[1].T, ((0, up_keep - up_rows), (0, 0))), misc.reshape(-1, 128)], 0
        )
    w_a = lax.all_to_all(payload, "seq", 0, 0, tiled=True)

    if staged:
        d = lax.axis_index("dp")
        y, z = d % 2, d // 2
        w_o = lax.ppermute(w_o, both, to_head)
        small_y = swap(small, "dp", 1)
        pair = put([(small, y), (small_y, 1 - y)])
        four = put([(pair, z % 2), (swap(pair, "dp", 2), 1 - z % 2)])
        x_near = swap(layer_input, "seq", 1)
        w_a, late_payload, four, x_near, w_o = fence(w_a, late_payload, four, x_near, w_o)
        a1, a3, a0y = rotate(w_a, 1), rotate(w_a, 3), swap(w_a, "dp", 1)
        small = put([(four, z // 2), (swap(four, "dp", 4), 1 - z // 2)])
        w_b = lax.all_to_all(late_payload, "seq", 0, 0, tiled=True)
        small_far = swap(small, "seq", 2)
        a1, a3, a0y, w_a, w_b, small, small_far, x0, x1, og0, og1 = fence(
            a1, a3, a0y, w_a, w_b, small, small_far, layer_input[:1], layer_input[1:],
            output_gradient[:1], output_gradient[1:],
        )
        a13y = swap(jnp.concatenate([a1, a3]), "dp", 1)
        a2 = rotate(w_a, 2)
        x_far0 = swap(x0, "seq", 2)
        beside = swap(jnp.concatenate([small, small_far]), "seq", 1)
        w_bo = jnp.concatenate([w_b, w_o])
        half_rows = small.shape[0]
        small = put(
            [
                (small, here), (beside[:half_rows], here ^ 1), (small_far, here ^ 2),
                (beside[half_rows:], here ^ 3),
            ]
        )
        at = [2 * lax.rem(z + 4 - r, 4) + y for r in range(4)]
        slots = [at[0], at[0] ^ 1, at[1], at[3], at[1] ^ 1, at[3] ^ 1, at[2], at[2] ^ 1]
        slots = jnp.stack(slots).astype(jnp.int32)
        x_order = jnp.arange(4, dtype=jnp.int32) ^ here
    else:
        w_b = lax.all_to_all(late_payload, "seq", 0, 0, tiled=True)
        w_o = lax.ppermute(w_o, both, to_head)
        small = lax.all_gather(lax.all_gather(small, "dp", tiled=True), "seq", tiled=True)
        wa_pieces = [lax.all_gather(w_a, "dp", tiled=True)]
        slots = jnp.zeros((1,), jnp.int32)
        x_order = jnp.arange(nb, dtype=jnp.int32)
        xs = [jnp.split(lax.all_gather(layer_input, "seq", axis=1, tiled=True), nb, axis=1)] * seqs
    docs = w_a[:, wa_cols - 1 - doc_cols : wa_cols - 1].reshape(n, -1)[:, : seqs * own_len]
    docs = jnp.moveaxis(docs.reshape(n, seqs, own_len), 0, 1).reshape(seqs, length)
    order = jnp.concatenate([x_order, slots])
    order_whole = jnp.concatenate([x_order, jnp.zeros((1,), jnp.int32)])

    small = small.reshape(n, dps, small_rows, 128)
    small = jnp.moveaxis(small, 0, 1).reshape(dps * n, small_rows, 128)
    up_full = small[:, :up_rows].reshape(cols, ranks)
    misc = small[:, up_keep:].reshape(dps * n, misc_rows, wide)
    conv_w = jnp.moveaxis(misc[:, :taps, :conv_rows], 1, 0).reshape(taps, -1).astype(f32)
    conv_b = misc[:, taps, :conv_rows].reshape(-1).astype(f32)
    every_index = misc[:, taps + 1, :seqs].reshape(dps, n, seqs)[:, 0].astype(jnp.int32)
    gate_gain = misc[:, taps + 2, :out_rows].reshape(-1).astype(f32)

    def mine(v):
        v = v.reshape(planes, n, v.shape[0] // (planes * n), *v.shape[1:])
        v = lax.dynamic_index_in_dim(v, here, 1, keepdims=False)
        return v.reshape(-1, *v.shape[2:])

    up_gate = mine(up_full[:inner])
    up_conv = jnp.concatenate([mine(up_full[inner : 2 * inner]), up_full[2 * inner :]], 0)
    conv_w = jnp.concatenate([mine(conv_w.T[:inner]), conv_w.T[inner:]], 0).T
    conv_b = jnp.concatenate([mine(conv_b[:inner]), conv_b[inner:]], 0)
    step_bias = mine(head_step_bias)
    decay_rate = -jnp.exp(mine(log_decay_rate))
    skip = mine(head_skip_gain)
    gate_gain = mine(gate_gain)

    chosen = (adapter_index[:, None] == jnp.arange(adapters, dtype=jnp.int32)[None, :]).astype(f32)
    mask = jnp.repeat(chosen, rank, axis=1)[:, None, :]

    doc_f = docs.astype(f32)

    def same_before(k):
        return jnp.pad(doc_f, ((0, 0), (k, 0)), constant_values=-1.0)[:, :length] == doc_f

    def same_after(k):
        return jnp.pad(doc_f, ((0, 0), (0, k)), constant_values=-1.0)[:, k:] == doc_f

    blocks = doc_f.reshape(seqs, nb, BLOCK)
    prior = jnp.concatenate([blocks[:, :1, 0], blocks[:, :-1, -1]], 1)
    keep = (blocks == prior[:, :, None]).reshape(seqs, length)
    ends = (blocks == blocks[:, :, -1:]).reshape(seqs, length)
    flags = [
        same_before(1), same_before(2), same_before(3), keep, ends, doc_f,
        same_after(1), same_after(2), same_after(3),
    ]
    meta = jnp.stack([v.astype(f32) for v in flags], -1)
    meta = jnp.pad(meta, ((0, 0), (0, 0), (0, 128 - len(flags))))
    doc_rows = blocks[:, :, None, :]

    def rows8(*vs):
        return jnp.pad(jnp.stack(vs), ((0, 8 - len(vs)), (0, 0)))

    conv_rows8 = rows8(conv_w[0], conv_w[1], conv_w[2], conv_w[3], conv_b)
    head_rows = rows8(
        jnp.pad(step_bias, (0, 128 - hn)), jnp.pad(decay_rate, (0, 128 - hn))
    )
    wide_rows = rows8(jnp.repeat(skip, hd), gate_gain)
    halves = jnp.pad(
        (jnp.arange(128)[None, :] // 64 == jnp.arange(2)[:, None]).astype(bf16), ((0, 14), (0, 0))
    )
    select = (jnp.arange(hc)[:, None] // hd == jnp.arange(128)[None, :]).astype(bf16)
    mask8 = jnp.broadcast_to(mask, (seqs, 8, ranks))
    cc = conv_cols
    anywhere = pl.BlockSpec(memory_space=pl.ANY)
    params = pltpu.CompilerParams(
        dimension_semantics=("arbitrary",), vmem_limit_bytes=VMEM_BYTES
    )

    def at(w, k=0):
        return pl.BlockSpec((1, BLOCK, w), lambda b, o: (k, b, 0))

    def once(v, *block):
        block = block or v.shape
        return pl.BlockSpec(block, lambda b, o: (0,) * len(block), pipeline_mode=pl.Buffered(1))

    def of_seq(v, s0):
        k = s0 if v.shape[0] > 1 else 0
        return pl.BlockSpec(
            (1,) + v.shape[1:], lambda b, o: (k, 0, 0), pipeline_mode=pl.Buffered(1)
        )

    def one(w, dtype):
        return jax.ShapeDtypeStruct((1, length, w), dtype)

    def cost(flops, mib):
        return pl.CostEstimate(flops=int(flops), bytes_accessed=mib << 20, transcendentals=0)

    def parts_specs():
        return [once(None, BLOCK, width), once(None, 2 * BLOCK, width), once(None, BLOCK, width)]

    parts_shapes = [
        jax.ShapeDtypeStruct((k * BLOCK, width), bf16) for k in (1, 2, 1)
    ]

    def forward(s0, order, blocks, pieces, keep):
        whole_w = jax.ShapeDtypeStruct((width, wa_cols), bf16)
        size = n * rows if len(pieces) > 1 else width
        total = sum(v.shape[0] for v in pieces) // size
        return pl.pallas_call(
            functools.partial(
                forward_kernel, hn=hn, hc=hc, count=len(pieces), size=size, keep=keep
            ),
            grid_spec=pltpu.PrefetchScalarGridSpec(
                num_scalar_prefetch=1,
                grid=(nb,),
                in_specs=[
                    *(of_seq(v, s0) for v in blocks), at(128, s0),
                    pl.BlockSpec((1, 1, 1, BLOCK), lambda b, o: (s0, b, 0, 0)),
                    once(up_conv), once(conv_rows8), once(head_rows), of_seq(mask8, s0), once(halves),
                    *([anywhere] * len(pieces)),
                ],
                out_specs=[
                    at(width), at(128), at(cc), at(cc), at(hc),
                    pl.BlockSpec((1, 1, hc, state), lambda b, o: (0, b, 0, 0)), at(384),
                    *([anywhere] if keep else []),
                ],
                scratch_shapes=[
                    pltpu.VMEM((BLOCK + 8, cc), f32), pltpu.VMEM((hc, state), f32),
                    pltpu.VMEM((BLOCK, width), bf16), pltpu.VMEM((width, wa_cols), bf16),
                    pltpu.VMEM((8, width), f32), pltpu.SemaphoreType.DMA((total,)),
                    pltpu.SemaphoreType.DMA,
                ],
            ),
            out_shape=[
                one(width, bf16), one(128, bf16), one(cc, bf16), one(cc, f32), one(hc, f32),
                jax.ShapeDtypeStruct((1, nb, hc, state), bf16), one(384, f32),
                *([whole_w] if keep else []),
            ],
            compiler_params=params,
            name="ssm_forward",
            cost_estimate=cost(2 * length * (width * wa_cols + 3 * BLOCK * hc), 20),
        )(order, *blocks, meta, doc_rows, up_conv, conv_rows8, head_rows, mask8, halves, *pieces)

    def middle(s0, order, scanned, blocks, gate_pieces, out_pieces, keep):
        normed, rank_in, vbc, _, ssm = scanned[:5]
        count = len(gate_pieces)
        merged = () if out_pieces else (n * rows, out_rows)
        wb_shape, wo_shape = (width, hc + ranks), (hc, width + ranks)
        return pl.pallas_call(
            functools.partial(
                middle_kernel, hc=hc, width=width, rank=rank, count=count, keep=keep,
                merged=merged,
            ),
            grid_spec=pltpu.PrefetchScalarGridSpec(
                num_scalar_prefetch=1,
                grid=(nb,),
                in_specs=[
                    at(width), at(128), at(cc), at(hc), *(of_seq(v, s0) for v in blocks),
                    once(up_gate), once(wide_rows), of_seq(mask8, s0), *([anywhere] * (count + len(out_pieces))),
                ],
                out_specs=[
                    at(hc), at(hc), at(128), *parts_specs(),
                    pl.BlockSpec((1, 8 + rank, BLOCK), lambda b, o: (0, 0, b)),
                    *([anywhere] * 2 if keep else []),
                ],
                scratch_shapes=[
                    pltpu.VMEM((BLOCK, width), bf16), pltpu.VMEM(wb_shape, bf16),
                    pltpu.VMEM(wo_shape, bf16), pltpu.SemaphoreType.DMA((3 * dps,)),
                    pltpu.SemaphoreType.DMA((count,)), pltpu.SemaphoreType.DMA((2,)),
                ],
            ),
            out_shape=[
                one(hc, f32), one(hc, f32), one(128, bf16), *parts_shapes,
                jax.ShapeDtypeStruct((1, 8 + rank, length), f32),
                *([jax.ShapeDtypeStruct(v, bf16) for v in (wb_shape, wo_shape)] if keep else []),
            ],
            compiler_params=params,
            name="output_side",
            cost_estimate=cost(2 * length * width * hc * 3, 25),
        )(
            order, normed, rank_in, vbc, ssm, *blocks, up_gate, wide_rows, mask8, *gate_pieces,
            *out_pieces,
        )

    def backward(s0, scanned, gate, q, rm, grad_rank_out):
        _, rank_in, vbc, pre, ssm, states_low, tok = scanned[:7]

        def back(w, k=0):
            return pl.BlockSpec((1, BLOCK, w), lambda b, o: (k, nb - 1 - b, 0))

        def back_state(shift):
            return pl.BlockSpec(
                (1, 1, hc, state), lambda b, o: (0, jnp.minimum(nb - 1 - b + shift, nb - 1), 0, 0)
            )

        return pl.pallas_call(
            functools.partial(backward_kernel, hn=hn, hc=hc, rank=rank),
            grid_spec=pltpu.PrefetchScalarGridSpec(
                num_scalar_prefetch=1,
                grid=(nb,),
                in_specs=[
                    back(hc), back(hc), back(hc), back(cc), back(cc), back(384),
                    pl.BlockSpec((1, 8, BLOCK), lambda b, o: (0, 0, nb - 1 - b)), back(128, s0),
                    pl.BlockSpec((1, 1, 1, BLOCK), lambda b, o: (s0, nb - 1 - b, 0, 0)),
                    back_state(0), back_state(1), back(128), back(128), once(conv_rows8),
                    once(head_rows), once(wide_rows), once(halves), once(select), once(up_gate),
                    once(up_conv), of_seq(mask8, s0), once(wa), once(wb),
                ],
                out_specs=[
                    *parts_specs(), once(None, 1, rank, 2 * hc + cc),
                    pl.BlockSpec((1, rank, BLOCK), lambda b, o: (0, 0, nb - 1 - b)),
                ],
                scratch_shapes=[
                    pltpu.VMEM((BLOCK + 8, cc), f32), pltpu.VMEM((hc, state), f32),
                ],
            ),
            out_shape=[
                *parts_shapes, jax.ShapeDtypeStruct((1, rank, 2 * hc + cc), f32),
                jax.ShapeDtypeStruct((1, rank, length), f32),
            ],
            compiler_params=params,
            name="ssm_backward",
            cost_estimate=cost(2 * length * (8 * BLOCK * hc + width * (hc + cc)), 30),
        )(
            x_order, q, gate, ssm, vbc, pre, tok, rm, meta, doc_rows, states_low, states_low, rank_in,
            grad_rank_out, conv_rows8, head_rows, wide_rows, halves, select, up_gate, up_conv, mask8,
            wa, wb,
        )

    def own_tokens(v, axis):
        return lax.dynamic_slice_in_dim(v, here * own_len, own_len, axis)

    def with_adapter(rows_of, table, s0):
        wide_rows_of = jnp.tile(rows_of, (adapters, 1)) * mask[s0, 0][:, None].astype(bf16)
        return mm("rt,dr->td", wide_rows_of, table)

    if staged:
        ready = (
            order, up_conv, up_gate, conv_rows8, head_rows, meta, doc_rows, mask8, halves, select,
            wide_rows, w_bo, order_whole, every_index,
        )
        a2, a13y, x_far0, x1, ready = fence(a2, a13y, x_far0, x1, ready)
        (
            order, up_conv, up_gate, conv_rows8, head_rows, meta, doc_rows, mask8, halves, select,
            wide_rows, w_bo, order_whole, every_index,
        ) = ready
        a2y = swap(a2, "dp", 1)
        x_both0 = swap(x_far0, "seq", 1)
        b1, b3 = rotate(w_bo, 1), rotate(w_bo, 3)
        x_far1 = swap(x1, "seq", 2)
        wa_pieces = [w_a, a0y, a1, a3, a13y, a2, a2y]
        xs = [[layer_input, x_near, x_far0, x_both0]]
        wa_pieces, xs[0], w_bo = fence(wa_pieces, xs[0], w_bo)
        *fwd0, wa = forward(0, order, xs[0], wa_pieces, True)
        b0y = swap(w_bo, "dp", 1)
        fwd0, wa, b1, b3, b0y, w_bo, x_far1 = fence(fwd0, wa, b1, b3, b0y, w_bo, x_far1)
        x_both1 = swap(x_far1, "seq", 1)
        x_both1, w_bo, og0, og1, og = fence(x_both1, w_bo, og0, og1, output_gradient)
        fwd1 = forward(1, order_whole, [layer_input, x_near, x_far1, x_both1], [wa], False)
        b1y, b3y = swap(b1, "dp", 1), swap(b3, "dp", 1)
        b2 = rotate(w_bo, 2)
        og_far0 = swap(og0, "seq", 2)
        og_near = swap(og, "seq", 1)
        fwd1, b1y, b3y, b2, og_far0, og_near, w_bo, og1 = fence(
            fwd1, b1y, b3y, b2, og_far0, og_near, w_bo, og1
        )
        b2y = swap(b2, "dp", 1)
        og_both0 = swap(og_far0, "seq", 1)
        fwd = [fwd0, fwd1]
        wb_pieces = [w_bo, b0y, b1, b3, b1y, b3y, b2, b2y]
        wo_pieces = []
        ogs = [[output_gradient, og_near, og_far0, og_both0]]
        wb_pieces, ogs[0], og1 = fence(wb_pieces, ogs[0], og1)
    else:
        fwd = [forward(0, order, xs[0], wa_pieces, True)]
        wa = fwd[0][-1]
        fwd += [forward(s0, order_whole, xs[s0], [wa], False) for s0 in range(1, seqs)]
        wb_pieces = [lax.all_gather(w_b, "dp", tiled=True)]
        wo_pieces = [lax.all_gather(w_o, "dp", tiled=True)]
        full = lax.all_gather(output_gradient, "seq", axis=1, tiled=True)
        ogs = [jnp.split(full, nb, axis=1)] * seqs
    gain = wa[:, -1].astype(f32)

    def normalisers(stats):
        inv_gated = lax.rsqrt(stats[:1] / inner + EPS)
        rm = jnp.pad(jnp.concatenate([inv_gated, stats[1:2] / inner], 0), ((0, 6), (0, 0)))[None]
        return inv_gated, rm, own_tokens((stats[8:] * inv_gated).astype(bf16), 1)

    def layer_output(s0, branch, inv_gated, rank_out):
        return (
            layer_input[s0].astype(f32)
            + branch * own_tokens(inv_gated, 1).T
            + with_adapter(rank_out, up_out, s0)
        ).astype(bf16)

    def down_gradient(s0, grad_rank_in):
        return mm("rt,td->rd", grad_rank_in, fwd[s0][0][0]).astype(bf16)

    def layer_gradient(s0, partial, grad_rank_in):
        grad_normed = partial + with_adapter(
            own_tokens(grad_rank_in, 1), down_in, s0
        )
        own = layer_input[s0].astype(f32)
        inv_own = lax.rsqrt(jnp.mean(own * own, -1, keepdims=True) + EPS)
        scaled_in = grad_normed * gain
        return (
            inv_own * scaled_in
            - own * inv_own**3 * jnp.mean(scaled_in * own, -1, keepdims=True)
            + output_gradient[s0].astype(f32)
        )

    *side0, wb, wo = middle(0, order, fwd[0], ogs[0], wb_pieces, wo_pieces, True)
    up_out = wb[:, hc:]
    down_in = wa[:, cc : cc + ranks]
    if staged:
        og_far1 = swap(og1, "seq", 2)
        side0, wb, wo, og_far1 = fence(side0, wb, wo, og_far1)
        ogs.append([output_gradient, og_near, og_far1, swap(og_far1, "seq", 1)])
        ogs[1], side0, wb, wo, up_out, down_in, gain = fence(
            ogs[1], side0, wb, wo, up_out, down_in, gain
        )
        gate0, q0, gro0, near0, pair0, far0, stats0 = side0
        side1 = middle(1, order_whole, fwd[1], ogs[1], [wb], [wo], False)
        got = others(stats0[0])
        pair0 = swap(pair0, "seq", 1)
        side1, got, pair0, far0 = fence(side1, got, pair0, far0)
        gate1, q1, gro1, near1, pair1, far1, stats1 = side1
        inv0, rm0, rank_out0 = normalisers(total_of(stats0[0], got))
        rm0, away, stats1, pair1 = fence(rm0, across(far0, pair0), stats1, pair1)

        back0 = backward(0, fwd[0], gate0, q0, rm0, gro0)
        away = swap(away, "seq", 2)
        got = others(stats1[0])
        pair1 = swap(pair1, "seq", 1)
        back0, away, got, pair1, far1 = fence(back0, away, got, pair1, far1)
        near_g0, pair_g0, far_g0, compact0, gri0 = back0
        pair_g0 = swap(pair_g0, "seq", 1)
        away0 = away
        inv1, rm1, rank_out1 = normalisers(total_of(stats1[0], got))
        rm1, away, gri0, away_g, away0, rank_out0, rank_out1 = fence(
            rm1, across(far1, pair1), gri0, across(far_g0, pair_g0), away0, rank_out0, rank_out1
        )

        back1 = backward(1, fwd[1], gate1, q1, rm1, gro1)
        away = swap(away, "seq", 2)
        away_g = swap(away_g, "seq", 2)
        got = others(gri0[0])
        back1, away, away_g, got, away0, rank_out0, rank_out1, near0, pair0, inv0 = fence(
            back1, away, away_g, got, away0, rank_out0, rank_out1, near0, pair0, inv0
        )
        near_g1, pair_g1, far_g1, compact1, gri1 = back1
        pair_g1 = swap(pair_g1, "seq", 1)
        got1 = others(gri1[0])
        g_out_up = mm("srt,std->srd", jnp.stack([rank_out0, rank_out1]), output_gradient)
        split = jnp.concatenate(
            [
                jnp.concatenate([compact0[0], compact1[0]]).astype(bf16),
                g_out_up.astype(bf16).reshape(seqs * rank, width),
            ],
            1,
        )
        away_g1, split, got1 = fence(across(far_g1, pair_g1), split, got1)
        away_g1 = swap(away_g1, "seq", 2)
        split_far = swap(split, "seq", 2)
        split_near = swap(split, "seq", 1)
        split_both = swap(split_far, "seq", 1)
        gri0 = total_of(gri0[0], got).astype(bf16)
        gri1 = total_of(gri1[0], got1).astype(bf16)
        downs = jnp.concatenate([down_gradient(0, gri0), down_gradient(1, gri1)])
        output0 = layer_output(0, own_sum(near0, pair0, away0), inv0, rank_out0)
        output1 = layer_output(1, own_sum(near1, pair1, away), inv1, rank_out1)
        grad0 = layer_gradient(0, own_sum(near_g0, pair_g0, away_g), gri0)
        grads_of_seq = [split, split_near, split_far, split_both]
        grads_order = x_order
    else:
        splits, downs, ranks_out, outputs, grads_in = [], [], [], [], []
        for s0 in range(seqs):
            if s0:
                side0 = middle(s0, order_whole, fwd[s0], ogs[s0], [wb], [wo], False)
            gate, q, gro, *parts, stats = side0
            inv_gated, rm, rank_out = normalisers(lax.psum(stats[0], "seq"))
            outputs.append(layer_output(s0, scatter_plain(*parts), inv_gated, rank_out))
            *parts, compacted, gri = backward(s0, fwd[s0], gate, q, rm, gro)
            gri = lax.psum(gri[0], "seq").astype(bf16)
            splits.append(compacted[0].astype(bf16))
            downs.append(down_gradient(s0, gri))
            ranks_out.append(rank_out)
            grads_in.append(layer_gradient(s0, scatter_plain(*parts), gri))
        g_out_up = mm("srt,std->srd", jnp.stack(ranks_out), output_gradient).astype(bf16)
        output = jnp.stack(outputs)
        grad_in = jnp.stack(grads_in)
        downs = jnp.concatenate(downs)
        split = jnp.concatenate(
            [jnp.concatenate(splits), g_out_up.reshape(seqs * rank, width)], 1
        )
        grads_of_seq = jnp.split(lax.all_gather(split, "seq", axis=0, tiled=True), n)

    widths = [v // (dps * n) for v in (width, cols, inner, width)]
    starts, lanes = [], 0
    for v in widths:
        starts.append(lanes)
        lanes += -(-v // 128) * 128
    pack_rows = seqs * rank
    if staged:
        packed = pl.pallas_call(
            functools.partial(
                pack_grads_kernel, n=n, hc=hc, inner=inner, width=width, widths=widths,
                starts=starts, planes=planes,
            ),
            in_specs=[
                pl.BlockSpec(memory_space=pltpu.SMEM),
                *[pl.BlockSpec(memory_space=pltpu.VMEM)] * 5,
            ],
            out_specs=pl.BlockSpec(memory_space=pltpu.VMEM),
            out_shape=jax.ShapeDtypeStruct((dps, pack_rows, lanes), bf16),
            scratch_shapes=[
                pltpu.VMEM((pack_rows, cols + 256), f32), pltpu.VMEM((pack_rows, inner + 256), f32),
                pltpu.VMEM((pack_rows, width + 256), f32),
            ],
            name="pack_grads",
        )(
            grads_order,
            *grads_of_seq, jnp.pad(downs, ((0, 0), (0, 256))),
        )
    else:
        pieces = jnp.stack(grads_of_seq)

        def by_heads(start):
            return jnp.concatenate([pieces[t, :, start : start + hc] for t in range(n)], -1)

        def summed(start, size):
            return pieces[..., start : start + size].astype(f32).sum(0).astype(bf16)

        full = [
            downs,
            jnp.concatenate([by_heads(0), by_heads(hc), summed(2 * hc, state2)], -1),
            by_heads(2 * hc + state2),
            summed(3 * hc + state2, width),
        ]
        packed = jnp.zeros((dps, pack_rows, lanes), bf16)
        for v, start, w in zip(full, starts, widths):
            v = lax.dynamic_index_in_dim(
                v.reshape(pack_rows, dps, n, w), here, 2, keepdims=False
            )
            packed = packed.at[:, :, start : start + w].set(v.transpose(1, 0, 2))
    got = lax.all_to_all(packed, "dp", 0, 0, tiled=True)
    if staged:
        grad1 = layer_gradient(1, own_sum(near_g1, pair_g1, away_g1), gri1)
        output = jnp.stack([output0, output1])
        grad_in = jnp.stack([grad0, grad1])
    all_chosen = (every_index[..., None] == jnp.arange(adapters)).astype(bf16)
    table = mm("dsk,dsrc->krc", all_chosen, got.reshape(dps, seqs, rank, lanes))
    grads = [table[..., start : start + w] for start, w in zip(starts, widths)]
    return (output, grad_in, grads[0], grads[1], grads[2], grads[3])


def solution(mesh):
    return jax.shard_map(
        per_device,
        mesh=mesh,
        in_specs=(
            P("dp", "seq", None),
            P("dp", "seq"),
            P("dp"),
            P(("dp", "seq")),
            P(("dp", "seq"), None),
            P(("dp", "seq"), None),
            P(("dp", "seq"), None),
            P(("dp", "seq")),
            P(),
            P(),
            P(),
            P(("dp", "seq")),
            P(("dp", "seq"), None),
            P(None, None, ("dp", "seq")),
            P(None, None, ("dp", "seq")),
            P(None, None, ("dp", "seq")),
            P(None, None, ("dp", "seq")),
            P("dp", "seq", None),
        ),
        out_specs=(
            P("dp", "seq", None),
            P("dp", "seq", None),
            P(None, None, ("dp", "seq")),
            P(None, None, ("dp", "seq")),
            P(None, None, ("dp", "seq")),
            P(None, None, ("dp", "seq")),
        ),
        check_vma=False,
    )
```

time: 482 us -> 397 us (0.82)
  local copies, waits for them, and re-layouts: 72 us -> 33.4 us
  Pallas kernels: 201 us -> 173 us
  starting transfers between devices: 81.1 us -> 67 us
  other arithmetic: 44.5 us -> 33.2 us
  waiting for transfers between devices: 61.4 us -> 67.2 us
    pallas_call x5 -> x2, Pallas kernels: 50.4 us -> 6.27 us  [the longest x1 3.23 us: per_device(): pl.pallas_call(functools.partial(pack_weights_kernel, n=n, hn=hn, hc=hc,...]
    ppermute x53 -> x45, waiting for transfers between devices: 22.6 us -> 62.6 us  [swap(): return lax.ppermute(v, axis, [(i, i ^ bit) for i in range(size)])]
    ppermute x12 -> x6, waiting for transfers between devices: 28.5 us -> 0.02 us  [rotate(): return lax.ppermute(v, 'dp', [(i, (i + 2 * r) % size) for i in range(size)])]
    pallas_call x2, Pallas kernels: 50.4 us -> 72.2 us  [backward(): pl.pallas_call(functools.partial(backward_kernel, hn=hn, hc=hc, rank=rank...]
    ppermute x12 -> x6, starting transfers between devices: 26.7 us -> 10.8 us  [rotate(): return lax.ppermute(v, 'dp', [(i, (i + 2 * r) % size) for i in range(size)])]
    pallas_call x4 -> x2, Pallas kernels: 66.7 us -> 52.1 us  [forward(): pl.pallas_call(functools.partial(forward_kernel, hn=hn, hc=hc, count=len(...]
    dynamic_update_slice x14 -> x10, local copies, waits for them, and re-layouts: 13.1 us -> 1.22 us  [put(): out = lax.dynamic_update_slice_in_dim(out, piece, slot * rows, 0)]
    unnamed x127 -> x106, local copies, waits for them, and re-layouts: 18.5 us -> 7.09 us
  transfers between devices with their start and end apart: 69 -> 55, of which waited for: 13 -> 11; matrix products, arithmetic and copies ran while one was open for 21% -> 16% of each run, Pallas kernels for 39% -> 43%
where the time goes in v2:
time: 397 us; the launch traced here: 391 us
  Pallas kernels  173 us (44%)
  waiting for transfers between devices  67.2 us (17%)
  starting transfers between devices  67 us (17%)
  local copies, waits for them, and re-layouts  33.4 us (8%)
  other arithmetic  33.2 us (8%)
  matrix products  14.8 us (4%)
    pallas_call x2, Pallas kernels, backward(): pl.pallas_call(functools.partial(backward_kernel, hn=hn, hc=hc, rank=rank...  72.2 us
    ppermute x45, waiting for transfers between devices, swap(): return lax.ppermute(v, axis, [(i, i ^ bit) for i in range(size)])  62.6 us
    pallas_call x2, Pallas kernels, forward(): pl.pallas_call(functools.partial(forward_kernel, hn=hn, hc=hc, count=len(...  52.1 us
    ppermute x45, starting transfers between devices, swap(): return lax.ppermute(v, axis, [(i, i ^ bit) for i in range(size)])  42.8 us
    pallas_call x2, Pallas kernels, middle(): pl.pallas_call(functools.partial(middle_kernel, hc=hc, width=width, rank=...  42.6 us
    dot_general x8, matrix products, mm(): return jnp.einsum(form, a, b, preferred_element_type=f32)  14.8 us
    ppermute x6, starting transfers between devices, rotate(): return lax.ppermute(v, 'dp', [(i, (i + 2 * r) % size) for i in range(size)])  10.8 us
    convert_element_type x4, other arithmetic, across(): return (far.astype(f32) + pair[BLOCK:].astype(f32)).astype(bf16)  8.22 us
  transfers between devices with their start and end apart: 55, of which 11 were waited for; matrix products, arithmetic and copies ran while one was open for 16% of the time, Pallas kernels for 43%

profile of v2, /device:TPU:0, one launch (start us, length us, event | category | flops | bytes accessed | tf_op | source)
XLA Modules:
  0.0 390.8 jit_solution(585058856960084720)
XLA Ops:
  4.5 3.2 pack_weights.1
  7.7 3.0 collective-permute-start
  12.3 4.1 %all-to-all-start = ((bf16[4,48,1280]{2,1,0:T(8,128)(2,1)}), bf16[4,48,1280]{2,1,0:T(8,128)(2,1)}, u32[]{:S(2)}, u32[]{:S(2)}) async-start(bf16[4,48,1280]{2,1,0:T(8,128)(2,1)} %bitcast.185), calls=%async_computation | async-start | bytes 983040 | tf_op jit(solution)/shard_map/all_to_all | solution.py:718
  19.0 3.2 fusion.70
  24.9 3.3 collective-permute-done.1
  37.8 15.0 %collective-permute-done.7 = bf16[896,128]{1,0:T(8,128)(2,1)S(1)} collective-permute-done((bf16[896,128]{1,0:T(8,128)(2,1)S(1)}, bf16[896,128]{1,0:T(8,128)(2,1)S(1)}, u32[]{:S(2)}, u32[]{:S(2)}) %collective-permute-start.7) | collective-permute-done | bytes 229408 | tf_op jit(solution)/shard_map/ppermute | solution.py:546
  55.3 3.5 all-to-all-start.1
  62.4 4.6 %all-to-all-done.1 = bf16[4,48,896]{2,1,0:T(8,128)(2,1)S(1)} async-done(((bf16[4,48,896]{2,1,0:T(8,128)(2,1)}), bf16[4,48,896]{2,1,0:T(8,128)(2,1)S(1)}, u32[]{:S(2)}, u32[]{:S(2)}) %all-to-all-start.1) | async-done | bytes 344096 | tf_op jit(solution)/shard_map/all_to_all | solution.py:731
  73.5 3.1 collective-permute-start.10
  92.3 4.3 %collective-permute-done.11.refs_2_ = bf16[1,256,1536]{2,1,0:T(8,128)(2,1)} collective-permute-done((bf16[1,256,1536]{2,1,0:T(8,128)(2,1)}, bf16[1,256,1536]{2,1,0:T(8,128)(2,1)}, u32[]{:S(2)}, u32[]{:S(2)}) %collective-permute-start.11) | collective-permute-done | bytes 786464 | tf_op jit(solution)/shard_map/ppermute | solution.py:546
  103.5 4.0 %collective-permute-start.16 = (bf16[384,896]{1,0:T(8,128)(2,1)}, bf16[384,896]{1,0:T(8,128)(2,1)}, u32[]{:S(2)}, u32[]{:S(2)}) collective-permute-start(bf16[384,896]{1,0:T(8,128)(2,1)} %pad_maximum_fusion.4.refs_11_), channel_id=1, source_target_pairs={{0,24},{4,28},{8,0},{12,4},{16,8},{20,12},{24,16},{28,20},{1,25},{... | collective-permute-start | bytes 2064392 | tf_op jit(solution)/shard_map/ppermute | solution.py:559
  107.5 6.5 %collective-permute-done.13.refs_17_ = bf16[192,1280]{1,0:T(8,128)(2,1)} collective-permute-done((bf16[192,1280]{1,0:T(8,128)(2,1)}, bf16[192,1280]{1,0:T(8,128)(2,1)}, u32[]{:S(2)}, u32[]{:S(2)}) %collective-permute-start.13) | collective-permute-done | bytes 491552 | tf_op jit(solution)/shard_map/ppermute | solution.py:546
  115.7 26.1 %ssm_forward.2 = (bf16[1,1024,1536]{2,1,0:T(8,128)(2,1)}, bf16[1,1024,128]{2,1,0:T(8,128)(2,1)}, bf16[1,1024,1024]{2,1,0:T(8,128)(2,1)}, f32[1,1024,1024]{2,1,0:...) custom-call(s32[12]{0:T(128)} %concatenate.48.order_ref, ...), custom_call_target="tpu_custom_call" | custom-call | flops 5234491392 | bytes 20971520 | tf_op jit(solution)/shard_map/ssm_forward/pallas_call | solution.py:861
  152.2 26.0 %ssm_forward.3 = (bf16[1,1024,1536]{2,1,0:T(8,128)(2,1)}, bf16[1,1024,128]{2,1,0:T(8,128)(2,1)}, bf16[1,1024,1024]{2,1,0:T(8,128)(2,1)}, f32[1,1024,1024]{2,1,0:...) custom-call(s32[5]{0:T(128)} %pad_add_fusion.order_ref, ...), custom_call_target="tpu_custom_call" | custom-call | flops 5234491392 | bytes 20971520 | tf_op jit(solution)/shard_map/ssm_forward/pallas_call | solution.py:861
  180.2 17.7 %collective-permute-done.25.refs_18_ = bf16[384,896]{1,0:T(8,128)(2,1)S(1)} collective-permute-done((bf16[384,896]{1,0:T(8,128)(2,1)}, bf16[384,896]{1,0:T(8,128)(2,1)S(1)}, u32[]{:S(2)}, u32[]{:S(2)}) %collective-permute-start.25) | collective-permute-done | bytes 688160 | tf_op jit(solution)/shard_map/ppermute | solution.py:546
  199.0 21.1 %output_side.2 = (f32[1,1024,768]{2,1,0:T(8,128)}, f32[1,1024,768]{2,1,0:T(8,128)}, bf16[1,1024,128]{2,1,0:T(8,128)(2,1)}, bf16[256,1536]{1,0:T(8,128)(2,1)}, bf...) custom-call(s32[12]{0:T(128)} %concatenate.48.order_ref, ...), custom_call_target="tpu_custom_call" | custom-call | flops 7247757312 | bytes 26214400 | tf_op jit(solution)/shard_map/output_side/pallas_call | solution.py:901
  227.7 21.5 %output_side.3 = (f32[1,1024,768]{2,1,0:T(8,128)}, f32[1,1024,768]{2,1,0:T(8,128)}, bf16[1,1024,128]{2,1,0:T(8,128)(2,1)}, bf16[256,1536]{1,0:T(8,128)(2,1)}, bf...) custom-call(s32[5]{0:T(128)} %pad_add_fusion.order_ref, ...), custom_call_target="tpu_custom_call" | custom-call | flops 7247757312 | bytes 26214400 | tf_op jit(solution)/shard_map/output_side/pallas_call | solution.py:901
  258.6 36.2 %ssm_backward.2 = (bf16[256,1536]{1,0:T(8,128)(2,1)}, bf16[512,1536]{1,0:T(8,128)(2,1)}, bf16[256,1536]{1,0:T(8,128)(2,1)}, f32[1,16,2560]{2,1,0:T(8,128)}, f32[1,16,1024]{2,1,0:T(8,128)}) custom-call(s32[4]{0:T(128)} %copy-done.38, f32[1,1024,768]{2,1,0:T(8,128)} %get-tuple-element.372.q_ref, f32[1,1024,768]{2,1,0:T(8,128)} %get-tuple-element.373.g_ref, ...), custom_call_target="tpu_custom_call" | custom-call | flops 8858370048 | bytes 31457280 | tf_op jit(solution)/shard_map/ssm_backward/pallas_call | solution.py:948
  305.8 35.9 %ssm_backward.3 = (bf16[256,1536]{1,0:T(8,128)(2,1)}, bf16[512,1536]{1,0:T(8,128)(2,1)}, bf16[256,1536]{1,0:T(8,128)(2,1)}, f32[1,16,2560]{2,1,0:T(8,128)}, f32[1,16,1024]{2,1,0:T(8,128)}) custom-call(s32[4]{0:T(128)} %copy-done.38, f32[1,1024,768]{2,1,0:T(8,128)} %get-tuple-element.360.q_ref, f32[1,1024,768]{2,1,0:T(8,128)} %get-tuple-element.361.g_ref, ...), custom_call_target="tpu_custom_call" | custom-call | flops 8858370048 | bytes 31457280 | tf_op jit(solution)/shard_map/ssm_backward/pallas_call | solution.py:948
  363.2 3.0 pack_grads.1
  366.3 4.2 %all-to-all-start.2 = ((bf16[8,32,640]{2,1,0:T(8,128)(2,1)}), bf16[8,32,640]{2,1,0:T(8,128)(2,1)}, u32[]{:S(2)}, u32[]{:S(2)}) async-start(bf16[8,32,640]{2,1,0:T(8,128)(2,1)} %pack_grads.1), calls=%async_computation.2 | async-start | bytes 655360 | tf_op jit(solution)/shard_map/all_to_all | solution.py:1198
  370.4 6.9 %collective-permute-done.48 = bf16[256,1536]{1,0:T(8,128)(2,1)} collective-permute-done((bf16[256,1536]{1,0:T(8,128)(2,1)}, bf16[256,1536]{1,0:T(8,128)(2,1)}, u32[]{:S(2)}, u32[]{:S(2)}) %collective-permute-start.48) | collective-permute-done | bytes 786464 | tf_op jit(solution)/shard_map/ppermute | solution.py:546
  377.3 4.4 %fusion.19 = (f32[256]{0:T(256)S(1)}, f32[256]{0:T(256)S(1)}, f32[256]{0:T(256)S(1)}, f32[256]{0:T(256)S(1)}, f32[256,1536]{1,0:T(8,128)S(1)}) fusion(f32[1536]{0:T(1024)S(1)} %copy-done.29, bf16[256,1536]{1,0:T(8,128)(2,1)} %collective-permute-done.40, bf16[512,1536]{1,0:T(8,128)(2,1)} %collective-permute-done.38, ...), kind=kOutput, calls=%fused_computation.27 | convolution fusion | flops 110099456 | bytes 9906176 | tf_op jit(solution)/shard_map/rt,dr->td/dot_general | solution.py:17
  381.8 3.0 fusion.18
  (358 shorter events, 125.0 us)
Async XLA Ops:
  31.1 35.9 %collective-permute-start.4 = (bf16[192,1280]{1,0:T(8,128)(2,1)}, bf16[192,1280]{1,0:T(8,128)(2,1)S(1)}, u32[]{:S(2)}, u32[]{:S(2)}) collective-permute-start(bf16[192,1280]{1,0:T(8,128)(2,1)} %bitcast.10.refs_11_), channel_id=1, source_target_pairs={{0,8},{4,12},{8,16},{12,20},{16,24},{20,28},{24,0},{28,4},{1,9},{5... | collective-permute-start | bytes 1474568 | tf_op jit(solution)/shard_map/ppermute | solution.py:559
  32.7 34.3 %collective-permute-start.5 = (bf16[192,1280]{1,0:T(8,128)(2,1)}, bf16[192,1280]{1,0:T(8,128)(2,1)S(1)}, u32[]{:S(2)}, u32[]{:S(2)}) collective-permute-start(bf16[192,1280]{1,0:T(8,128)(2,1)} %bitcast.10.refs_11_), channel_id=1, source_target_pairs={{0,24},{4,28},{8,0},{12,4},{16,8},{20,12},{24,16},{28,20},{1,25},{... | collective-permute-start | bytes 1474568 | tf_op jit(solution)/shard_map/ppermute | solution.py:559
  34.9 32.1 %collective-permute-start.6 = (bf16[192,1280]{1,0:T(8,128)(2,1)}, bf16[192,1280]{1,0:T(8,128)(2,1)S(1)}, u32[]{:S(2)}, u32[]{:S(2)}) collective-permute-start(bf16[192,1280]{1,0:T(8,128)(2,1)} %bitcast.10.refs_11_), channel_id=1, source_target_pairs={{0,4},{4,0},{8,12},{12,8},{16,20},{20,16},{24,28},{28,24},{1,5},{5... | collective-permute-start | bytes 1474568 | tf_op jit(solution)/shard_map/ppermute | solution.py:546
  73.5 25.9 %collective-permute-start.10 = (bf16[384,1280]{1,0:T(8,128)(2,1)}, bf16[384,1280]{1,0:T(8,128)(2,1)}, u32[]{:S(2)}, u32[]{:S(2)}) collective-permute-start(bf16[384,1280]{1,0:T(8,128)(2,1)} %pad_maximum_fusion.2), channel_id=1, source_target_pairs={{0,4},{4,0},{8,12},{12,8},{16,20},{20,16},{24,28},{28,24},{1,5},{5... | collective-permute-start | bytes 2949128 | tf_op jit(solution)/shard_map/ppermute | solution.py:546
  101.7 40.1 %collective-permute-start.18 = (bf16[1,256,1536]{2,1,0:T(8,128)(2,1)}, bf16[1,256,1536]{2,1,0:T(8,128)(2,1)S(1)}, u32[]{:S(2)}, u32[]{:S(2)}) collective-permute-start(bf16[1,256,1536]{2,1,0:T(8,128)(2,1)} %get-tuple-element.274), channel_id=1, source_target_pairs={{0,2},{1,3},{2,0},{3,1},{4,6},{5,7},{6,4},{7,5},{8,10},{9,11},{10,... | collective-permute-start | bytes 2359304 | tf_op jit(solution)/shard_map/ppermute | solution.py:546
  103.5 38.3 %collective-permute-start.15 = (bf16[384,896]{1,0:T(8,128)(2,1)}, bf16[384,896]{1,0:T(8,128)(2,1)}, u32[]{:S(2)}, u32[]{:S(2)}) collective-permute-start(bf16[384,896]{1,0:T(8,128)(2,1)} %pad_maximum_fusion.4.refs_11_), channel_id=1, source_target_pairs={{0,8},{4,12},{8,16},{12,20},{16,24},{20,28},{24,0},{28,4},{1,9},{5... | collective-permute-start | bytes 2064392 | tf_op jit(solution)/shard_map/ppermute | solution.py:559
  103.5 38.3 %collective-permute-start.16 = (bf16[384,896]{1,0:T(8,128)(2,1)}, bf16[384,896]{1,0:T(8,128)(2,1)}, u32[]{:S(2)}, u32[]{:S(2)}) collective-permute-start(bf16[384,896]{1,0:T(8,128)(2,1)} %pad_maximum_fusion.4.refs_11_), channel_id=1, source_target_pairs={{0,24},{4,28},{8,0},{12,4},{16,8},{20,12},{24,16},{28,20},{1,25},{... | collective-permute-start | bytes 2064392 | tf_op jit(solution)/shard_map/ppermute | solution.py:559
  113.9 27.9 %collective-permute-start.17 = (bf16[384,896]{1,0:T(8,128)(2,1)}, bf16[384,896]{1,0:T(8,128)(2,1)}, u32[]{:S(2)}, u32[]{:S(2)}) collective-permute-start(bf16[384,896]{1,0:T(8,128)(2,1)} %pad_maximum_fusion.4.refs_11_), channel_id=1, source_target_pairs={{0,4},{4,0},{8,12},{12,8},{16,20},{20,16},{24,28},{28,24},{1,5},{5... | collective-permute-start | bytes 2064392 | tf_op jit(solution)/shard_map/ppermute | solution.py:546
  145.4 34.4 %collective-permute-start.24 = (bf16[2,256,1536]{2,1,0:T(8,128)(2,1)}, bf16[2,256,1536]{2,1,0:T(8,128)(2,1)}, u32[]{:S(2)}, u32[]{:S(2)}) collective-permute-start(bf16[2,256,1536]{2,1,0:T(8,128)(2,1)} %refs_4_.1), channel_id=1, source_target_pairs={{0,1},{1,0},{2,3},{3,2},{4,5},{5,4},{6,7},{7,6},{8,9},{9,8},{10,11... | collective-permute-start | bytes 4718600 | tf_op jit(solution)/shard_map/ppermute | solution.py:546
  145.5 34.2 %collective-permute-start.23 = (bf16[1,256,1536]{2,1,0:T(8,128)(2,1)}, bf16[1,256,1536]{2,1,0:T(8,128)(2,1)}, u32[]{:S(2)}, u32[]{:S(2)}) collective-permute-start(bf16[1,256,1536]{2,1,0:T(8,128)(2,1)} %get-tuple-element.291), channel_id=1, source_target_pairs={{0,2},{1,3},{2,0},{3,1},{4,6},{5,7},{6,4},{7,5},{8,10},{9,11},{10,... | collective-permute-start | bytes 2359304 | tf_op jit(solution)/shard_map/ppermute | solution.py:546
  147.2 30.9 %collective-permute-start.20 = (bf16[384,896]{1,0:T(8,128)(2,1)}, bf16[384,896]{1,0:T(8,128)(2,1)}, u32[]{:S(2)}, u32[]{:S(2)}) collective-permute-start(bf16[384,896]{1,0:T(8,128)(2,1)} %collective-permute-done.15.refs_13_), channel_id=1, source_target_pairs={{0,4},{4,0},{8,12},{12,8},{16,20},{20,16},{24,28},{28,24},{1,5},{5... | collective-permute-start | bytes 2064392 | tf_op jit(solution)/shard_map/ppermute | solution.py:546
  147.5 32.2 %collective-permute-start.21 = (bf16[384,896]{1,0:T(8,128)(2,1)}, bf16[384,896]{1,0:T(8,128)(2,1)}, u32[]{:S(2)}, u32[]{:S(2)}) collective-permute-start(bf16[384,896]{1,0:T(8,128)(2,1)} %collective-permute-done.16.refs_14_), channel_id=1, source_target_pairs={{0,4},{4,0},{8,12},{12,8},{16,20},{20,16},{24,28},{28,24},{1,5},{5... | collective-permute-start | bytes 2064392 | tf_op jit(solution)/shard_map/ppermute | solution.py:546
  149.3 30.5 %collective-permute-start.22 = (bf16[384,896]{1,0:T(8,128)(2,1)}, bf16[384,896]{1,0:T(8,128)(2,1)}, u32[]{:S(2)}, u32[]{:S(2)}) collective-permute-start(bf16[384,896]{1,0:T(8,128)(2,1)} %pad_maximum_fusion.4.refs_11_), channel_id=1, source_target_pairs={{0,16},{4,20},{8,24},{12,28},{16,0},{20,4},{24,8},{28,12},{1,17},{... | collective-permute-start | bytes 2064392 | tf_op jit(solution)/shard_map/ppermute | solution.py:559
  253.4 41.6 %collective-permute-start.37 = (bf16[512,1536]{1,0:T(8,128)(2,1)}, bf16[512,1536]{1,0:T(8,128)(2,1)}, u32[]{:S(2)}, u32[]{:S(2)}) collective-permute-start(bf16[512,1536]{1,0:T(8,128)(2,1)} %get-tuple-element.386), channel_id=1, source_target_pairs={{0,1},{1,0},{2,3},{3,2},{4,5},{5,4},{6,7},{7,6},{8,9},{9,8},{10,11... | collective-permute-start | bytes 4718600 | tf_op jit(solution)/shard_map/ppermute | solution.py:546
  255.0 39.9 %collective-permute-start.34 = (f32[24,1024]{1,0:T(8,128)S(1)}, f32[24,1024]{1,0:T(8,128)S(1)}, u32[]{:S(2)}, u32[]{:S(2)}) collective-permute-start(f32[24,1024]{1,0:T(8,128)S(1)} %bitcast.199), channel_id=1, source_target_pairs={{0,1},{1,0},{2,3},{3,2},{4,5},{5,4},{6,7},{7,6},{8,9},{9,8},{10,11... | collective-permute-start | bytes 294920 | tf_op jit(solution)/shard_map/ppermute | solution.py:546
  255.2 39.7 %collective-permute-start.35 = (f32[24,1024]{1,0:T(8,128)S(1)}, f32[24,1024]{1,0:T(8,128)S(1)}, u32[]{:S(2)}, u32[]{:S(2)}) collective-permute-start(f32[24,1024]{1,0:T(8,128)S(1)} %bitcast.200), channel_id=1, source_target_pairs={{0,2},{1,3},{2,0},{3,1},{4,6},{5,7},{6,4},{7,5},{8,10},{9,11},{10,... | collective-permute-start | bytes 294920 | tf_op jit(solution)/shard_map/ppermute | solution.py:546
  256.9 38.0 %collective-permute-start.36 = (f32[24,1024]{1,0:T(8,128)S(1)}, f32[24,1024]{1,0:T(8,128)S(1)}, u32[]{:S(2)}, u32[]{:S(2)}) collective-permute-start(f32[24,1024]{1,0:T(8,128)S(1)} %bitcast.201), channel_id=1, source_target_pairs={{0,3},{1,2},{2,1},{3,0},{4,7},{5,6},{6,5},{7,4},{8,11},{9,10},{10,... | collective-permute-start | bytes 294920 | tf_op jit(solution)/shard_map/ppermute | solution.py:546
  256.9 38.0 %collective-permute-start.33 = (bf16[256,1536]{1,0:T(8,128)(2,1)}, bf16[256,1536]{1,0:T(8,128)(2,1)}, u32[]{:S(2)}, u32[]{:S(2)}) collective-permute-start(bf16[256,1536]{1,0:T(8,128)(2,1)} %add_convert_fusion.3), channel_id=1, source_target_pairs={{0,2},{1,3},{2,0},{3,1},{4,6},{5,7},{6,4},{7,5},{8,10},{9,11},{10,... | collective-permute-start | bytes 2359304 | tf_op jit(solution)/shard_map/ppermute | solution.py:546
  301.9 39.8 %collective-permute-start.41 = (f32[16,1024]{1,0:T(8,128)S(1)}, f32[16,1024]{1,0:T(8,128)S(1)}, u32[]{:S(2)}, u32[]{:S(2)}) collective-permute-start(f32[16,1024]{1,0:T(8,128)S(1)} %bitcast.205), channel_id=1, source_target_pairs={{0,1},{1,0},{2,3},{3,2},{4,5},{5,4},{6,7},{7,6},{8,9},{9,8},{10,11... | collective-permute-start | bytes 196616 | tf_op jit(solution)/shard_map/ppermute | solution.py:546
  302.2 39.6 %collective-permute-start.42 = (f32[16,1024]{1,0:T(8,128)S(1)}, f32[16,1024]{1,0:T(8,128)S(1)}, u32[]{:S(2)}, u32[]{:S(2)}) collective-permute-start(f32[16,1024]{1,0:T(8,128)S(1)} %bitcast.206), channel_id=1, source_target_pairs={{0,2},{1,3},{2,0},{3,1},{4,6},{5,7},{6,4},{7,5},{8,10},{9,11},{10,... | collective-permute-start | bytes 196616 | tf_op jit(solution)/shard_map/ppermute | solution.py:546
  302.7 39.1 %collective-permute-start.43 = (f32[16,1024]{1,0:T(8,128)S(1)}, f32[16,1024]{1,0:T(8,128)S(1)}, u32[]{:S(2)}, u32[]{:S(2)}) collective-permute-start(f32[16,1024]{1,0:T(8,128)S(1)} %bitcast.207), channel_id=1, source_target_pairs={{0,3},{1,2},{2,1},{3,0},{4,7},{5,6},{6,5},{7,4},{8,11},{9,10},{10,... | collective-permute-start | bytes 196616 | tf_op jit(solution)/shard_map/ppermute | solution.py:546
  303.8 38.0 %collective-permute-start.39 = (bf16[256,1536]{1,0:T(8,128)(2,1)}, bf16[256,1536]{1,0:T(8,128)(2,1)}, u32[]{:S(2)}, u32[]{:S(2)}) collective-permute-start(bf16[256,1536]{1,0:T(8,128)(2,1)} %add_convert_fusion.2), channel_id=1, source_target_pairs={{0,2},{1,3},{2,0},{3,1},{4,6},{5,7},{6,4},{7,5},{8,10},{9,11},{10,... | collective-permute-start | bytes 2359304 | tf_op jit(solution)/shard_map/ppermute | solution.py:546
  304.2 37.5 %collective-permute-start.40 = (bf16[256,1536]{1,0:T(8,128)(2,1)}, bf16[256,1536]{1,0:T(8,128)(2,1)}, u32[]{:S(2)}, u32[]{:S(2)}) collective-permute-start(bf16[256,1536]{1,0:T(8,128)(2,1)} %add_convert_fusion.1), channel_id=1, source_target_pairs={{0,2},{1,3},{2,0},{3,1},{4,6},{5,7},{6,4},{7,5},{8,10},{9,11},{10,... | collective-permute-start | bytes 2359304 | tf_op jit(solution)/shard_map/ppermute | solution.py:546
  352.4 24.9 %collective-permute-start.48 = (bf16[256,1536]{1,0:T(8,128)(2,1)}, bf16[256,1536]{1,0:T(8,128)(2,1)}, u32[]{:S(2)}, u32[]{:S(2)}) collective-permute-start(bf16[256,1536]{1,0:T(8,128)(2,1)} %add_convert_fusion), channel_id=1, source_target_pairs={{0,2},{1,3},{2,0},{3,1},{4,6},{5,7},{6,4},{7,5},{8,10},{9,11},{10,... | collective-permute-start | bytes 2359304 | tf_op jit(solution)/shard_map/ppermute | solution.py:546
  (80 other events, 789.1 us)

commit v3 on v2

--- a/solution.py
+++ b/solution.py
@@ -33,10 +33,12 @@
     return lax.dot_general(a, b, (((0,), (0,)), ((), ())), preferred_element_type=f32)
 
 
-def dot_exact(a, b):
-    return lax.dot_general(
-        a, b, (((1,), (0,)), ((), ())), preferred_element_type=f32, precision=lax.Precision.HIGHEST
-    )
+def dot_exact(chosen, v):
+    hi = v.astype(bf16)
+    rest = v - hi.astype(f32)
+    mid = rest.astype(bf16)
+    lo = (rest - mid.astype(f32)).astype(bf16)
+    return dot_nn(chosen, hi) + (dot_nn(chosen, mid) + dot_nn(chosen, lo))
 
 
 def sigmoid(v):
@@ -85,27 +87,36 @@
         copy.wait()
 
 
-def choose(order_ref, b, blocks, target):
+def fetch(order_ref, b, blocks, s0, target, sem):
     for i, block in enumerate(blocks):
 
         @pl.when(order_ref[b] == i)
         def _(block=block):
-            target[...] = block[0]
-
-
-def forward_kernel(order_ref, *refs, hn, hc, count, size, keep):
+            row = s0 if block.shape[0] > 1 else 0
+            pltpu.make_async_copy(block.at[row], target, sem).start()
+
+
+def arrived(blocks, target, sem):
+    pltpu.make_async_copy(blocks[0].at[0], target, sem).wait()
+
+
+def forward_kernel(order_ref, *refs, hn, hc, count, size, s0, keep):
     (x0, x1, x2, x3, meta_ref, doc_ref, up_ref, conv_ref, head_ref, mask_ref, half_ref) = refs[:11]
     pieces = refs[11 : 11 + count]
     normed_ref, rank_ref, vbc_ref, pre_ref, ssm_ref, state_ref, tok_ref, *rest = refs[11 + count :]
     if keep:
         full_ref, rest = rest[0], rest[1:]
-    buf, carry, x_buf, wa_ref, gain_ref, sems, full_sem = rest
+    buf, carry, x_buf, wa_ref, gain_ref, pa_buf, normed_buf, sems, full_sem, x_sems = rest
     pairs = hn // 2
     cc = hc + 256
     b = pl.program_id(0)
 
+    xs = (x0, x1, x2, x3)
+
     @pl.when(b == 0)
     def _():
+        for k in (0, 1):
+            fetch(order_ref, k, xs, s0, x_buf.at[k], x_sems.at[k])
         assemble(order_ref, 4, pieces, size, wa_ref, sems)
         if keep:
             pltpu.make_async_copy(wa_ref, full_ref, full_sem).start()
@@ -113,15 +124,41 @@
         carry[...] = jnp.zeros_like(carry)
         buf[0:8, :] = jnp.zeros((8, cc), f32)
 
-    choose(order_ref, b, (x0, x1, x2, x3), x_buf)
-    x = x_buf[...].astype(f32)
-    inv = lax.rsqrt(jnp.mean(x * x, -1, keepdims=True) + EPS)
-    normed = (x * inv * gain_ref[7:8, :]).astype(bf16)
-    normed_ref[0] = normed
-    pa = dot_nn(normed, wa_ref[...])
-    rank = (pa[:, cc : cc + 128] * mask_ref[0, 0:1, :]).astype(bf16)
+    blocks = pl.num_programs(0)
+    now, later = lax.rem(b, 2), lax.rem(b + 1, 2)
+    chunks = wa_ref.shape[1] // 128
+    chunks = chunks // 2 if chunks % 2 == 0 else chunks
+    span = wa_ref.shape[1] // chunks
+
+    def normalise(slot):
+        x = x_buf[slot].astype(f32)
+        inv = lax.rsqrt(jnp.mean(x * x, -1, keepdims=True) + EPS)
+        normed_buf[slot] = (x * inv * gain_ref[7:8, :]).astype(bf16)
+
+    def project(slot, c):
+        at = slice(span * c, span * c + span)
+        pa_buf[slot, :, at] = dot_nn(normed_buf[slot], wa_ref[:, at])
+
+    @pl.when(b == 0)
+    def _():
+        arrived(xs, x_buf.at[0], x_sems.at[0])
+        normalise(0)
+        for c in range(chunks):
+            project(0, c)
+
+    @pl.when(b + 2 < blocks)
+    def _():
+        fetch(order_ref, b + 2, xs, s0, x_buf.at[now], x_sems.at[now])
+
+    @pl.when(b + 1 < blocks)
+    def _():
+        arrived(xs, x_buf.at[later], x_sems.at[later])
+
+    normalise(later)
+    normed_ref[0] = normed_buf[now]
+    rank = (pa_buf[now, :, cc : cc + 128] * mask_ref[0, 0:1, :]).astype(bf16)
     rank_ref[0] = rank
-    conv_in = (pa[:, :cc] + dot_nt(rank, up_ref[...])).astype(bf16).astype(f32)
+    conv_in = (pa_buf[now, :, :cc] + dot_nt(rank, up_ref[...])).astype(bf16).astype(f32)
     buf[8:, :] = conv_in
     meta = meta_ref[0]
     pre = conv_ref[4:5, :] + conv_ref[3:4, :] * conv_in
@@ -134,11 +171,11 @@
     values = vbc[:, :hc]
     in_state = vbc[:, hc : hc + 128]
     out_state = vbc[:, hc + 128 :]
-    arg = pa[:, cc + 128 : cc + 256] + head_ref[0:1, :]
+    arg = pa_buf[now, :, cc + 128 : cc + 256] + head_ref[0:1, :]
     dt = jnp.maximum(arg, 0.0) + jnp.log1p(jnp.exp(-jnp.abs(arg)))
     row = lax.broadcasted_iota(jnp.int32, (BLOCK, BLOCK), 0)
     col = lax.broadcasted_iota(jnp.int32, (BLOCK, BLOCK), 1)
-    cum = dot_exact((row >= col).astype(f32), dt * head_ref[1:2, :])
+    cum = dot_exact((row >= col).astype(f32).astype(bf16), dt * head_ref[1:2, :])
     tok_ref[0, :, 0:128] = dt
     tok_ref[0, :, 128:256] = cum
     tok_ref[0, :, 256:384] = arg
@@ -156,6 +193,8 @@
     half = BLOCK // 2
     scaled = []
     for j in range(pairs):
+        for c in range(j * chunks // pairs, (j + 1) * chunks // pairs):
+            project(later, c)
         at = slice(128 * j, 128 * j + 128)
         v = values[:, at]
         ys = []
@@ -210,13 +249,10 @@
         )
         for j, (source, target) in enumerate(moves):
             copies.append(pltpu.make_async_copy(source, target, sems.at[3 * i + j]))
-    for copy in copies:
-        copy.start()
-    for copy in copies:
-        copy.wait()
-
-
-def middle_kernel(order_ref, *refs, hc, width, rank, count, keep, merged):
+    return copies
+
+
+def middle_kernel(order_ref, *refs, hc, width, rank, count, keep, merged, s0):
     (
         normed_ref, rank_ref, vbc_ref, ssm_ref, og0, og1, og2, og3, up_ref, row_ref, mask_ref,
     ) = refs[:11]
@@ -227,7 +263,8 @@
     g_ref, q_ref, gro_ref, near_ref, pair_ref, far_ref, stat_ref, *rest = refs[first_out:]
     if keep:
         wb_full, wo_full, rest = rest[0], rest[1], rest[2:]
-    og_buf, wb_ref, wo_ref, sems, more_sems, full_sems = rest
+    og_buf, wb_ref, wo_ref, sems, more_sems, full_sems, og_sems = rest
+    ogs = (og0, og1, og2, og3)
     b = pl.program_id(0)
 
     def keeping():
@@ -236,23 +273,44 @@
             pltpu.make_async_copy(wo_ref, wo_full, full_sems.at[1]),
         )
 
+    now, later = lax.rem(b, 2), lax.rem(b + 1, 2)
+    if merged:
+        copies = assemble_both(order_ref, 4, gate_pieces, *merged, wb_ref, wo_ref, sems)
+        gate_copies = copies[::3]
+        out_copies = [c for i, c in enumerate(copies) if i % 3]
+    else:
+        gate_copies = [pltpu.make_async_copy(gate_pieces[0], wb_ref, sems.at[0])]
+        out_copies = [pltpu.make_async_copy(out_pieces[0], wo_ref, more_sems.at[0])]
+
     @pl.when(b == 0)
     def _():
-        if merged:
-            assemble_both(order_ref, 4, gate_pieces, *merged, wb_ref, wo_ref, sems)
-        else:
-            assemble(order_ref, 4, gate_pieces, wb_ref.shape[0], wb_ref, sems)
-            assemble(order_ref, 4, out_pieces, wo_ref.shape[0], wo_ref, more_sems)
+        for copy in gate_copies:
+            copy.start()
+        fetch(order_ref, 0, ogs, s0, og_buf.at[0], og_sems.at[0])
+        for copy in out_copies:
+            copy.start()
+        for copy in gate_copies:
+            copy.wait()
+
+    @pl.when(b + 1 < pl.num_programs(0))
+    def _():
+        fetch(order_ref, b + 1, ogs, s0, og_buf.at[later], og_sems.at[later])
+
+    gate = dot_nn(normed_ref[0], wb_ref[:, :hc]) + dot_nt(rank_ref[0], up_ref[...])
+    g_ref[0] = gate
+
+    @pl.when(b == 0)
+    def _():
+        for copy in out_copies:
+            copy.wait()
         if keep:
             for copy in keeping():
                 copy.start()
 
-    choose(order_ref, b, (og0, og1, og2, og3), og_buf)
-    gate = dot_nn(normed_ref[0], wb_ref[:, :hc]) + dot_nt(rank_ref[0], up_ref[...])
-    g_ref[0] = gate
+    arrived(ogs, og_buf.at[now], og_sems.at[now])
     mixed = ssm_ref[0] + row_ref[0:1, :] * vbc_ref[0, :, :hc].astype(f32)
     gated = mixed * (gate * sigmoid(gate))
-    og = og_buf[...]
+    og = og_buf[now]
     gro = (dot_nn(og, wb_ref[:, hc:]) * mask_ref[0, 0:1, :]).astype(bf16)
     gro_ref[0] = gro
     q = dot_nt(og, wo_ref[:, :width]) + dot_nt(gro, wo_ref[:, width : width + 128])
@@ -279,10 +337,22 @@
     rank_ref, gro_ref, conv_ref, head_ref, row_ref, half_ref, select_ref, upg_ref, upc_ref, mask_ref,
     wa_ref, wb_ref,
     near_ref, pair_ref, far_ref, grads_ref, gri_ref,
-    buf, carry,
+    buf, carry, held_gate, held_conv, held_step, part_buf,
     *, hn, hc, rank,
 ):
     pairs = hn // 2
+    step = pl.program_id(0)
+    blocks = pl.num_programs(0)
+    chunks = part_buf.shape[1] // 256
+
+    def product(c):
+        rows = slice(256 * c, 256 * c + 256)
+        part_buf[:, rows] = (
+            dot_nt(held_gate[...], wb_ref[rows, :hc])
+            + dot_nt(held_conv[...], wa_ref[rows, :cc])
+            + dot_nt(held_step[...], wa_ref[rows, cc + 128 :])
+        ).astype(bf16)
+
     cc = hc + 256
     first = pl.program_id(0) == 0
 
@@ -344,6 +414,8 @@
     g_con = [jnp.zeros((half, BLOCK), f32), jnp.zeros((half, half), f32)]
     g_val = []
     for j in range(pairs):
+        for c in range(j * chunks // pairs, (j + 1) * chunks // pairs):
+            product(c)
         at = slice(128 * j, 128 * j + 128)
         v = values[:, at]
         gs = gsum[:, at]
@@ -377,7 +449,7 @@
     last = jnp.sum(jnp.concatenate(parts, 0).T, 0, keepdims=True)
     where_last = lax.broadcasted_iota(jnp.int32, (BLOCK, 128), 0) == BLOCK - 1
     grad_cum = gained - spent + jnp.where(where_last, last, 0.0)
-    grad_log = dot_exact((col >= row).astype(f32), grad_cum)
+    grad_log = dot_exact((col >= row).astype(f32).astype(bf16), grad_cum)
     sig = sigmoid(arg)
     g_step = (
         spent * (sig / jnp.maximum(dt, 1e-37)) + head_ref[1:2, :] * grad_log * sig
@@ -406,17 +478,25 @@
     gri_ref[0] = fold(
         (dot_nn(gp_gate, upg_ref[...]) + dot_nn(gp_conv, upc_ref[...])) * mask_ref[0, 0:1, :], rank
     )
-    part = (
-        dot_nt(gp_gate, wb_ref[:, :hc])
-        + dot_nt(gp_conv, wa_ref[:, :cc])
-        + dot_nt(g_step, wa_ref[:, cc + 128 :])
-    ).astype(bf16)
-    route(order_ref, pl.num_programs(0) - 1 - pl.program_id(0), part, near_ref, pair_ref, far_ref)
+
+    @pl.when(step > 0)
+    def _():
+        route(order_ref, blocks - step, part_buf[...], near_ref, pair_ref, far_ref)
+
+    held_gate[...] = gp_gate
+    held_conv[...] = gp_conv
+    held_step[...] = g_step
+
+    @pl.when(step == blocks - 1)
+    def _():
+        for c in range(chunks):
+            product(c)
+        route(order_ref, 0, part_buf[...], near_ref, pair_ref, far_ref)
 
 
 def pack_weights_kernel(
     ip_ref, sp_ref, idn_ref, iup_ref, odn_ref, oup_ref, op_ref, cw_ref, cb_ref, idx_ref, gg_ref, tail_ref,
-    a_ref, b_ref, o_ref, small_ref,
+    a_ref, o_ref, small_ref,
     turn, misc,
     *, n, hn, hc, inner, planes,
 ):
@@ -436,7 +516,9 @@
     chunk = hc // planes
     heads = hn // planes
 
-    def columns(base, t, target, to):
+    b_at = hc + 256 + ranks + 128
+
+    def columns(base, t, to, at0):
         for p in range(0, planes, 2):
             got = []
             for q in (p, p + 1):
@@ -445,16 +527,16 @@
                 v = ip_ref[:, low : low + 256].astype(f32)
                 got.append(pltpu.roll(v, 256 - (start - low), 1) if start > low else v)
             second = pltpu.roll(got[1], 64, 1)
-            at = p * chunk
-            target[to, at : at + 128] = got[0][:, :128].astype(bf16)
-            target[to, at + 128 : at + 256] = jnp.where(
+            at = at0 + p * chunk
+            a_ref[to, at : at + 128] = got[0][:, :128].astype(bf16)
+            a_ref[to, at + 128 : at + 256] = jnp.where(
                 lane < 64, got[0][:, 128:], second[:, :128]
             ).astype(bf16)
-            target[to, at + 256 : at + 384] = second[:, 128:].astype(bf16)
+            a_ref[to, at + 256 : at + 384] = second[:, 128:].astype(bf16)
 
     for t in range(n):
         to = slice(t * rows, (t + 1) * rows)
-        columns(inner, t, a_ref, to)
+        columns(inner, t, to, 0)
         a_ref[to, hc : hc + 256] = ip_ref[:, 2 * inner :]
         a_ref[to, hc + 256 : hc + 256 + ranks] = down
         last = tail_ref[...]
@@ -462,9 +544,9 @@
             shift = (p * heads - (p * n + t) * heads) % 128
             mine = pltpu.roll(step, shift, 1) if shift else step
             last = jnp.where((lane >= p * heads) & (lane < (p + 1) * heads), mine, last)
-        a_ref[to, hc + 256 + ranks :] = last.astype(bf16)
-        columns(0, t, b_ref, to)
-        b_ref[to, hc:] = late
+        a_ref[to, hc + 256 + ranks : b_at] = last.astype(bf16)
+        columns(0, t, to, b_at)
+        a_ref[to, b_at + hc :] = late
     out_rows, width = op_ref.shape
     part = o_ref.shape[1]
     o_ref[:out_rows, :] = op_ref[:, :part]
@@ -475,14 +557,95 @@
     )
     keep = -(-up_rows // 16) * 16
     small_ref[:keep, :] = turned(iup_ref)[:keep].astype(bf16)
-    turn[...] = jnp.zeros_like(turn)
-    turn[: cw_ref.shape[0], : cw_ref.shape[1]] = cw_ref[...].astype(f32)
     misc[...] = jnp.zeros_like(misc)
-    misc[0:8, :] = turn[:, 0:128].T[0:8]
+    misc[0:4, : cw_ref.shape[1]] = cw_ref[...].astype(f32)
     misc[4:5, : cb_ref.shape[1]] = cb_ref[...].astype(f32)
     misc[5:6, : idx_ref.shape[1]] = idx_ref[...].astype(f32)
     misc[6:7, : gg_ref.shape[1]] = gg_ref[...].astype(f32)
     small_ref[keep:, :] = misc[...].astype(bf16)
+
+
+def unpack_kernel(
+    order_ref, own_ref, far_ref, beside_ref,
+    up_gate_ref, up_conv_ref, conv_ref, gain_ref, index_ref,
+    held, up, conv, gains,
+    *, n, planes, up_rows, rows, inner, hc, conv_rows, out_rows,
+):
+    size = own_ref.shape[0]
+    sources = (own_ref, beside_ref.at[0:size], far_ref, beside_ref.at[size : 2 * size])
+    for t in range(n):
+        for i, source in enumerate(sources):
+
+            @pl.when(order_ref[t] == i)
+            def _(t=t, source=source):
+                held[t] = source[...]
+
+    conv[...] = jnp.zeros_like(conv)
+    gains[...] = jnp.zeros_like(gains)
+    keep = -(-up_rows // 16) * 16
+
+    def add(target, v, start):
+        low = start // 128 * 128
+        v = jnp.concatenate([v, jnp.zeros_like(v)], 1)
+        v = pltpu.roll(v, start - low, 1) if start > low else v
+        target[:, low : low + 256] = target[:, low : low + 256] + v
+
+    for t in range(n):
+        for y in range(2):
+            for z in range(planes):
+                owner = (2 * z + y) * n + t
+                base = (y * planes + z) * rows
+                up[up_rows * owner : up_rows * (owner + 1), :] = held[
+                    t, base : base + up_rows, :
+                ].astype(f32)
+                misc = held[t, base + keep : base + keep + 16, :].astype(f32)[:8]
+                add(conv, misc, conv_rows * owner)
+                add(gains, misc, out_rows * owner)
+                index_ref[owner : owner + 1, :] = misc[5:6]
+    here = order_ref[0]
+    chunk = hc // planes
+    for p in range(planes):
+        start = pl.multiple_of((p * n + here) * chunk, 8)
+        to = slice(p * chunk, (p + 1) * chunk)
+        up_gate_ref[to, :] = up[pl.ds(start, chunk), :].astype(bf16)
+        up_conv_ref[to, :] = up[pl.ds(inner + start, chunk), :].astype(bf16)
+    up_conv_ref[hc:, :] = up[2 * inner :, :].astype(bf16)
+    conv_ref[:, hc:] = conv[:, inner : inner + 256]
+    lane = lax.broadcasted_iota(jnp.int32, (8, 128), 1)
+
+    def select(source, target, t):
+        for p in range(0, planes, 2):
+            got = []
+            for q in (p, p + 1):
+                start = (q * n + t) * chunk
+                low = start // 128 * 128
+                v = source[:, low : low + 256]
+                got.append(pltpu.roll(v, 256 - (start - low), 1) if start > low else v)
+            second = pltpu.roll(got[1], 64, 1)
+            at = p * chunk
+            target[:, at : at + 128] = got[0][:, :128]
+            target[:, at + 128 : at + 256] = jnp.where(lane < 64, got[0][:, 128:], second[:, :128])
+            target[:, at + 256 : at + 384] = second[:, 128:]
+
+    for t in range(n):
+
+        @pl.when(here == t)
+        def _(t=t):
+            select(conv, conv_ref, t)
+            select(gains, gain_ref, t)
+
+
+def final_kernel(*refs, held):
+    near_ref, pair_ref, far_ref, rows_ref, down_ref, x_ref, og_ref, gain_ref = refs[:8]
+    out_ref = refs[8 + held]
+    wide = rows_ref[...].T.astype(bf16)
+    grad = near_ref[...].astype(f32) + pair_ref[...].astype(f32) + far_ref[0].astype(f32)
+    grad = grad + dot_nt(wide, down_ref[...])
+    x = x_ref[0].astype(f32)
+    inv = lax.rsqrt(jnp.mean(x * x, -1, keepdims=True) + EPS)
+    scaled = grad * gain_ref[0:1, :]
+    mean = jnp.mean(scaled * x, -1, keepdims=True)
+    out_ref[0] = inv * (scaled - x * (inv * inv * mean)) + og_ref[0].astype(f32)
 
 
 def pack_grads_kernel(
@@ -655,13 +818,12 @@
     ]
     if staged:
         tail = jnp.pad(tail.astype(f32), ((0, 0), (127 - doc_cols, 0)))
-        payload, late_payload, w_o, small = pl.pallas_call(
+        payload, w_o, small = pl.pallas_call(
             functools.partial(
                 pack_weights_kernel, n=n, hn=hn, hc=hc, inner=inner, planes=planes
             ),
             out_shape=[
-                jax.ShapeDtypeStruct((n * rows, wa_cols), bf16),
-                jax.ShapeDtypeStruct((n * rows, hc + ranks), bf16),
+                jax.ShapeDtypeStruct((n * rows, wa_cols + hc + ranks), bf16),
                 jax.ShapeDtypeStruct((2 * out_rows, hc + ranks), bf16),
                 jax.ShapeDtypeStruct((small_rows, 128), bf16),
             ],
@@ -669,7 +831,7 @@
             name="pack_weights",
         )(
             input_projection, step_projection, *tables[:2], *tables[2:], output_projection,
-            convolution_weight, convolution_bias[None], adapter_index[None], gated_norm_gain[None], tail,
+            convolution_weight.T, convolution_bias[None], adapter_index[None], gated_norm_gain[None], tail,
         )
     else:
         gap = jnp.zeros((rows, 127 - hn - doc_cols), bf16)
@@ -721,31 +883,16 @@
         d = lax.axis_index("dp")
         y, z = d % 2, d // 2
         w_o = lax.ppermute(w_o, both, to_head)
+        turned = [rotate(small, r) for r in (1, 2, 3)]
+        w_a, small, turned, w_o = fence(w_a, small, turned, w_o)
+        w_a, w_b = w_a[:, :wa_cols], w_a[:, wa_cols:]
+        small = put([(small, z)] + [(v, lax.rem(z + 3 - r, 4)) for r, v in enumerate(turned)])
+        a1, a3, a0y = rotate(w_a, 1), rotate(w_a, 3), swap(w_a, "dp", 1)
         small_y = swap(small, "dp", 1)
-        pair = put([(small, y), (small_y, 1 - y)])
-        four = put([(pair, z % 2), (swap(pair, "dp", 2), 1 - z % 2)])
-        x_near = swap(layer_input, "seq", 1)
-        w_a, late_payload, four, x_near, w_o = fence(w_a, late_payload, four, x_near, w_o)
-        a1, a3, a0y = rotate(w_a, 1), rotate(w_a, 3), swap(w_a, "dp", 1)
-        small = put([(four, z // 2), (swap(four, "dp", 4), 1 - z // 2)])
-        w_b = lax.all_to_all(late_payload, "seq", 0, 0, tiled=True)
-        small_far = swap(small, "seq", 2)
-        a1, a3, a0y, w_a, w_b, small, small_far, x0, x1, og0, og1 = fence(
-            a1, a3, a0y, w_a, w_b, small, small_far, layer_input[:1], layer_input[1:],
-            output_gradient[:1], output_gradient[1:],
-        )
-        a13y = swap(jnp.concatenate([a1, a3]), "dp", 1)
-        a2 = rotate(w_a, 2)
+        x0 = after(layer_input, w_a)[:1]
         x_far0 = swap(x0, "seq", 2)
-        beside = swap(jnp.concatenate([small, small_far]), "seq", 1)
-        w_bo = jnp.concatenate([w_b, w_o])
-        half_rows = small.shape[0]
-        small = put(
-            [
-                (small, here), (beside[:half_rows], here ^ 1), (small_far, here ^ 2),
-                (beside[half_rows:], here ^ 3),
-            ]
-        )
+        x1, og = after(layer_input, w_a)[1:], after(output_gradient, w_a)
+        og0, og1 = og[:1], og[1:]
         at = [2 * lax.rem(z + 4 - r, 4) + y for r in range(4)]
         slots = [at[0], at[0] ^ 1, at[1], at[3], at[1] ^ 1, at[3] ^ 1, at[2], at[2] ^ 1]
         slots = jnp.stack(slots).astype(jnp.int32)
@@ -754,6 +901,7 @@
         w_b = lax.all_to_all(late_payload, "seq", 0, 0, tiled=True)
         w_o = lax.ppermute(w_o, both, to_head)
         small = lax.all_gather(lax.all_gather(small, "dp", tiled=True), "seq", tiled=True)
+        small = jnp.moveaxis(small.reshape(n, dps, small_rows, 128), 0, 1)
         wa_pieces = [lax.all_gather(w_a, "dp", tiled=True)]
         slots = jnp.zeros((1,), jnp.int32)
         x_order = jnp.arange(nb, dtype=jnp.int32)
@@ -763,28 +911,28 @@
     order = jnp.concatenate([x_order, slots])
     order_whole = jnp.concatenate([x_order, jnp.zeros((1,), jnp.int32)])
 
-    small = small.reshape(n, dps, small_rows, 128)
-    small = jnp.moveaxis(small, 0, 1).reshape(dps * n, small_rows, 128)
-    up_full = small[:, :up_rows].reshape(cols, ranks)
-    misc = small[:, up_keep:].reshape(dps * n, misc_rows, wide)
-    conv_w = jnp.moveaxis(misc[:, :taps, :conv_rows], 1, 0).reshape(taps, -1).astype(f32)
-    conv_b = misc[:, taps, :conv_rows].reshape(-1).astype(f32)
-    every_index = misc[:, taps + 1, :seqs].reshape(dps, n, seqs)[:, 0].astype(jnp.int32)
-    gate_gain = misc[:, taps + 2, :out_rows].reshape(-1).astype(f32)
-
     def mine(v):
         v = v.reshape(planes, n, v.shape[0] // (planes * n), *v.shape[1:])
         v = lax.dynamic_index_in_dim(v, here, 1, keepdims=False)
         return v.reshape(-1, *v.shape[2:])
 
-    up_gate = mine(up_full[:inner])
-    up_conv = jnp.concatenate([mine(up_full[inner : 2 * inner]), up_full[2 * inner :]], 0)
-    conv_w = jnp.concatenate([mine(conv_w.T[:inner]), conv_w.T[inner:]], 0).T
-    conv_b = jnp.concatenate([mine(conv_b[:inner]), conv_b[inner:]], 0)
+    if not staged:
+        small = small.reshape(dps * n, small_rows, 128)
+        up_full = small[:, :up_rows].reshape(cols, ranks)
+        misc = small[:, up_keep:].reshape(dps * n, misc_rows, wide)
+        conv_w = jnp.moveaxis(misc[:, :taps, :conv_rows], 1, 0).reshape(taps, -1).astype(f32)
+        conv_b = misc[:, taps, :conv_rows].reshape(-1).astype(f32)
+        every_index = misc[:, taps + 1, :seqs].reshape(dps, n, seqs)[:, 0].astype(jnp.int32)
+        gate_gain = misc[:, taps + 2, :out_rows].reshape(-1).astype(f32)
+
+        up_gate = mine(up_full[:inner])
+        up_conv = jnp.concatenate([mine(up_full[inner : 2 * inner]), up_full[2 * inner :]], 0)
+        conv_w = jnp.concatenate([mine(conv_w.T[:inner]), conv_w.T[inner:]], 0).T
+        conv_b = jnp.concatenate([mine(conv_b[:inner]), conv_b[inner:]], 0)
     step_bias = mine(head_step_bias)
     decay_rate = -jnp.exp(mine(log_decay_rate))
     skip = mine(head_skip_gain)
-    gate_gain = mine(gate_gain)
+    gate_gain = None if staged else mine(gate_gain)
 
     chosen = (adapter_index[:, None] == jnp.arange(adapters, dtype=jnp.int32)[None, :]).astype(f32)
     mask = jnp.repeat(chosen, rank, axis=1)[:, None, :]
@@ -812,11 +960,12 @@
     def rows8(*vs):
         return jnp.pad(jnp.stack(vs), ((0, 8 - len(vs)), (0, 0)))
 
-    conv_rows8 = rows8(conv_w[0], conv_w[1], conv_w[2], conv_w[3], conv_b)
+    if not staged:
+        conv_rows8 = rows8(conv_w[0], conv_w[1], conv_w[2], conv_w[3], conv_b)
+        wide_rows = rows8(jnp.repeat(skip, hd), gate_gain)
     head_rows = rows8(
         jnp.pad(step_bias, (0, 128 - hn)), jnp.pad(decay_rate, (0, 128 - hn))
     )
-    wide_rows = rows8(jnp.repeat(skip, hd), gate_gain)
     halves = jnp.pad(
         (jnp.arange(128)[None, :] // 64 == jnp.arange(2)[:, None]).astype(bf16), ((0, 14), (0, 0))
     )
@@ -860,13 +1009,13 @@
         total = sum(v.shape[0] for v in pieces) // size
         return pl.pallas_call(
             functools.partial(
-                forward_kernel, hn=hn, hc=hc, count=len(pieces), size=size, keep=keep
+                forward_kernel, hn=hn, hc=hc, count=len(pieces), size=size, s0=s0, keep=keep
             ),
             grid_spec=pltpu.PrefetchScalarGridSpec(
                 num_scalar_prefetch=1,
                 grid=(nb,),
                 in_specs=[
-                    *(of_seq(v, s0) for v in blocks), at(128, s0),
+                    *([anywhere] * len(blocks)), at(128, s0),
                     pl.BlockSpec((1, 1, 1, BLOCK), lambda b, o: (s0, b, 0, 0)),
                     once(up_conv), once(conv_rows8), once(head_rows), of_seq(mask8, s0), once(halves),
                     *([anywhere] * len(pieces)),
@@ -878,9 +1027,10 @@
                 ],
                 scratch_shapes=[
                     pltpu.VMEM((BLOCK + 8, cc), f32), pltpu.VMEM((hc, state), f32),
-                    pltpu.VMEM((BLOCK, width), bf16), pltpu.VMEM((width, wa_cols), bf16),
-                    pltpu.VMEM((8, width), f32), pltpu.SemaphoreType.DMA((total,)),
-                    pltpu.SemaphoreType.DMA,
+                    pltpu.VMEM((2, BLOCK, width), bf16), pltpu.VMEM((width, wa_cols), bf16),
+                    pltpu.VMEM((8, width), f32), pltpu.VMEM((2, BLOCK, wa_cols), f32),
+                    pltpu.VMEM((2, BLOCK, width), bf16), pltpu.SemaphoreType.DMA((total,)),
+                    pltpu.SemaphoreType.DMA, pltpu.SemaphoreType.DMA((2,)),
                 ],
             ),
             out_shape=[
@@ -901,13 +1051,13 @@
         return pl.pallas_call(
             functools.partial(
                 middle_kernel, hc=hc, width=width, rank=rank, count=count, keep=keep,
-                merged=merged,
+                merged=merged, s0=s0,
             ),
             grid_spec=pltpu.PrefetchScalarGridSpec(
                 num_scalar_prefetch=1,
                 grid=(nb,),
                 in_specs=[
-                    at(width), at(128), at(cc), at(hc), *(of_seq(v, s0) for v in blocks),
+                    at(width), at(128), at(cc), at(hc), *([anywhere] * len(blocks)),
                     once(up_gate), once(wide_rows), of_seq(mask8, s0), *([anywhere] * (count + len(out_pieces))),
                 ],
                 out_specs=[
@@ -916,9 +1066,10 @@
                     *([anywhere] * 2 if keep else []),
                 ],
                 scratch_shapes=[
-                    pltpu.VMEM((BLOCK, width), bf16), pltpu.VMEM(wb_shape, bf16),
+                    pltpu.VMEM((2, BLOCK, width), bf16), pltpu.VMEM(wb_shape, bf16),
                     pltpu.VMEM(wo_shape, bf16), pltpu.SemaphoreType.DMA((3 * dps,)),
                     pltpu.SemaphoreType.DMA((count,)), pltpu.SemaphoreType.DMA((2,)),
+                    pltpu.SemaphoreType.DMA((2,)),
                 ],
             ),
             out_shape=[
@@ -964,6 +1115,8 @@
                 ],
                 scratch_shapes=[
                     pltpu.VMEM((BLOCK + 8, cc), f32), pltpu.VMEM((hc, state), f32),
+                    pltpu.VMEM((BLOCK, hc), bf16), pltpu.VMEM((BLOCK, cc), bf16),
+                    pltpu.VMEM((BLOCK, 128), bf16), pltpu.VMEM((BLOCK, width), bf16),
                 ],
             ),
             out_shape=[
@@ -987,30 +1140,61 @@
         return mm("rt,dr->td", wide_rows_of, table)
 
     if staged:
-        ready = (
-            order, up_conv, up_gate, conv_rows8, head_rows, meta, doc_rows, mask8, halves, select,
-            wide_rows, w_bo, order_whole, every_index,
-        )
-        a2, a13y, x_far0, x1, ready = fence(a2, a13y, x_far0, x1, ready)
-        (
-            order, up_conv, up_gate, conv_rows8, head_rows, meta, doc_rows, mask8, halves, select,
-            wide_rows, w_bo, order_whole, every_index,
-        ) = ready
+        ready = (head_rows, meta, doc_rows, mask8, halves, select, order, order_whole, x1, og0, og1)
+        a1, a3, a0y, w_a, small, small_y, x_far0, w_b, w_o, ready = fence(
+            a1, a3, a0y, w_a, small, small_y, x_far0, w_b, w_o, ready
+        )
+        head_rows, meta, doc_rows, mask8, halves, select, order, order_whole, x1, og0, og1 = ready
+        a13y = swap(jnp.concatenate([a1, a3]), "dp", 1)
+        a2 = rotate(w_a, 2)
+        small = put([(small, y), (small_y, 1 - y)])
+        small_far = swap(small, "seq", 2)
+        x_both0 = swap(x_far0, "seq", 1)
+        x_near = swap(after(layer_input, w_a), "seq", 1)
+        w_bo = jnp.concatenate([w_b, w_o])
+        a2, a13y, small, small_far, x_both0, x_near, w_bo, x1 = fence(
+            a2, a13y, small, small_far, x_both0, x_near, w_bo, x1
+        )
         a2y = swap(a2, "dp", 1)
-        x_both0 = swap(x_far0, "seq", 1)
+        beside = swap(jnp.concatenate([small, small_far]), "seq", 1)
         b1, b3 = rotate(w_bo, 1), rotate(w_bo, 3)
         x_far1 = swap(x1, "seq", 2)
+        up_gate, up_conv, conv_rows8, gains, index_rows = pl.pallas_call(
+            functools.partial(
+                unpack_kernel, n=n, planes=planes, up_rows=up_rows, rows=small_rows, inner=inner,
+                hc=hc, conv_rows=conv_rows, out_rows=out_rows,
+            ),
+            in_specs=[
+                pl.BlockSpec(memory_space=pltpu.SMEM),
+                *[pl.BlockSpec(memory_space=pltpu.VMEM)] * 3,
+            ],
+            out_specs=[pl.BlockSpec(memory_space=pltpu.VMEM)] * 5,
+            out_shape=[
+                jax.ShapeDtypeStruct((hc, ranks), bf16), jax.ShapeDtypeStruct((cc, ranks), bf16),
+                jax.ShapeDtypeStruct((8, cc), f32), jax.ShapeDtypeStruct((8, hc), f32),
+                jax.ShapeDtypeStruct((dps * n, 128), f32),
+            ],
+            scratch_shapes=[
+                pltpu.VMEM((n, *small.shape), bf16), pltpu.VMEM((cols, ranks), f32),
+                pltpu.VMEM((8, inner + state2 + 256), f32), pltpu.VMEM((8, inner + 256), f32),
+            ],
+            compiler_params=pltpu.CompilerParams(vmem_limit_bytes=VMEM_BYTES),
+            name="unpack_small",
+        )(x_order, small, small_far, beside)
+        every_index = index_rows.reshape(dps, n, 128)[:, 0, :seqs].astype(jnp.int32)
+        wide_rows = rows8(jnp.repeat(skip, hd), gains[6])
         wa_pieces = [w_a, a0y, a1, a3, a13y, a2, a2y]
         xs = [[layer_input, x_near, x_far0, x_both0]]
-        wa_pieces, xs[0], w_bo = fence(wa_pieces, xs[0], w_bo)
+        wa_pieces, xs[0], w_bo, up_conv, up_gate, conv_rows8 = fence(
+            wa_pieces, xs[0], w_bo, up_conv, up_gate, conv_rows8
+        )
         *fwd0, wa = forward(0, order, xs[0], wa_pieces, True)
-        b0y = swap(w_bo, "dp", 1)
+        b0y, b2 = swap(w_bo, "dp", 1), rotate(w_bo, 2)
         fwd0, wa, b1, b3, b0y, w_bo, x_far1 = fence(fwd0, wa, b1, b3, b0y, w_bo, x_far1)
         x_both1 = swap(x_far1, "seq", 1)
         x_both1, w_bo, og0, og1, og = fence(x_both1, w_bo, og0, og1, output_gradient)
         fwd1 = forward(1, order_whole, [layer_input, x_near, x_far1, x_both1], [wa], False)
         b1y, b3y = swap(b1, "dp", 1), swap(b3, "dp", 1)
-        b2 = rotate(w_bo, 2)
         og_far0 = swap(og0, "seq", 2)
         og_near = swap(og, "seq", 1)
         fwd1, b1y, b3y, b2, og_far0, og_near, w_bo, og1 = fence(
@@ -1032,6 +1216,7 @@
         full = lax.all_gather(output_gradient, "seq", axis=1, tiled=True)
         ogs = [jnp.split(full, nb, axis=1)] * seqs
     gain = wa[:, -1].astype(f32)
+    gain_rows = jnp.broadcast_to(gain[None], (8, width))
 
     def normalisers(stats):
         inv_gated = lax.rsqrt(stats[:1] / inner + EPS)
@@ -1061,6 +1246,37 @@
             + output_gradient[s0].astype(f32)
         )
 
+    def final_gradient(s0, near, pair, far, grad_rank_in, earlier):
+        rows_of = jnp.tile(own_tokens(grad_rank_in, 1).astype(f32), (adapters, 1)) * mask[s0, 0][:, None]
+
+        tile_rows = 128
+        mine_of_seq = pl.BlockSpec((1, tile_rows, width), lambda i: (s0, i, 0))
+        by_rows = pl.BlockSpec((tile_rows, width), lambda i: (i, 0))
+
+        def full(*block):
+            return pl.BlockSpec(block, lambda i: (0,) * len(block))
+
+        ins = [near, pair, far[None], rows_of, down_in, layer_input, output_gradient, gain_rows]
+        specs = [
+            by_rows, by_rows, pl.BlockSpec((1, tile_rows, width), lambda i: (0, i, 0)),
+            pl.BlockSpec((ranks, tile_rows), lambda i: (0, i)), full(width, ranks), mine_of_seq,
+            mine_of_seq, full(8, width),
+        ]
+        if earlier is not None:
+            ins.append(earlier)
+            specs.append(anywhere)
+        return pl.pallas_call(
+            functools.partial(final_kernel, held=len(ins) - 8),
+            grid=(own_len // tile_rows,),
+            in_specs=specs,
+            out_specs=mine_of_seq,
+            out_shape=jax.ShapeDtypeStruct((seqs, own_len, width), f32),
+            input_output_aliases={8: 0} if earlier is not None else {},
+            compiler_params=params,
+            name="final_gradient",
+            cost_estimate=cost(2 * BLOCK * width * ranks, 5),
+        )(*ins)
+
     *side0, wb, wo = middle(0, order, fwd[0], ogs[0], wb_pieces, wo_pieces, True)
     up_out = wb[:, hc:]
     down_in = wa[:, cc : cc + ranks]
@@ -1068,8 +1284,8 @@
         og_far1 = swap(og1, "seq", 2)
         side0, wb, wo, og_far1 = fence(side0, wb, wo, og_far1)
         ogs.append([output_gradient, og_near, og_far1, swap(og_far1, "seq", 1)])
-        ogs[1], side0, wb, wo, up_out, down_in, gain = fence(
-            ogs[1], side0, wb, wo, up_out, down_in, gain
+        ogs[1], side0, wb, wo, up_out, down_in, gain_rows = fence(
+            ogs[1], side0, wb, wo, up_out, down_in, gain_rows
         )
         gate0, q0, gro0, near0, pair0, far0, stats0 = side0
         side1 = middle(1, order_whole, fwd[1], ogs[1], [wb], [wo], False)
@@ -1111,7 +1327,10 @@
             ],
             1,
         )
-        away_g1, split, got1 = fence(across(far_g1, pair_g1), split, got1)
+        away_g1, split, got1, got, gri0, near0, pair0, near1, pair1, near_g0, pair_g0, down_in = fence(
+            across(far_g1, pair_g1), split, got1, got, gri0, near0, pair0, near1, pair1, near_g0,
+            pair_g0, down_in,
+        )
         away_g1 = swap(away_g1, "seq", 2)
         split_far = swap(split, "seq", 2)
         split_near = swap(split, "seq", 1)
@@ -1119,9 +1338,9 @@
         gri0 = total_of(gri0[0], got).astype(bf16)
         gri1 = total_of(gri1[0], got1).astype(bf16)
         downs = jnp.concatenate([down_gradient(0, gri0), down_gradient(1, gri1)])
+        grad0 = final_gradient(0, near_g0, pair_g0, away_g, gri0, None)
         output0 = layer_output(0, own_sum(near0, pair0, away0), inv0, rank_out0)
         output1 = layer_output(1, own_sum(near1, pair1, away), inv1, rank_out1)
-        grad0 = layer_gradient(0, own_sum(near_g0, pair_g0, away_g), gri0)
         grads_of_seq = [split, split_near, split_far, split_both]
         grads_order = x_order
     else:
@@ -1197,12 +1416,13 @@
             packed = packed.at[:, :, start : start + w].set(v.transpose(1, 0, 2))
     got = lax.all_to_all(packed, "dp", 0, 0, tiled=True)
     if staged:
-        grad1 = layer_gradient(1, own_sum(near_g1, pair_g1, away_g1), gri1)
         output = jnp.stack([output0, output1])
-        grad_in = jnp.stack([grad0, grad1])
     all_chosen = (every_index[..., None] == jnp.arange(adapters)).astype(bf16)
     table = mm("dsk,dsrc->krc", all_chosen, got.reshape(dps, seqs, rank, lanes))
     grads = [table[..., start : start + w] for start, w in zip(starts, widths)]
+    if staged:
+        grad0, output, away_g1, near_g1, pair_g1 = fence(grad0, output, away_g1, near_g1, pair_g1)
+        grad_in = final_gradient(1, near_g1, pair_g1, away_g1, gri1, grad0)
     return (output, grad_in, grads[0], grads[1], grads[2], grads[3])
 
 

time: 397 us -> 370 us (0.932)
  waiting for transfers between devices: 67.2 us -> 83.3 us
  starting transfers between devices: 67 us -> 54.8 us
  local copies, waits for them, and re-layouts: 33.4 us -> 23 us
  other arithmetic: 33.2 us -> 24.1 us
  matrix products: 14.8 us -> 8.3 us
    ppermute x6 -> x9, waiting for transfers between devices: 0.02 us -> 20.3 us  [rotate(): return lax.ppermute(v, 'dp', [(i, (i + 2 * r) % size) for i in range(size)])]
    ppermute x45 -> x43, waiting for transfers between devices: 62.6 us -> 48 us  [swap(): return lax.ppermute(v, axis, [(i, i ^ bit) for i in range(size)])]
    ppermute x45 -> x43, starting transfers between devices: 42.8 us -> 30.4 us  [swap(): return lax.ppermute(v, axis, [(i, i ^ bit) for i in range(size)])]
    all_to_all x1, waiting for transfers between devices: 0.01 us -> 11.4 us  [per_device(): w_a = lax.all_to_all(payload, 'seq', 0, 0, tiled=True)]
    pallas_call x0 -> x3, Pallas kernels: none -> 10.9 us  [the longest x2 7.82 us: final_gradient(): pl.pallas_call(functools.partial(final_kernel, held=len(ins) - 8), grid=(...]
    pallas_call x2, Pallas kernels: 52.1 us -> 44 us  [forward(): pl.pallas_call(functools.partial(forward_kernel, hn=hn, hc=hc, count=len(...]
    dot_general x8 -> x6, matrix products: 14.8 us -> 8.3 us  [mm(): return jnp.einsum(form, a, b, preferred_element_type=f32)]
    pallas_call x2, Pallas kernels: 72.2 us -> 66.3 us  [backward(): pl.pallas_call(functools.partial(backward_kernel, hn=hn, hc=hc, rank=rank...]
  transfers between devices with their start and end apart: 55 -> 55, of which waited for: 11 -> 16; matrix products, arithmetic and copies ran while one was open for 16% -> 11% of each run, Pallas kernels for 43% -> 46%
where the time goes in v3:
time: 370 us; the launch traced here: 365 us
  Pallas kernels  170 us (46%)
  waiting for transfers between devices  83.3 us (23%)
  starting transfers between devices  54.8 us (15%)
  other arithmetic  24.1 us (7%)
  local copies, waits for them, and re-layouts  23 us (6%)
  matrix products  8.3 us (2%)
    pallas_call x2, Pallas kernels, backward(): pl.pallas_call(functools.partial(backward_kernel, hn=hn, hc=hc, rank=rank...  66.3 us
    ppermute x43, waiting for transfers between devices, swap(): return lax.ppermute(v, axis, [(i, i ^ bit) for i in range(size)])  48 us
    pallas_call x2, Pallas kernels, forward(): pl.pallas_call(functools.partial(forward_kernel, hn=hn, hc=hc, count=len(...  44 us
    pallas_call x2, Pallas kernels, middle(): pl.pallas_call(functools.partial(middle_kernel, hc=hc, width=width, rank=...  42.2 us
    ppermute x43, starting transfers between devices, swap(): return lax.ppermute(v, axis, [(i, i ^ bit) for i in range(size)])  30.4 us
    ppermute x9, waiting for transfers between devices, rotate(): return lax.ppermute(v, 'dp', [(i, (i + 2 * r) % size) for i in range(size)])  20.3 us
    ppermute x9, starting transfers between devices, rotate(): return lax.ppermute(v, 'dp', [(i, (i + 2 * r) % size) for i in range(size)])  14.7 us
    all_to_all x1, waiting for transfers between devices, per_device(): w_a = lax.all_to_all(payload, 'seq', 0, 0, tiled=True)  11.4 us
  transfers between devices with their start and end apart: 55, of which 16 were waited for; matrix products, arithmetic and copies ran while one was open for 11% of the time, Pallas kernels for 46%

profile of v3, /device:TPU:0, one launch (start us, length us, event | category | flops | bytes accessed | tf_op | source)
XLA Modules:
  0.0 365.0 jit_solution(6088219476599290383)
XLA Ops:
  3.0 3.2 pack_weights.1
  14.8 3.6 all-to-all-start
  22.7 11.4 %all-to-all-done = bf16[4,48,2176]{2,1,0:T(8,128)(2,1)S(1)} async-done(((bf16[4,48,2176]{2,1,0:T(8,128)(2,1)}), bf16[4,48,2176]{2,1,0:T(8,128)(2,1)S(1)}, u32[]{:S(2)}, u32[]{:S(2)}) %all-to-all-start) | async-done | bytes 835616 | tf_op jit(solution)/shard_map/all_to_all | solution.py:880
  35.5 3.1 collective-permute-start.5
  49.3 6.7 %collective-permute-done.7 = bf16[896,128]{1,0:T(8,128)(2,1)} collective-permute-done((bf16[896,128]{1,0:T(8,128)(2,1)S(1)}, bf16[896,128]{1,0:T(8,128)(2,1)}, u32[]{:S(2)}, u32[]{:S(2)}) %collective-permute-start.7) | collective-permute-done | bytes 229408 | tf_op jit(solution)/shard_map/ppermute | solution.py:709
  58.7 3.1 collective-permute-done.8.refs_2_
  71.3 9.1 %collective-permute-done.11.far_ref = bf16[1792,128]{1,0:T(8,128)(2,1)S(1)} collective-permute-done((bf16[1792,128]{1,0:T(8,128)(2,1)S(1)}, bf16[1792,128]{1,0:T(8,128)(2,1)S(1)}, u32[]{:S(2)}, u32[]{:S(2)}) %collective-permute-start.11) | collective-permute-done | bytes 458784 | tf_op jit(solution)/shard_map/ppermute | solution.py:709
  80.4 9.4 %collective-permute-done.9.refs_16_ = bf16[192,1280]{1,0:T(8,128)(2,1)} collective-permute-done((bf16[192,1280]{1,0:T(8,128)(2,1)S(1)}, bf16[192,1280]{1,0:T(8,128)(2,1)}, u32[]{:S(2)}, u32[]{:S(2)}) %collective-permute-start.9) | collective-permute-done | bytes 491552 | tf_op jit(solution)/shard_map/ppermute | solution.py:722
  92.7 3.8 %collective-permute-start.17 = (bf16[384,896]{1,0:T(8,128)(2,1)}, bf16[384,896]{1,0:T(8,128)(2,1)}, u32[]{:S(2)}, u32[]{:S(2)}) collective-permute-start(bf16[384,896]{1,0:T(8,128)(2,1)} %pad_maximum_fusion.3.refs_11_), channel_id=1, source_target_pairs={{0,24},{4,28},{8,0},{12,4},{16,8},{20,12},{24,16},{28,20},{1,25},{... | collective-permute-start | bytes 2064392 | tf_op jit(solution)/shard_map/ppermute | solution.py:722
  96.5 3.0 unpack_small.1
  99.6 4.2 %collective-permute-done.14.refs_17_ = bf16[192,1280]{1,0:T(8,128)(2,1)S(1)} collective-permute-done((bf16[192,1280]{1,0:T(8,128)(2,1)}, bf16[192,1280]{1,0:T(8,128)(2,1)S(1)}, u32[]{:S(2)}, u32[]{:S(2)}) %collective-permute-start.14) | collective-permute-done | bytes 491552 | tf_op jit(solution)/shard_map/ppermute | solution.py:709
  105.5 22.1 %ssm_forward.2 = (bf16[1,1024,1536]{2,1,0:T(8,128)(2,1)}, bf16[1,1024,128]{2,1,0:T(8,128)(2,1)}, bf16[1,1024,1024]{2,1,0:T(8,128)(2,1)}, f32[1,1024,1024]{2,1,0:...) custom-call(s32[12]{0:T(128)} %concatenate.39.order_ref, ...), custom_call_target="tpu_custom_call" | custom-call | flops 5234491392 | bytes 20971520 | tf_op jit(solution)/shard_map/ssm_forward/pallas_call | solution.py:1010
  135.1 21.9 %ssm_forward.3 = (bf16[1,1024,1536]{2,1,0:T(8,128)(2,1)}, bf16[1,1024,128]{2,1,0:T(8,128)(2,1)}, bf16[1,1024,1024]{2,1,0:T(8,128)(2,1)}, f32[1,1024,1024]{2,1,0:...) custom-call(s32[5]{0:T(128)} %pad_add_fusion.order_ref, ...), custom_call_target="tpu_custom_call" | custom-call | flops 5234491392 | bytes 20971520 | tf_op jit(solution)/shard_map/ssm_forward/pallas_call | solution.py:1010
  157.0 8.2 %collective-permute-done.23.refs_17_ = bf16[384,896]{1,0:T(8,128)(2,1)} collective-permute-done((bf16[384,896]{1,0:T(8,128)(2,1)}, bf16[384,896]{1,0:T(8,128)(2,1)}, u32[]{:S(2)}, u32[]{:S(2)}) %collective-permute-start.23) | collective-permute-done | bytes 688160 | tf_op jit(solution)/shard_map/ppermute | solution.py:722
  168.1 15.6 %collective-permute-done.26.refs_18_ = bf16[384,896]{1,0:T(8,128)(2,1)S(1)} collective-permute-done((bf16[384,896]{1,0:T(8,128)(2,1)}, bf16[384,896]{1,0:T(8,128)(2,1)S(1)}, u32[]{:S(2)}, u32[]{:S(2)}) %collective-permute-start.26) | collective-permute-done | bytes 688160 | tf_op jit(solution)/shard_map/ppermute | solution.py:709
  185.4 21.4 %output_side.2 = (f32[1,1024,768]{2,1,0:T(8,128)}, f32[1,1024,768]{2,1,0:T(8,128)}, bf16[1,1024,128]{2,1,0:T(8,128)(2,1)}, bf16[256,1536]{1,0:T(8,128)(2,1)}, bf...) custom-call(s32[12]{0:T(128)} %concatenate.39.order_ref, ...), custom_call_target="tpu_custom_call" | custom-call | flops 7247757312 | bytes 26214400 | tf_op jit(solution)/shard_map/output_side/pallas_call | solution.py:1051
  214.1 20.8 %output_side.3 = (f32[1,1024,768]{2,1,0:T(8,128)}, f32[1,1024,768]{2,1,0:T(8,128)}, bf16[1,1024,128]{2,1,0:T(8,128)(2,1)}, bf16[256,1536]{1,0:T(8,128)(2,1)}, bf...) custom-call(s32[5]{0:T(128)} %pad_add_fusion.order_ref, ...), custom_call_target="tpu_custom_call" | custom-call | flops 7247757312 | bytes 26214400 | tf_op jit(solution)/shard_map/output_side/pallas_call | solution.py:1051
  243.3 33.3 %ssm_backward.2 = (bf16[256,1536]{1,0:T(8,128)(2,1)}, bf16[512,1536]{1,0:T(8,128)(2,1)}, bf16[256,1536]{1,0:T(8,128)(2,1)}, f32[1,16,2560]{2,1,0:T(8,128)}, f32[1,16,1024]{2,1,0:T(8,128)}) custom-call(s32[4]{0:T(128)} %copy-done.31, f32[1,1024,768]{2,1,0:T(8,128)} %get-tuple-element.408.q_ref, f32[1,1024,768]{2,1,0:T(8,128)} %get-tuple-element.409.g_ref, ...), custom_call_target="tpu_custom_call" | custom-call | flops 8858370048 | bytes 31457280 | tf_op jit(solution)/shard_map/ssm_backward/pallas_call | solution.py:1099
  286.7 33.0 %ssm_backward.3 = (bf16[256,1536]{1,0:T(8,128)(2,1)}, bf16[512,1536]{1,0:T(8,128)(2,1)}, bf16[256,1536]{1,0:T(8,128)(2,1)}, f32[1,16,2560]{2,1,0:T(8,128)}, f32[1,16,1024]{2,1,0:T(8,128)}) custom-call(s32[4]{0:T(128)} %copy-done.31, f32[1,1024,768]{2,1,0:T(8,128)} %get-tuple-element.396.q_ref, f32[1,1024,768]{2,1,0:T(8,128)} %get-tuple-element.397.g_ref, ...), custom_call_target="tpu_custom_call" | custom-call | flops 8858370048 | bytes 31457280 | tf_op jit(solution)/shard_map/ssm_backward/pallas_call | solution.py:1099
  338.7 3.9 %final_gradient.2.refs_8_ = f32[2,256,1536]{2,1,0:T(8,128)} custom-call(bf16[256,1536]{1,0:T(8,128)(2,1)} %get-tuple-element.463.refs_0_, bf16[512,1536]{1,0:T(8,128)(2,1)} %copy-done.5, bf16[1,256,1536]{2,1,0:T(8,128)(2,1)} %bitcast.44.refs_2_, f32[128,256]{1,0:T(8,128)} %bitcast_multiply_fusion.1.refs_3_, bf16[1536,128]{1,0:T(8,128)(2,1)} %slice.156.refs_4_, ...), custom_call_target="tpu_custom_call" | custom-call | flops 100663296 | bytes 5242880 | tf_op jit(solution)/shard_map/final_gradient/pallas_call | solution.py:1268
  343.3 3.1 pack_grads.1
  346.4 4.5 %all-to-all-start.1 = ((bf16[8,32,640]{2,1,0:T(8,128)(2,1)}), bf16[8,32,640]{2,1,0:T(8,128)(2,1)S(1)}, u32[]{:S(2)}, u32[]{:S(2)}) async-start(bf16[8,32,640]{2,1,0:T(8,128)(2,1)} %pack_grads.1), calls=%async_computation.1 | async-start | bytes 655360 | tf_op jit(solution)/shard_map/all_to_all | solution.py:1417
  354.4 3.9 %final_gradient.3 = f32[2,256,1536]{2,1,0:T(8,128)} custom-call(bf16[256,1536]{1,0:T(8,128)(2,1)} %get-tuple-element.483.refs_0_, bf16[512,1536]{1,0:T(8,128)(2,1)} %copy-done.6, bf16[1,256,1536]{2,1,0:T(8,128)(2,1)} %bitcast.57.refs_2_, f32[128,256]{1,0:T(8,128)} %bitcast_multiply_fusion.refs_3_, ...), custom_call_target="tpu_custom_call", output_to_operand_aliasing={{}: (8, {})} | custom-call | flops 100663296 | bytes 5242880 | tf_op jit(solution)/shard_map/final_gradient/pallas_call | solution.py:1268
  358.4 3.5 all-to-all-done.1
  (318 shorter events, 107.2 us)
Async XLA Ops:
  62.4 27.4 %collective-permute-start.13 = (bf16[2,256,1536]{2,1,0:T(8,128)(2,1)S(1)}, bf16[2,256,1536]{2,1,0:T(8,128)(2,1)}, u32[]{:S(2)}, u32[]{:S(2)}) collective-permute-start(bf16[2,256,1536]{2,1,0:T(8,128)(2,1)S(1)} %copy-done), channel_id=1, source_target_pairs={{0,1},{1,0},{2,3},{3,2},{4,5},{5,4},{6,7},{7,6},{8,9},{9,8},{10,11... | collective-permute-start | bytes 4718600 | tf_op jit(solution)/shard_map/ppermute | solution.py:709
  64.6 25.2 %collective-permute-start.10 = (bf16[384,1280]{1,0:T(8,128)(2,1)}, bf16[384,1280]{1,0:T(8,128)(2,1)}, u32[]{:S(2)}, u32[]{:S(2)}) collective-permute-start(bf16[384,1280]{1,0:T(8,128)(2,1)} %pad_maximum_fusion.1), channel_id=1, source_target_pairs={{0,4},{4,0},{8,12},{12,8},{16,20},{20,16},{24,28},{28,24},{1,5},{5... | collective-permute-start | bytes 2949128 | tf_op jit(solution)/shard_map/ppermute | solution.py:709
  66.3 23.5 %collective-permute-start.12 = (bf16[1,256,1536]{2,1,0:T(8,128)(2,1)}, bf16[1,256,1536]{2,1,0:T(8,128)(2,1)}, u32[]{:S(2)}, u32[]{:S(2)}) collective-permute-start(bf16[1,256,1536]{2,1,0:T(8,128)(2,1)} %collective-permute-done.8.refs_2_), channel_id=1, source_target_pairs={{0,1},{1,0},{2,3},{3,2},{4,5},{5,4},{6,7},{7,6},{8,9},{9,8},{10,11... | collective-permute-start | bytes 2359304 | tf_op jit(solution)/shard_map/ppermute | solution.py:709
  66.5 23.3 %collective-permute-start.9 = (bf16[192,1280]{1,0:T(8,128)(2,1)S(1)}, bf16[192,1280]{1,0:T(8,128)(2,1)}, u32[]{:S(2)}, u32[]{:S(2)}) collective-permute-start(bf16[192,1280]{1,0:T(8,128)(2,1)S(1)} %slice.137.refs_11_), channel_id=1, source_target_pairs={{0,16},{4,20},{8,24},{12,28},{16,0},{20,4},{24,8},{28,12},{1,17},{... | collective-permute-start | bytes 1474568 | tf_op jit(solution)/shard_map/ppermute | solution.py:722
  90.9 36.7 %collective-permute-start.19 = (bf16[1,256,1536]{2,1,0:T(8,128)(2,1)}, bf16[1,256,1536]{2,1,0:T(8,128)(2,1)}, u32[]{:S(2)}, u32[]{:S(2)}) collective-permute-start(bf16[1,256,1536]{2,1,0:T(8,128)(2,1)} %get-tuple-element.310), channel_id=1, source_target_pairs={{0,2},{1,3},{2,0},{3,1},{4,6},{5,7},{6,4},{7,5},{8,10},{9,11},{10,... | collective-permute-start | bytes 2359304 | tf_op jit(solution)/shard_map/ppermute | solution.py:709
  92.7 34.9 %collective-permute-start.16 = (bf16[384,896]{1,0:T(8,128)(2,1)}, bf16[384,896]{1,0:T(8,128)(2,1)}, u32[]{:S(2)}, u32[]{:S(2)}) collective-permute-start(bf16[384,896]{1,0:T(8,128)(2,1)} %pad_maximum_fusion.3.refs_11_), channel_id=1, source_target_pairs={{0,8},{4,12},{8,16},{12,20},{16,24},{20,28},{24,0},{28,4},{1,9},{5... | collective-permute-start | bytes 2064392 | tf_op jit(solution)/shard_map/ppermute | solution.py:722
  92.7 34.9 %collective-permute-start.17 = (bf16[384,896]{1,0:T(8,128)(2,1)}, bf16[384,896]{1,0:T(8,128)(2,1)}, u32[]{:S(2)}, u32[]{:S(2)}) collective-permute-start(bf16[384,896]{1,0:T(8,128)(2,1)} %pad_maximum_fusion.3.refs_11_), channel_id=1, source_target_pairs={{0,24},{4,28},{8,0},{12,4},{16,8},{20,12},{24,16},{28,20},{1,25},{... | collective-permute-start | bytes 2064392 | tf_op jit(solution)/shard_map/ppermute | solution.py:722
  131.2 34.4 %collective-permute-start.25 = (bf16[2,256,1536]{2,1,0:T(8,128)(2,1)}, bf16[2,256,1536]{2,1,0:T(8,128)(2,1)}, u32[]{:S(2)}, u32[]{:S(2)}) collective-permute-start(bf16[2,256,1536]{2,1,0:T(8,128)(2,1)} %refs_6_.3), channel_id=1, source_target_pairs={{0,1},{1,0},{2,3},{3,2},{4,5},{5,4},{6,7},{7,6},{8,9},{9,8},{10,11... | collective-permute-start | bytes 4718600 | tf_op jit(solution)/shard_map/ppermute | solution.py:709
  131.4 34.2 %collective-permute-start.24 = (bf16[1,256,1536]{2,1,0:T(8,128)(2,1)}, bf16[1,256,1536]{2,1,0:T(8,128)(2,1)}, u32[]{:S(2)}, u32[]{:S(2)}) collective-permute-start(bf16[1,256,1536]{2,1,0:T(8,128)(2,1)} %get-tuple-element.326), channel_id=1, source_target_pairs={{0,2},{1,3},{2,0},{3,1},{4,6},{5,7},{6,4},{7,5},{8,10},{9,11},{10,... | collective-permute-start | bytes 2359304 | tf_op jit(solution)/shard_map/ppermute | solution.py:709
  133.1 32.1 %collective-permute-start.23 = (bf16[384,896]{1,0:T(8,128)(2,1)}, bf16[384,896]{1,0:T(8,128)(2,1)}, u32[]{:S(2)}, u32[]{:S(2)}) collective-permute-start(bf16[384,896]{1,0:T(8,128)(2,1)} %pad_maximum_fusion.3.refs_11_), channel_id=1, source_target_pairs={{0,16},{4,20},{8,24},{12,28},{16,0},{20,4},{24,8},{28,12},{1,17},{... | collective-permute-start | bytes 2064392 | tf_op jit(solution)/shard_map/ppermute | solution.py:722
  133.1 32.1 %collective-permute-start.21 = (bf16[384,896]{1,0:T(8,128)(2,1)}, bf16[384,896]{1,0:T(8,128)(2,1)}, u32[]{:S(2)}, u32[]{:S(2)}) collective-permute-start(bf16[384,896]{1,0:T(8,128)(2,1)} %collective-permute-done.16.refs_13_), channel_id=1, source_target_pairs={{0,4},{4,0},{8,12},{12,8},{16,20},{20,16},{24,28},{28,24},{1,5},{5... | collective-permute-start | bytes 2064392 | tf_op jit(solution)/shard_map/ppermute | solution.py:709
  134.2 31.4 %collective-permute-start.22 = (bf16[384,896]{1,0:T(8,128)(2,1)}, bf16[384,896]{1,0:T(8,128)(2,1)}, u32[]{:S(2)}, u32[]{:S(2)}) collective-permute-start(bf16[384,896]{1,0:T(8,128)(2,1)} %collective-permute-done.17.refs_14_), channel_id=1, source_target_pairs={{0,4},{4,0},{8,12},{12,8},{16,20},{20,16},{24,28},{28,24},{1,5},{5... | collective-permute-start | bytes 2064392 | tf_op jit(solution)/shard_map/ppermute | solution.py:709
  211.7 23.2 %collective-permute-start.33 = (bf16[512,1536]{1,0:T(8,128)(2,1)}, bf16[512,1536]{1,0:T(8,128)(2,1)}, u32[]{:S(2)}, u32[]{:S(2)}) collective-permute-start(bf16[512,1536]{1,0:T(8,128)(2,1)} %get-tuple-element.394), channel_id=1, source_target_pairs={{0,1},{1,0},{2,3},{3,2},{4,5},{5,4},{6,7},{7,6},{8,9},{9,8},{10,11... | collective-permute-start | bytes 4718600 | tf_op jit(solution)/shard_map/ppermute | solution.py:709
  238.1 38.7 %collective-permute-start.38 = (bf16[512,1536]{1,0:T(8,128)(2,1)}, bf16[512,1536]{1,0:T(8,128)(2,1)}, u32[]{:S(2)}, u32[]{:S(2)}) collective-permute-start(bf16[512,1536]{1,0:T(8,128)(2,1)} %get-tuple-element.422), channel_id=1, source_target_pairs={{0,1},{1,0},{2,3},{3,2},{4,5},{5,4},{6,7},{7,6},{8,9},{9,8},{10,11... | collective-permute-start | bytes 4718600 | tf_op jit(solution)/shard_map/ppermute | solution.py:709
  240.6 36.1 %collective-permute-start.35 = (f32[24,1024]{1,0:T(8,128)S(1)}, f32[24,1024]{1,0:T(8,128)S(1)}, u32[]{:S(2)}, u32[]{:S(2)}) collective-permute-start(f32[24,1024]{1,0:T(8,128)S(1)} %bitcast.153), channel_id=1, source_target_pairs={{0,1},{1,0},{2,3},{3,2},{4,5},{5,4},{6,7},{7,6},{8,9},{9,8},{10,11... | collective-permute-start | bytes 294920 | tf_op jit(solution)/shard_map/ppermute | solution.py:709
  240.8 35.9 %collective-permute-start.36 = (f32[24,1024]{1,0:T(8,128)S(1)}, f32[24,1024]{1,0:T(8,128)S(1)}, u32[]{:S(2)}, u32[]{:S(2)}) collective-permute-start(f32[24,1024]{1,0:T(8,128)S(1)} %bitcast.154), channel_id=1, source_target_pairs={{0,2},{1,3},{2,0},{3,1},{4,6},{5,7},{6,4},{7,5},{8,10},{9,11},{10,... | collective-permute-start | bytes 294920 | tf_op jit(solution)/shard_map/ppermute | solution.py:709
  241.8 34.9 %collective-permute-start.37 = (f32[24,1024]{1,0:T(8,128)S(1)}, f32[24,1024]{1,0:T(8,128)S(1)}, u32[]{:S(2)}, u32[]{:S(2)}) collective-permute-start(f32[24,1024]{1,0:T(8,128)S(1)} %bitcast.155), channel_id=1, source_target_pairs={{0,3},{1,2},{2,1},{3,0},{4,7},{5,6},{6,5},{7,4},{8,11},{9,10},{10,... | collective-permute-start | bytes 294920 | tf_op jit(solution)/shard_map/ppermute | solution.py:709
  242.5 34.2 %collective-permute-start.34 = (bf16[256,1536]{1,0:T(8,128)(2,1)}, bf16[256,1536]{1,0:T(8,128)(2,1)}, u32[]{:S(2)}, u32[]{:S(2)}) collective-permute-start(bf16[256,1536]{1,0:T(8,128)(2,1)} %add_convert_fusion.3), channel_id=1, source_target_pairs={{0,2},{1,3},{2,0},{3,1},{4,6},{5,7},{6,4},{7,5},{8,10},{9,11},{10,... | collective-permute-start | bytes 2359304 | tf_op jit(solution)/shard_map/ppermute | solution.py:709
  282.8 36.9 %collective-permute-start.42 = (f32[16,1024]{1,0:T(8,128)S(1)}, f32[16,1024]{1,0:T(8,128)S(1)}, u32[]{:S(2)}, u32[]{:S(2)}) collective-permute-start(f32[16,1024]{1,0:T(8,128)S(1)} %bitcast.162), channel_id=1, source_target_pairs={{0,1},{1,0},{2,3},{3,2},{4,5},{5,4},{6,7},{7,6},{8,9},{9,8},{10,11... | collective-permute-start | bytes 196616 | tf_op jit(solution)/shard_map/ppermute | solution.py:709
  283.1 36.6 %collective-permute-start.43 = (f32[16,1024]{1,0:T(8,128)S(1)}, f32[16,1024]{1,0:T(8,128)S(1)}, u32[]{:S(2)}, u32[]{:S(2)}) collective-permute-start(f32[16,1024]{1,0:T(8,128)S(1)} %bitcast.163), channel_id=1, source_target_pairs={{0,2},{1,3},{2,0},{3,1},{4,6},{5,7},{6,4},{7,5},{8,10},{9,11},{10,... | collective-permute-start | bytes 196616 | tf_op jit(solution)/shard_map/ppermute | solution.py:709
  284.2 35.5 %collective-permute-start.44 = (f32[16,1024]{1,0:T(8,128)S(1)}, f32[16,1024]{1,0:T(8,128)S(1)}, u32[]{:S(2)}, u32[]{:S(2)}) collective-permute-start(f32[16,1024]{1,0:T(8,128)S(1)} %bitcast.164), channel_id=1, source_target_pairs={{0,3},{1,2},{2,1},{3,0},{4,7},{5,6},{6,5},{7,4},{8,11},{9,10},{10,... | collective-permute-start | bytes 196616 | tf_op jit(solution)/shard_map/ppermute | solution.py:709
  284.7 35.1 %collective-permute-start.40 = (bf16[256,1536]{1,0:T(8,128)(2,1)}, bf16[256,1536]{1,0:T(8,128)(2,1)}, u32[]{:S(2)}, u32[]{:S(2)}) collective-permute-start(bf16[256,1536]{1,0:T(8,128)(2,1)} %add_convert_fusion.2), channel_id=1, source_target_pairs={{0,2},{1,3},{2,0},{3,1},{4,6},{5,7},{6,4},{7,5},{8,10},{9,11},{10,... | collective-permute-start | bytes 2359304 | tf_op jit(solution)/shard_map/ppermute | solution.py:709
  285.8 36.8 %collective-permute-start.41 = (bf16[256,1536]{1,0:T(8,128)(2,1)}, bf16[256,1536]{1,0:T(8,128)(2,1)}, u32[]{:S(2)}, u32[]{:S(2)}) collective-permute-start(bf16[256,1536]{1,0:T(8,128)(2,1)} %add_convert_fusion.1), channel_id=1, source_target_pairs={{0,2},{1,3},{2,0},{3,1},{4,6},{5,7},{6,4},{7,5},{8,10},{9,11},{10,... | collective-permute-start | bytes 2359304 | tf_op jit(solution)/shard_map/ppermute | solution.py:709
  331.1 23.3 %collective-permute-start.49 = (bf16[256,1536]{1,0:T(8,128)(2,1)}, bf16[256,1536]{1,0:T(8,128)(2,1)}, u32[]{:S(2)}, u32[]{:S(2)}) collective-permute-start(bf16[256,1536]{1,0:T(8,128)(2,1)} %add_convert_fusion), channel_id=1, source_target_pairs={{0,2},{1,3},{2,0},{3,1},{4,6},{5,7},{6,4},{7,5},{8,10},{9,11},{10,... | collective-permute-start | bytes 2359304 | tf_op jit(solution)/shard_map/ppermute | solution.py:709
  (76 other events, 916.1 us)

commit v4 on v3

--- a/solution.py
+++ b/solution.py
@@ -56,9 +56,11 @@
 
 
 def per_head(v, select):
-    hi = v.astype(bf16)
-    lo = (v - hi.astype(f32)).astype(bf16)
-    return dot_nn(hi, select) + dot_nn(lo, select)
+    return dot_nn(v.astype(bf16), select)
+
+
+def chunks_at(slot, slots, chunks):
+    return [c for c in range(chunks) if c * slots // chunks == slot]
 
 
 def by_rank(t, rank):
@@ -105,7 +107,7 @@
     pieces = refs[11 : 11 + count]
     normed_ref, rank_ref, vbc_ref, pre_ref, ssm_ref, state_ref, tok_ref, *rest = refs[11 + count :]
     if keep:
-        full_ref, rest = rest[0], rest[1:]
+        full_ref, down_ref, gain_out, *rest = rest
     buf, carry, x_buf, wa_ref, gain_ref, pa_buf, normed_buf, sems, full_sem, x_sems = rest
     pairs = hn // 2
     cc = hc + 256
@@ -121,6 +123,9 @@
         if keep:
             pltpu.make_async_copy(wa_ref, full_ref, full_sem).start()
         gain_ref[...] = wa_ref[:, cc + 128 :].astype(f32).T[120:, :]
+        if keep:
+            down_ref[...] = wa_ref[:, cc : cc + 128]
+            gain_out[...] = jnp.broadcast_to(gain_ref[7:8, :], gain_out.shape)
         carry[...] = jnp.zeros_like(carry)
         buf[0:8, :] = jnp.zeros((8, cc), f32)
 
@@ -262,7 +267,7 @@
     first_out = after_gate + len(out_pieces)
     g_ref, q_ref, gro_ref, near_ref, pair_ref, far_ref, stat_ref, *rest = refs[first_out:]
     if keep:
-        wb_full, wo_full, rest = rest[0], rest[1], rest[2:]
+        wb_full, wo_full, up_out_ref, *rest = rest
     og_buf, wb_ref, wo_ref, sems, more_sems, full_sems, og_sems = rest
     ogs = (og0, og1, og2, og3)
     b = pl.program_id(0)
@@ -304,6 +309,7 @@
         for copy in out_copies:
             copy.wait()
         if keep:
+            up_out_ref[...] = wb_ref[:, hc:]
             for copy in keeping():
                 copy.start()
 
@@ -362,6 +368,13 @@
         buf[BLOCK:, :] = jnp.zeros((8, cc), f32)
         grads_ref[...] = jnp.zeros_like(grads_ref)
 
+    slots = 3 + (pairs + 1) // 2
+
+    def beside(slot):
+        for c in chunks_at(slot, slots, chunks):
+            product(c)
+
+    beside(0)
     rm = jnp.concatenate([rm_ref[0]] * 16, 0).T
     inv = rm[:, 0:1]
     mean = rm[:, 1:2]
@@ -390,6 +403,7 @@
     gsum = grad_mixed.astype(bf16)
     gsum_f = gsum.astype(f32)
 
+    beside(1)
     dt = tok_ref[0, :, 0:128]
     cum = tok_ref[0, :, 128:256]
     arg = tok_ref[0, :, 256:384]
@@ -414,8 +428,8 @@
     g_con = [jnp.zeros((half, BLOCK), f32), jnp.zeros((half, half), f32)]
     g_val = []
     for j in range(pairs):
-        for c in range(j * chunks // pairs, (j + 1) * chunks // pairs):
-            product(c)
+        if j % 2 == 0:
+            beside(2 + j // 2)
         at = slice(128 * j, 128 * j + 128)
         v = values[:, at]
         gs = gsum[:, at]
@@ -460,6 +474,7 @@
         at = slice(64 * h, 64 * h + 64)
         carry[at, :] = passing[:, h : h + 1] * later[at] + direct[at]
 
+    beside(slots - 1)
     pre = pre_ref[0]
     sp = sigmoid(pre)
     grad_out = jnp.concatenate([skip * grad_mixed + g_val, g_in, g_out], 1)
@@ -633,6 +648,20 @@
         def _(t=t):
             select(conv, conv_ref, t)
             select(gains, gain_ref, t)
+
+
+def owners_kernel(chosen_ref, got_ref, *outs, rank, starts):
+    sources, rows, _ = got_ref.shape
+    for k in range(outs[0].shape[0]):
+        total = None
+        for d in range(sources):
+            for b in range(rows // rank):
+                term = chosen_ref[d * (rows // rank) + b, k] * got_ref[
+                    d, b * rank : (b + 1) * rank, :
+                ].astype(f32)
+                total = term if total is None else total + term
+        for out, start in zip(outs, starts):
+            out[k] = total[:, start : start + out.shape[2]]
 
 
 def final_kernel(*refs, held):
@@ -1023,7 +1052,7 @@
                 out_specs=[
                     at(width), at(128), at(cc), at(cc), at(hc),
                     pl.BlockSpec((1, 1, hc, state), lambda b, o: (0, b, 0, 0)), at(384),
-                    *([anywhere] if keep else []),
+                    *([anywhere, once(None, width, 128), once(None, 8, width)] if keep else []),
                 ],
                 scratch_shapes=[
                     pltpu.VMEM((BLOCK + 8, cc), f32), pltpu.VMEM((hc, state), f32),
@@ -1036,7 +1065,14 @@
             out_shape=[
                 one(width, bf16), one(128, bf16), one(cc, bf16), one(cc, f32), one(hc, f32),
                 jax.ShapeDtypeStruct((1, nb, hc, state), bf16), one(384, f32),
-                *([whole_w] if keep else []),
+                *(
+                    [
+                        whole_w, jax.ShapeDtypeStruct((width, 128), bf16),
+                        jax.ShapeDtypeStruct((8, width), f32),
+                    ]
+                    if keep
+                    else []
+                ),
             ],
             compiler_params=params,
             name="ssm_forward",
@@ -1063,7 +1099,7 @@
                 out_specs=[
                     at(hc), at(hc), at(128), *parts_specs(),
                     pl.BlockSpec((1, 8 + rank, BLOCK), lambda b, o: (0, 0, b)),
-                    *([anywhere] * 2 if keep else []),
+                    *([anywhere, anywhere, once(None, width, 128)] if keep else []),
                 ],
                 scratch_shapes=[
                     pltpu.VMEM((2, BLOCK, width), bf16), pltpu.VMEM(wb_shape, bf16),
@@ -1075,7 +1111,11 @@
             out_shape=[
                 one(hc, f32), one(hc, f32), one(128, bf16), *parts_shapes,
                 jax.ShapeDtypeStruct((1, 8 + rank, length), f32),
-                *([jax.ShapeDtypeStruct(v, bf16) for v in (wb_shape, wo_shape)] if keep else []),
+                *(
+                    [jax.ShapeDtypeStruct(v, bf16) for v in (wb_shape, wo_shape, (width, 128))]
+                    if keep
+                    else []
+                ),
             ],
             compiler_params=params,
             name="output_side",
@@ -1188,7 +1228,7 @@
         wa_pieces, xs[0], w_bo, up_conv, up_gate, conv_rows8 = fence(
             wa_pieces, xs[0], w_bo, up_conv, up_gate, conv_rows8
         )
-        *fwd0, wa = forward(0, order, xs[0], wa_pieces, True)
+        *fwd0, wa, down_in, gain_rows = forward(0, order, xs[0], wa_pieces, True)
         b0y, b2 = swap(w_bo, "dp", 1), rotate(w_bo, 2)
         fwd0, wa, b1, b3, b0y, w_bo, x_far1 = fence(fwd0, wa, b1, b3, b0y, w_bo, x_far1)
         x_both1 = swap(x_far1, "seq", 1)
@@ -1202,21 +1242,21 @@
         )
         b2y = swap(b2, "dp", 1)
         og_both0 = swap(og_far0, "seq", 1)
+        og_far1 = swap(og1, "seq", 2)
         fwd = [fwd0, fwd1]
         wb_pieces = [w_bo, b0y, b1, b3, b1y, b3y, b2, b2y]
         wo_pieces = []
         ogs = [[output_gradient, og_near, og_far0, og_both0]]
-        wb_pieces, ogs[0], og1 = fence(wb_pieces, ogs[0], og1)
+        wb_pieces, ogs[0], og_far1 = fence(wb_pieces, ogs[0], og_far1)
+        og_both1 = swap(og_far1, "seq", 1)
     else:
-        fwd = [forward(0, order, xs[0], wa_pieces, True)]
-        wa = fwd[0][-1]
+        *fwd0, wa, down_in, gain_rows = forward(0, order, xs[0], wa_pieces, True)
+        fwd = [fwd0]
         fwd += [forward(s0, order_whole, xs[s0], [wa], False) for s0 in range(1, seqs)]
         wb_pieces = [lax.all_gather(w_b, "dp", tiled=True)]
         wo_pieces = [lax.all_gather(w_o, "dp", tiled=True)]
         full = lax.all_gather(output_gradient, "seq", axis=1, tiled=True)
         ogs = [jnp.split(full, nb, axis=1)] * seqs
-    gain = wa[:, -1].astype(f32)
-    gain_rows = jnp.broadcast_to(gain[None], (8, width))
 
     def normalisers(stats):
         inv_gated = lax.rsqrt(stats[:1] / inner + EPS)
@@ -1239,7 +1279,7 @@
         )
         own = layer_input[s0].astype(f32)
         inv_own = lax.rsqrt(jnp.mean(own * own, -1, keepdims=True) + EPS)
-        scaled_in = grad_normed * gain
+        scaled_in = grad_normed * gain_rows[0]
         return (
             inv_own * scaled_in
             - own * inv_own**3 * jnp.mean(scaled_in * own, -1, keepdims=True)
@@ -1277,16 +1317,10 @@
             cost_estimate=cost(2 * BLOCK * width * ranks, 5),
         )(*ins)
 
-    *side0, wb, wo = middle(0, order, fwd[0], ogs[0], wb_pieces, wo_pieces, True)
-    up_out = wb[:, hc:]
-    down_in = wa[:, cc : cc + ranks]
+    *side0, wb, wo, up_out = middle(0, order, fwd[0], ogs[0], wb_pieces, wo_pieces, True)
     if staged:
-        og_far1 = swap(og1, "seq", 2)
-        side0, wb, wo, og_far1 = fence(side0, wb, wo, og_far1)
-        ogs.append([output_gradient, og_near, og_far1, swap(og_far1, "seq", 1)])
-        ogs[1], side0, wb, wo, up_out, down_in, gain_rows = fence(
-            ogs[1], side0, wb, wo, up_out, down_in, gain_rows
-        )
+        side0, wb, wo, og_both1 = fence(side0, wb, wo, og_both1)
+        ogs.append([output_gradient, og_near, og_far1, og_both1])
         gate0, q0, gro0, near0, pair0, far0, stats0 = side0
         side1 = middle(1, order_whole, fwd[1], ogs[1], [wb], [wo], False)
         got = others(stats0[0])
@@ -1417,9 +1451,22 @@
     got = lax.all_to_all(packed, "dp", 0, 0, tiled=True)
     if staged:
         output = jnp.stack([output0, output1])
-    all_chosen = (every_index[..., None] == jnp.arange(adapters)).astype(bf16)
-    table = mm("dsk,dsrc->krc", all_chosen, got.reshape(dps, seqs, rank, lanes))
-    grads = [table[..., start : start + w] for start, w in zip(starts, widths)]
+    all_chosen = every_index[..., None] == jnp.arange(adapters)
+    if staged:
+        grads = pl.pallas_call(
+            functools.partial(owners_kernel, rank=rank, starts=starts),
+            in_specs=[
+                pl.BlockSpec(memory_space=pltpu.SMEM), pl.BlockSpec(memory_space=pltpu.VMEM)
+            ],
+            out_specs=[pl.BlockSpec(memory_space=pltpu.VMEM)] * len(widths),
+            out_shape=[jax.ShapeDtypeStruct((adapters, rank, w), f32) for w in widths],
+            name="owners_sum",
+        )(all_chosen.astype(f32).reshape(-1, adapters), got)
+    else:
+        table = mm(
+            "dsk,dsrc->krc", all_chosen.astype(bf16), got.reshape(dps, seqs, rank, lanes)
+        )
+        grads = [table[..., start : start + w] for start, w in zip(starts, widths)]
     if staged:
         grad0, output, away_g1, near_g1, pair_g1 = fence(grad0, output, away_g1, near_g1, pair_g1)
         grad_in = final_gradient(1, near_g1, pair_g1, away_g1, gri1, grad0)

time: 370 us -> 369 us (level)
  local copies, waits for them, and re-layouts: 23 us -> 15.5 us
  waiting for transfers between devices: 83.3 us -> 87.2 us
    dot_general x6 -> x5, matrix products: 8.3 us -> 6.98 us  [mm(): return jnp.einsum(form, a, b, preferred_element_type=f32)]
  transfers between devices with their start and end apart: 55 -> 55, of which waited for: 16 -> 15; matrix products, arithmetic and copies ran while one was open for 11% -> 10% of each run, Pallas kernels for 46% -> 45%
where the time goes in v4:
time: 369 us; the launch traced here: 364 us
  Pallas kernels  170 us (46%)
  waiting for transfers between devices  87.2 us (24%)
  starting transfers between devices  55.1 us (15%)
  other arithmetic  27.1 us (7%)
  local copies, waits for them, and re-layouts  15.5 us (4%)
  matrix products  6.98 us (2%)
    pallas_call x2, Pallas kernels, backward(): pl.pallas_call(functools.partial(backward_kernel, hn=hn, hc=hc, rank=rank...  64.1 us
    ppermute x43, waiting for transfers between devices, swap(): return lax.ppermute(v, axis, [(i, i ^ bit) for i in range(size)])  51 us
    pallas_call x2, Pallas kernels, forward(): pl.pallas_call(functools.partial(forward_kernel, hn=hn, hc=hc, count=len(...  44.2 us
    pallas_call x2, Pallas kernels, middle(): pl.pallas_call(functools.partial(middle_kernel, hc=hc, width=width, rank=...  42.3 us
    ppermute x43, starting transfers between devices, swap(): return lax.ppermute(v, axis, [(i, i ^ bit) for i in range(size)])  30.6 us
    ppermute x9, waiting for transfers between devices, rotate(): return lax.ppermute(v, 'dp', [(i, (i + 2 * r) % size) for i in range(size)])  21.8 us
    ppermute x9, starting transfers between devices, rotate(): return lax.ppermute(v, 'dp', [(i, (i + 2 * r) % size) for i in range(size)])  14.6 us
    all_to_all x1, waiting for transfers between devices, per_device(): w_a = lax.all_to_all(payload, 'seq', 0, 0, tiled=True)  10.9 us
  transfers between devices with their start and end apart: 55, of which 15 were waited for; matrix products, arithmetic and copies ran while one was open for 10% of the time, Pallas kernels for 45%

profile of v4, /device:TPU:0, one launch (start us, length us, event | category | flops | bytes accessed | tf_op | source)
XLA Modules:
  0.0 363.5 jit_solution(14084556515836561977)
XLA Ops:
  3.0 3.2 pack_weights.1
  14.8 3.6 all-to-all-start
  23.3 10.9 %all-to-all-done = bf16[4,48,2176]{2,1,0:T(8,128)(2,1)S(1)} async-done(((bf16[4,48,2176]{2,1,0:T(8,128)(2,1)}), bf16[4,48,2176]{2,1,0:T(8,128)(2,1)S(1)}, u32[]{:S(2)}, u32[]{:S(2)}) %all-to-all-start) | async-done | bytes 835616 | tf_op jit(solution)/shard_map/all_to_all | solution.py:909
  36.2 3.1 collective-permute-start.5
  48.4 8.3 %collective-permute-done.7 = bf16[896,128]{1,0:T(8,128)(2,1)S(1)} collective-permute-done((bf16[896,128]{1,0:T(8,128)(2,1)S(1)}, bf16[896,128]{1,0:T(8,128)(2,1)S(1)}, u32[]{:S(2)}, u32[]{:S(2)}) %collective-permute-start.7) | collective-permute-done | bytes 229408 | tf_op jit(solution)/shard_map/ppermute | solution.py:738
  69.2 10.1 %collective-permute-done.11.far_ref = bf16[1792,128]{1,0:T(8,128)(2,1)S(1)} collective-permute-done((bf16[1792,128]{1,0:T(8,128)(2,1)S(1)}, bf16[1792,128]{1,0:T(8,128)(2,1)S(1)}, u32[]{:S(2)}, u32[]{:S(2)}) %collective-permute-start.11) | collective-permute-done | bytes 458784 | tf_op jit(solution)/shard_map/ppermute | solution.py:738
  79.3 10.5 %collective-permute-done.9.refs_16_ = bf16[192,1280]{1,0:T(8,128)(2,1)} collective-permute-done((bf16[192,1280]{1,0:T(8,128)(2,1)}, bf16[192,1280]{1,0:T(8,128)(2,1)}, u32[]{:S(2)}, u32[]{:S(2)}) %collective-permute-start.9) | collective-permute-done | bytes 491552 | tf_op jit(solution)/shard_map/ppermute | solution.py:751
  92.6 3.8 %collective-permute-start.17 = (bf16[384,896]{1,0:T(8,128)(2,1)}, bf16[384,896]{1,0:T(8,128)(2,1)}, u32[]{:S(2)}, u32[]{:S(2)}) collective-permute-start(bf16[384,896]{1,0:T(8,128)(2,1)} %pad_maximum_fusion.3.refs_11_), channel_id=1, source_target_pairs={{0,24},{4,28},{8,0},{12,4},{16,8},{20,12},{24,16},{28,20},{1,25},{... | collective-permute-start | bytes 2064392 | tf_op jit(solution)/shard_map/ppermute | solution.py:751
  96.4 3.0 unpack_small.1
  99.4 4.4 %collective-permute-done.14.refs_17_ = bf16[192,1280]{1,0:T(8,128)(2,1)S(1)} collective-permute-done((bf16[192,1280]{1,0:T(8,128)(2,1)}, bf16[192,1280]{1,0:T(8,128)(2,1)S(1)}, u32[]{:S(2)}, u32[]{:S(2)}) %collective-permute-start.14) | collective-permute-done | bytes 491552 | tf_op jit(solution)/shard_map/ppermute | solution.py:738
  105.4 22.3 %ssm_forward.2 = (bf16[1,1024,1536]{2,1,0:T(8,128)(2,1)}, bf16[1,1024,128]{2,1,0:T(8,128)(2,1)}, bf16[1,1024,1024]{2,1,0:T(8,128)(2,1)}, f32[1,1024,1024]{2,1,0:...) custom-call(s32[12]{0:T(128)} %concatenate.39.order_ref, ...), custom_call_target="tpu_custom_call" | custom-call | flops 5234491392 | bytes 20971520 | tf_op jit(solution)/shard_map/ssm_forward/pallas_call | solution.py:1039
  135.3 21.8 %ssm_forward.3 = (bf16[1,1024,1536]{2,1,0:T(8,128)(2,1)}, bf16[1,1024,128]{2,1,0:T(8,128)(2,1)}, bf16[1,1024,1024]{2,1,0:T(8,128)(2,1)}, f32[1,1024,1024]{2,1,0:...) custom-call(s32[5]{0:T(128)} %pad_add_fusion.order_ref, ...), custom_call_target="tpu_custom_call" | custom-call | flops 5234491392 | bytes 20971520 | tf_op jit(solution)/shard_map/ssm_forward/pallas_call | solution.py:1039
  157.1 8.4 %collective-permute-done.23.refs_17_ = bf16[384,896]{1,0:T(8,128)(2,1)} collective-permute-done((bf16[384,896]{1,0:T(8,128)(2,1)}, bf16[384,896]{1,0:T(8,128)(2,1)}, u32[]{:S(2)}, u32[]{:S(2)}) %collective-permute-start.23) | collective-permute-done | bytes 688160 | tf_op jit(solution)/shard_map/ppermute | solution.py:751
  168.7 15.1 %collective-permute-done.26.refs_18_ = bf16[384,896]{1,0:T(8,128)(2,1)S(1)} collective-permute-done((bf16[384,896]{1,0:T(8,128)(2,1)}, bf16[384,896]{1,0:T(8,128)(2,1)S(1)}, u32[]{:S(2)}, u32[]{:S(2)}) %collective-permute-start.26) | collective-permute-done | bytes 688160 | tf_op jit(solution)/shard_map/ppermute | solution.py:738
  186.4 21.5 %output_side.2 = (f32[1,1024,768]{2,1,0:T(8,128)}, f32[1,1024,768]{2,1,0:T(8,128)}, bf16[1,1024,128]{2,1,0:T(8,128)(2,1)}, bf16[256,1536]{1,0:T(8,128)(2,1)}, bf...) custom-call(s32[12]{0:T(128)} %concatenate.39.order_ref, ...), custom_call_target="tpu_custom_call" | custom-call | flops 7247757312 | bytes 26214400 | tf_op jit(solution)/shard_map/output_side/pallas_call | solution.py:1087
  210.8 20.8 %output_side.3 = (f32[1,1024,768]{2,1,0:T(8,128)}, f32[1,1024,768]{2,1,0:T(8,128)}, bf16[1,1024,128]{2,1,0:T(8,128)(2,1)}, bf16[256,1536]{1,0:T(8,128)(2,1)}, bf...) custom-call(s32[5]{0:T(128)} %pad_add_fusion.order_ref, ...), custom_call_target="tpu_custom_call" | custom-call | flops 7247757312 | bytes 26214400 | tf_op jit(solution)/shard_map/output_side/pallas_call | solution.py:1087
  241.8 32.2 %ssm_backward.2 = (bf16[256,1536]{1,0:T(8,128)(2,1)}, bf16[512,1536]{1,0:T(8,128)(2,1)}, bf16[256,1536]{1,0:T(8,128)(2,1)}, f32[1,16,2560]{2,1,0:T(8,128)}, f32[1,16,1024]{2,1,0:T(8,128)}) custom-call(s32[4]{0:T(128)} %copy-done.29, f32[1,1024,768]{2,1,0:T(8,128)} %get-tuple-element.386.q_ref, f32[1,1024,768]{2,1,0:T(8,128)} %get-tuple-element.387.g_ref, ...), custom_call_target="tpu_custom_call" | custom-call | flops 8858370048 | bytes 31457280 | tf_op jit(solution)/shard_map/ssm_backward/pallas_call | solution.py:1139
  285.1 31.9 %ssm_backward.3 = (bf16[256,1536]{1,0:T(8,128)(2,1)}, bf16[512,1536]{1,0:T(8,128)(2,1)}, bf16[256,1536]{1,0:T(8,128)(2,1)}, f32[1,16,2560]{2,1,0:T(8,128)}, f32[1,16,1024]{2,1,0:T(8,128)}) custom-call(s32[4]{0:T(128)} %copy-done.29, f32[1,1024,768]{2,1,0:T(8,128)} %get-tuple-element.374.q_ref, f32[1,1024,768]{2,1,0:T(8,128)} %get-tuple-element.375.g_ref, ...), custom_call_target="tpu_custom_call" | custom-call | flops 8858370048 | bytes 31457280 | tf_op jit(solution)/shard_map/ssm_backward/pallas_call | solution.py:1139
  317.1 4.0 %collective-permute-done.41 = bf16[256,1536]{1,0:T(8,128)(2,1)} collective-permute-done((bf16[256,1536]{1,0:T(8,128)(2,1)}, bf16[256,1536]{1,0:T(8,128)(2,1)}, u32[]{:S(2)}, u32[]{:S(2)}) %collective-permute-start.41) | collective-permute-done | bytes 786464 | tf_op jit(solution)/shard_map/ppermute | solution.py:738
  337.7 3.9 %final_gradient.2.refs_8_ = f32[2,256,1536]{2,1,0:T(8,128)} custom-call(bf16[256,1536]{1,0:T(8,128)(2,1)} %get-tuple-element.441.refs_0_, bf16[512,1536]{1,0:T(8,128)(2,1)} %copy-done.5, bf16[1,256,1536]{2,1,0:T(8,128)(2,1)} %bitcast.44.refs_2_, f32[128,256]{1,0:T(8,128)} %bitcast_multiply_fusion.1.refs_3_, bf16[1536,128]{1,0:T(8,128)(2,1)} %get-tuple-element.448.refs_4_, ...), custom_call_target="tpu_custom_call" | custom-call | flops 100663296 | bytes 5242880 | tf_op jit(solution)/shard_map/final_gradient/pallas_call | solution.py:1308
  342.3 3.1 pack_grads.1
  345.3 4.7 %all-to-all-start.1 = ((bf16[8,32,640]{2,1,0:T(8,128)(2,1)}), bf16[8,32,640]{2,1,0:T(8,128)(2,1)}, u32[]{:S(2)}, u32[]{:S(2)}) async-start(bf16[8,32,640]{2,1,0:T(8,128)(2,1)} %pack_grads.1), calls=%async_computation.1 | async-start | bytes 655360 | tf_op jit(solution)/shard_map/all_to_all | solution.py:1451
  353.7 3.9 %final_gradient.3 = f32[2,256,1536]{2,1,0:T(8,128)} custom-call(bf16[256,1536]{1,0:T(8,128)(2,1)} %get-tuple-element.461.refs_0_, bf16[512,1536]{1,0:T(8,128)(2,1)} %copy-done.6, bf16[1,256,1536]{2,1,0:T(8,128)(2,1)} %bitcast.57.refs_2_, f32[128,256]{1,0:T(8,128)} %bitcast_multiply_fusion.refs_3_, ...), custom_call_target="tpu_custom_call", output_to_operand_aliasing={{}: (8, {})} | custom-call | flops 100663296 | bytes 5242880 | tf_op jit(solution)/shard_map/final_gradient/pallas_call | solution.py:1308
  357.6 3.6 all-to-all-done.1.got_ref
  (304 shorter events, 103.4 us)
Async XLA Ops:
  36.2 23.4 %collective-permute-start.5 = (bf16[192,1280]{1,0:T(8,128)(2,1)}, bf16[192,1280]{1,0:T(8,128)(2,1)}, u32[]{:S(2)}, u32[]{:S(2)}) collective-permute-start(bf16[192,1280]{1,0:T(8,128)(2,1)} %slice.116.refs_11_), channel_id=1, source_target_pairs={{0,24},{4,28},{8,0},{12,4},{16,8},{20,12},{24,16},{28,20},{1,25},{... | collective-permute-start | bytes 1474568 | tf_op jit(solution)/shard_map/ppermute | solution.py:751
  62.2 27.6 %collective-permute-start.13 = (bf16[2,256,1536]{2,1,0:T(8,128)(2,1)S(1)}, bf16[2,256,1536]{2,1,0:T(8,128)(2,1)}, u32[]{:S(2)}, u32[]{:S(2)}) collective-permute-start(bf16[2,256,1536]{2,1,0:T(8,128)(2,1)S(1)} %copy-done), channel_id=1, source_target_pairs={{0,1},{1,0},{2,3},{3,2},{4,5},{5,4},{6,7},{7,6},{8,9},{9,8},{10,11... | collective-permute-start | bytes 4718600 | tf_op jit(solution)/shard_map/ppermute | solution.py:738
  64.5 25.4 %collective-permute-start.10 = (bf16[384,1280]{1,0:T(8,128)(2,1)}, bf16[384,1280]{1,0:T(8,128)(2,1)}, u32[]{:S(2)}, u32[]{:S(2)}) collective-permute-start(bf16[384,1280]{1,0:T(8,128)(2,1)} %pad_maximum_fusion.1), channel_id=1, source_target_pairs={{0,4},{4,0},{8,12},{12,8},{16,20},{20,16},{24,28},{28,24},{1,5},{5... | collective-permute-start | bytes 2949128 | tf_op jit(solution)/shard_map/ppermute | solution.py:738
  66.2 23.7 %collective-permute-start.12 = (bf16[1,256,1536]{2,1,0:T(8,128)(2,1)}, bf16[1,256,1536]{2,1,0:T(8,128)(2,1)}, u32[]{:S(2)}, u32[]{:S(2)}) collective-permute-start(bf16[1,256,1536]{2,1,0:T(8,128)(2,1)} %collective-permute-done.8.refs_2_), channel_id=1, source_target_pairs={{0,1},{1,0},{2,3},{3,2},{4,5},{5,4},{6,7},{7,6},{8,9},{9,8},{10,11... | collective-permute-start | bytes 2359304 | tf_op jit(solution)/shard_map/ppermute | solution.py:738
  66.3 23.5 %collective-permute-start.9 = (bf16[192,1280]{1,0:T(8,128)(2,1)}, bf16[192,1280]{1,0:T(8,128)(2,1)}, u32[]{:S(2)}, u32[]{:S(2)}) collective-permute-start(bf16[192,1280]{1,0:T(8,128)(2,1)} %slice.116.refs_11_), channel_id=1, source_target_pairs={{0,16},{4,20},{8,24},{12,28},{16,0},{20,4},{24,8},{28,12},{1,17},{... | collective-permute-start | bytes 1474568 | tf_op jit(solution)/shard_map/ppermute | solution.py:751
  90.8 36.9 %collective-permute-start.19 = (bf16[1,256,1536]{2,1,0:T(8,128)(2,1)}, bf16[1,256,1536]{2,1,0:T(8,128)(2,1)}, u32[]{:S(2)}, u32[]{:S(2)}) collective-permute-start(bf16[1,256,1536]{2,1,0:T(8,128)(2,1)} %get-tuple-element.301), channel_id=1, source_target_pairs={{0,2},{1,3},{2,0},{3,1},{4,6},{5,7},{6,4},{7,5},{8,10},{9,11},{10,... | collective-permute-start | bytes 2359304 | tf_op jit(solution)/shard_map/ppermute | solution.py:738
  92.6 35.2 %collective-permute-start.16 = (bf16[384,896]{1,0:T(8,128)(2,1)}, bf16[384,896]{1,0:T(8,128)(2,1)}, u32[]{:S(2)}, u32[]{:S(2)}) collective-permute-start(bf16[384,896]{1,0:T(8,128)(2,1)} %pad_maximum_fusion.3.refs_11_), channel_id=1, source_target_pairs={{0,8},{4,12},{8,16},{12,20},{16,24},{20,28},{24,0},{28,4},{1,9},{5... | collective-permute-start | bytes 2064392 | tf_op jit(solution)/shard_map/ppermute | solution.py:751
  92.6 35.2 %collective-permute-start.17 = (bf16[384,896]{1,0:T(8,128)(2,1)}, bf16[384,896]{1,0:T(8,128)(2,1)}, u32[]{:S(2)}, u32[]{:S(2)}) collective-permute-start(bf16[384,896]{1,0:T(8,128)(2,1)} %pad_maximum_fusion.3.refs_11_), channel_id=1, source_target_pairs={{0,24},{4,28},{8,0},{12,4},{16,8},{20,12},{24,16},{28,20},{1,25},{... | collective-permute-start | bytes 2064392 | tf_op jit(solution)/shard_map/ppermute | solution.py:751
  131.3 34.4 %collective-permute-start.25 = (bf16[2,256,1536]{2,1,0:T(8,128)(2,1)}, bf16[2,256,1536]{2,1,0:T(8,128)(2,1)}, u32[]{:S(2)}, u32[]{:S(2)}) collective-permute-start(bf16[2,256,1536]{2,1,0:T(8,128)(2,1)} %refs_6_.3), channel_id=1, source_target_pairs={{0,1},{1,0},{2,3},{3,2},{4,5},{5,4},{6,7},{7,6},{8,9},{9,8},{10,11... | collective-permute-start | bytes 4718600 | tf_op jit(solution)/shard_map/ppermute | solution.py:738
  131.5 34.3 %collective-permute-start.24 = (bf16[1,256,1536]{2,1,0:T(8,128)(2,1)}, bf16[1,256,1536]{2,1,0:T(8,128)(2,1)}, u32[]{:S(2)}, u32[]{:S(2)}) collective-permute-start(bf16[1,256,1536]{2,1,0:T(8,128)(2,1)} %get-tuple-element.317), channel_id=1, source_target_pairs={{0,2},{1,3},{2,0},{3,1},{4,6},{5,7},{6,4},{7,5},{8,10},{9,11},{10,... | collective-permute-start | bytes 2359304 | tf_op jit(solution)/shard_map/ppermute | solution.py:738
  133.2 32.3 %collective-permute-start.23 = (bf16[384,896]{1,0:T(8,128)(2,1)}, bf16[384,896]{1,0:T(8,128)(2,1)}, u32[]{:S(2)}, u32[]{:S(2)}) collective-permute-start(bf16[384,896]{1,0:T(8,128)(2,1)} %pad_maximum_fusion.3.refs_11_), channel_id=1, source_target_pairs={{0,16},{4,20},{8,24},{12,28},{16,0},{20,4},{24,8},{28,12},{1,17},{... | collective-permute-start | bytes 2064392 | tf_op jit(solution)/shard_map/ppermute | solution.py:751
  133.2 32.3 %collective-permute-start.21 = (bf16[384,896]{1,0:T(8,128)(2,1)}, bf16[384,896]{1,0:T(8,128)(2,1)}, u32[]{:S(2)}, u32[]{:S(2)}) collective-permute-start(bf16[384,896]{1,0:T(8,128)(2,1)} %collective-permute-done.16.refs_13_), channel_id=1, source_target_pairs={{0,4},{4,0},{8,12},{12,8},{16,20},{20,16},{24,28},{28,24},{1,5},{5... | collective-permute-start | bytes 2064392 | tf_op jit(solution)/shard_map/ppermute | solution.py:738
  134.5 31.2 %collective-permute-start.22 = (bf16[384,896]{1,0:T(8,128)(2,1)}, bf16[384,896]{1,0:T(8,128)(2,1)}, u32[]{:S(2)}, u32[]{:S(2)}) collective-permute-start(bf16[384,896]{1,0:T(8,128)(2,1)} %collective-permute-done.17.refs_14_), channel_id=1, source_target_pairs={{0,4},{4,0},{8,12},{12,8},{16,20},{20,16},{24,28},{28,24},{1,5},{5... | collective-permute-start | bytes 2064392 | tf_op jit(solution)/shard_map/ppermute | solution.py:738
  208.0 23.6 %collective-permute-start.33 = (bf16[512,1536]{1,0:T(8,128)(2,1)}, bf16[512,1536]{1,0:T(8,128)(2,1)}, u32[]{:S(2)}, u32[]{:S(2)}) collective-permute-start(bf16[512,1536]{1,0:T(8,128)(2,1)} %get-tuple-element.372), channel_id=1, source_target_pairs={{0,1},{1,0},{2,3},{3,2},{4,5},{5,4},{6,7},{7,6},{8,9},{9,8},{10,11... | collective-permute-start | bytes 4718600 | tf_op jit(solution)/shard_map/ppermute | solution.py:738
  235.6 38.5 %collective-permute-start.38 = (bf16[512,1536]{1,0:T(8,128)(2,1)}, bf16[512,1536]{1,0:T(8,128)(2,1)}, u32[]{:S(2)}, u32[]{:S(2)}) collective-permute-start(bf16[512,1536]{1,0:T(8,128)(2,1)} %get-tuple-element.400), channel_id=1, source_target_pairs={{0,1},{1,0},{2,3},{3,2},{4,5},{5,4},{6,7},{7,6},{8,9},{9,8},{10,11... | collective-permute-start | bytes 4718600 | tf_op jit(solution)/shard_map/ppermute | solution.py:738
  239.4 34.6 %collective-permute-start.35 = (f32[24,1024]{1,0:T(8,128)S(1)}, f32[24,1024]{1,0:T(8,128)}, u32[]{:S(2)}, u32[]{:S(2)}) collective-permute-start(f32[24,1024]{1,0:T(8,128)S(1)} %bitcast.146), channel_id=1, source_target_pairs={{0,1},{1,0},{2,3},{3,2},{4,5},{5,4},{6,7},{7,6},{8,9},{9,8},{10,11... | collective-permute-start | bytes 294920 | tf_op jit(solution)/shard_map/ppermute | solution.py:738
  239.4 34.7 %collective-permute-start.36 = (f32[24,1024]{1,0:T(8,128)S(1)}, f32[24,1024]{1,0:T(8,128)}, u32[]{:S(2)}, u32[]{:S(2)}) collective-permute-start(f32[24,1024]{1,0:T(8,128)S(1)} %bitcast.147), channel_id=1, source_target_pairs={{0,2},{1,3},{2,0},{3,1},{4,6},{5,7},{6,4},{7,5},{8,10},{9,11},{10,... | collective-permute-start | bytes 294920 | tf_op jit(solution)/shard_map/ppermute | solution.py:738
  240.0 34.1 %collective-permute-start.37 = (f32[24,1024]{1,0:T(8,128)S(1)}, f32[24,1024]{1,0:T(8,128)}, u32[]{:S(2)}, u32[]{:S(2)}) collective-permute-start(f32[24,1024]{1,0:T(8,128)S(1)} %bitcast.148), channel_id=1, source_target_pairs={{0,3},{1,2},{2,1},{3,0},{4,7},{5,6},{6,5},{7,4},{8,11},{9,10},{10,... | collective-permute-start | bytes 294920 | tf_op jit(solution)/shard_map/ppermute | solution.py:738
  241.3 32.8 %collective-permute-start.34 = (bf16[256,1536]{1,0:T(8,128)(2,1)}, bf16[256,1536]{1,0:T(8,128)(2,1)S(1)}, u32[]{:S(2)}, u32[]{:S(2)}) collective-permute-start(bf16[256,1536]{1,0:T(8,128)(2,1)} %add_convert_fusion.3), channel_id=1, source_target_pairs={{0,2},{1,3},{2,0},{3,1},{4,6},{5,7},{6,4},{7,5},{8,10},{9,11},{10,... | collective-permute-start | bytes 2359304 | tf_op jit(solution)/shard_map/ppermute | solution.py:738
  281.2 35.8 %collective-permute-start.42 = (f32[16,1024]{1,0:T(8,128)S(1)}, f32[16,1024]{1,0:T(8,128)S(1)}, u32[]{:S(2)}, u32[]{:S(2)}) collective-permute-start(f32[16,1024]{1,0:T(8,128)S(1)} %bitcast.155), channel_id=1, source_target_pairs={{0,1},{1,0},{2,3},{3,2},{4,5},{5,4},{6,7},{7,6},{8,9},{9,8},{10,11... | collective-permute-start | bytes 196616 | tf_op jit(solution)/shard_map/ppermute | solution.py:738
  281.4 35.7 %collective-permute-start.43 = (f32[16,1024]{1,0:T(8,128)S(1)}, f32[16,1024]{1,0:T(8,128)}, u32[]{:S(2)}, u32[]{:S(2)}) collective-permute-start(f32[16,1024]{1,0:T(8,128)S(1)} %bitcast.156), channel_id=1, source_target_pairs={{0,2},{1,3},{2,0},{3,1},{4,6},{5,7},{6,4},{7,5},{8,10},{9,11},{10,... | collective-permute-start | bytes 196616 | tf_op jit(solution)/shard_map/ppermute | solution.py:738
  282.8 34.2 %collective-permute-start.44 = (f32[16,1024]{1,0:T(8,128)S(1)}, f32[16,1024]{1,0:T(8,128)}, u32[]{:S(2)}, u32[]{:S(2)}) collective-permute-start(f32[16,1024]{1,0:T(8,128)S(1)} %bitcast.157), channel_id=1, source_target_pairs={{0,3},{1,2},{2,1},{3,0},{4,7},{5,6},{6,5},{7,4},{8,11},{9,10},{10,... | collective-permute-start | bytes 196616 | tf_op jit(solution)/shard_map/ppermute | solution.py:738
  283.0 34.0 %collective-permute-start.40 = (bf16[256,1536]{1,0:T(8,128)(2,1)}, bf16[256,1536]{1,0:T(8,128)(2,1)S(1)}, u32[]{:S(2)}, u32[]{:S(2)}) collective-permute-start(bf16[256,1536]{1,0:T(8,128)(2,1)} %add_convert_fusion.2), channel_id=1, source_target_pairs={{0,2},{1,3},{2,0},{3,1},{4,6},{5,7},{6,4},{7,5},{8,10},{9,11},{10,... | collective-permute-start | bytes 2359304 | tf_op jit(solution)/shard_map/ppermute | solution.py:738
  284.5 36.5 %collective-permute-start.41 = (bf16[256,1536]{1,0:T(8,128)(2,1)}, bf16[256,1536]{1,0:T(8,128)(2,1)}, u32[]{:S(2)}, u32[]{:S(2)}) collective-permute-start(bf16[256,1536]{1,0:T(8,128)(2,1)} %add_convert_fusion.1), channel_id=1, source_target_pairs={{0,2},{1,3},{2,0},{3,1},{4,6},{5,7},{6,4},{7,5},{8,10},{9,11},{10,... | collective-permute-start | bytes 2359304 | tf_op jit(solution)/shard_map/ppermute | solution.py:738
  (74 other events, 895.8 us)
